TPU v7x, 32 devices: a whole 2x2x4 slice. The times are simulated.
32 devices in a mesh: tm: 4 (over z), rows: 8 (over y, x, core).
Axes of the slice: x: 2, y: 2, z: 4, core: 2. Of those that a mesh axis runs over, the one named last changes fastest.
Arguments:
- snapshots: float32 [196608, 256], P('rows', 'tm'), may hold values from -100 to 100
- last_snapshot: float32 [196608], P('rows'), may hold values from -100 to 100
Outputs:
- basis_rows: float32 [8, 4, 6144, 256], P('rows', 'tm')
- factor: float32 [256, 256], replicated
- projected: float32 [256, 256], replicated
- operator: float32 [256, 256], replicated
All inputs are finite; a program needn't handle non-finite values.
Results may differ from a plain program's by a relative error of at most 0.0003.
Values sent between devices are 32-bit elements; how exact they have to be, the bound alone decides.
No kernel may reach another device: no remote copies, remote signals or barrier semaphores. Data moves between devices by JAX's collectives and lax.ppermute only.
A program may use at most 128 MiB of HBM per device.

v0:
```python
import jax
import jax.numpy as jnp
from jax import lax
from jax.sharding import PartitionSpec as P


def sum_moments(first_part, second_part):
    first_total, second_total = lax.psum((first_part, second_part), ("tm", "rows"))
    return (first_total, second_total)


def shards(snapshots, last_snapshot):
    highest = lax.Precision.HIGHEST
    local_rows = lax.all_to_all(snapshots, "tm", split_axis=0, concat_axis=1, tiled=True)
    row_count = local_rows.shape[0]
    col_count = local_rows.shape[1]
    last_column = lax.dynamic_slice_in_dim(
        last_snapshot, lax.axis_index("tm") * row_count, row_count, 0
    )
    gram_part = jnp.dot(
        local_rows.T, local_rows, precision=highest, preferred_element_type=jnp.float32
    )
    tail_part = jnp.dot(
        last_column, local_rows, precision=highest, preferred_element_type=jnp.float32
    )
    gram_total, tail_total = sum_moments(gram_part, tail_part)
    samples = row_count * lax.axis_size("tm") * lax.axis_size("rows")
    gram_matrix = gram_total / samples
    tail_column = tail_total / samples
    cross_matrix = jnp.concatenate([gram_matrix[:, 1:], tail_column[:, None]], axis=1)
    lower_factor = jnp.linalg.cholesky(gram_matrix)
    identity = jnp.eye(col_count, dtype=jnp.float32)
    inverse = jax.scipy.linalg.solve_triangular(lower_factor, identity, lower=True)
    factor = lower_factor.T
    basis_rows = jnp.dot(
        local_rows, inverse.T, precision=highest, preferred_element_type=jnp.float32
    )
    projected = jnp.dot(
        inverse, cross_matrix, precision=highest, preferred_element_type=jnp.float32
    )
    operator = jnp.dot(projected, inverse.T, precision=highest, preferred_element_type=jnp.float32)
    return (basis_rows.reshape(1, 1, row_count, col_count), factor, projected, operator)


def solution(mesh):
    in_specs = (P("rows", "tm"), P("rows"))
    out_specs = (P("rows", "tm", None, None), P(), P(), P())
    return jax.shard_map(shards, mesh=mesh, in_specs=in_specs, out_specs=out_specs, check_vma=False)
```

profile of v0, /device:TPU:0, one launch (start us, length us, event | category | flops | bytes accessed | tf_op | source)
XLA Modules:
  0.0 436.9 jit_solution(7543601814728142755)
XLA Ops:
  7.2 0.0 copy-start
  7.2 6.2 %copy.27 = f32[8,4,8,6144]{3,2,0,1:T(8,128)} copy(f32[8,4,8,6144]{3,2,1,0:T(8,128)} %bitcast.54) | data formatting | bytes 12582912 | tf_op jit(solution)/shard_map/all_to_all | solution.py:14
  13.4 6.3 %all-to-all-start = ((f32[4,6144,64]{1,2,0:T(8,128)}), f32[4,6144,64]{1,2,0:T(8,128)}, u32[]{:S(2)}, u32[]{:S(2)}) async-start(f32[4,6144,64]{1,2,0:T(8,128)} %bitcast.53), calls=%async_computation | async-start | bytes 12582912 | tf_op jit(solution)/shard_map/all_to_all | solution.py:14
  19.7 0.0 all-reduce.3.cloned.1.call-start
  19.7 0.0 copy-done
  19.8 138.7 %all-to-all-done = f32[4,6144,64]{1,2,0:T(8,128)} async-done(((f32[4,6144,64]{1,2,0:T(8,128)}), f32[4,6144,64]{1,2,0:T(8,128)}, u32[]{:S(2)}, u32[]{:S(2)}) %all-to-all-start) | async-done | bytes 6291488 | tf_op jit(solution)/shard_map/all_to_all | solution.py:14
  158.4 17.7 %fusion.19 = f32[256,256]{0,1:T(8,128)} fusion(f32[6144,256]{0,1:T(8,128)} %bitcast.1), kind=kOutput, calls=%fused_computation.44 | convolution fusion | flops 4831838208 | bytes 6553600 | tf_op jit(solution)/shard_map/dot_general | solution.py:20
  176.2 7.0 %fusion.20 = f32[1,256]{1,0:T(1,128)S(1)} fusion(f32[6144,1]{0,1:T(1,128)S(1)} %bitcast.55, f32[6144,256]{0,1:T(8,128)} %bitcast.1), kind=kOutput, calls=%fused_computation.45 | convolution fusion | flops 18874368 | bytes 6317056 | tf_op jit(solution)/shard_map/dot_general | solution.py:23
  183.1 38.1 %psum.15 = f32[256]{0:T(256)S(1)} all-reduce(f32[256]{0:T(256)S(1)} %bitcast.57), channel_id=1, replica_groups=mesh['tm'=4,'rows'=8] {'tm','rows'}, use_global_device_ids=true, to_apply=%region_5.6 | all-reduce | flops 256 | bytes 2048 | tf_op jit(solution)/shard_map/psum | solution.py:8
  221.2 0.0 all-reduce.3.cloned.1.call-update
  221.2 125.6 %all-reduce.3.cloned.1.call-done = f32[256,256]{0,1:T(8,128)} async-done(((f32[256,256]{0,1:T(8,128)}), f32[256,256]{0,1:T(8,128)}) %all-reduce.3.cloned.1.call-update) | async-done | bytes 262160 | tf_op jit(solution)/shard_map/psum | solution.py:8
  346.8 1.0 broadcast_multiply_fusion
  347.8 0.1 copy.21
  347.9 1.0 fusion.4
  348.9 11.7 %cholesky.50 = f32[128,128]{1,0:T(8,128)S(1)} custom-call(f32[128,128]{1,0:T(8,128)S(1)} %cholesky.118), custom_call_target="Cholesky" | custom-call | tf_op jit(solution)/shard_map/jit(cholesky)/cholesky | solution.py:31
  360.7 9.8 %custom-call.15 = f32[1,128,128]{1,2,0:T(8,128)S(1)} custom-call(f32[1,128,128]{2,1,0:T(8,128)S(1)} %get-tuple-element.43), custom_call_target="InvertDiagBlocksLowerTriangular" | custom-call | tf_op jit(solution)/shard_map/jit(cholesky)/cholesky | solution.py:31
  370.5 0.2 constant_dynamic-update-slice_fusion.1
  370.8 0.3 convolution_subtract_fusion.1
  371.0 11.7 %cholesky.105 = f32[128,128]{1,0:T(8,128)S(1)} custom-call(f32[128,128]{1,0:T(8,128)S(1)} %convolution_subtract_fusion.1), custom_call_target="Cholesky" | custom-call | tf_op jit(solution)/shard_map/jit(cholesky)/cholesky | solution.py:31
  382.8 0.6 compare_reduce_fusion
  384.8 0.8 copy.23
  385.6 0.1 triangular_solve.63
  385.7 4.0 while.1
  385.7 0.6 fusion.32
  386.3 1.4 bitcast_dynamic-update-slice_fusion.2
  387.7 0.6 fusion.32
  388.3 1.4 bitcast_dynamic-update-slice_fusion.2
  389.7 19.9 %custom-call.16 = f32[2,128,128]{1,2,0:T(8,128)S(1)} custom-call(f32[2,128,128]{2,1,0:T(8,128)S(1)} %get-tuple-element.11), custom_call_target="InvertDiagBlocksLowerTriangular" | custom-call | tf_op jit(solution)/shard_map/jit(_solve_triangular)/triangular_solve | solution.py:33
  409.6 0.3 fusion.8
  409.8 0.3 convolution_subtract_fusion
  410.1 0.3 fusion.11
  410.4 11.5 %convolution_bitcast_fusion = f32[1,1,6144,256]{2,3,1,0:T(8,128)} fusion(f32[6144,256]{0,1:T(8,128)} %bitcast.1, f32[128,256]{1,0:T(8,128)S(1)} %fusion.11, f32[128,256]{1,0:T(8,128)S(1)} %fusion.8), kind=kOutput, calls=%fused_computation.2 | convolution fusion | flops 4831903744 | bytes 12845056 | tf_op jit(solution)/shard_map/dot_general | solution.py:35
  421.9 0.4 fusion
  422.3 0.0 copy-start.1
  422.4 1.1 fusion.7
  423.5 6.6 %copy.22 = f32[1,1,6144,256]{3,2,1,0:T(8,128)} copy(f32[1,1,6144,256]{2,3,1,0:T(8,128)} %convolution_bitcast_fusion) | data formatting | bytes 12582912
  430.0 0.0 copy-done.1
  (13 shorter events, 0.2 us)
Async XLA Ops:
  7.2 12.5 %copy-start = (f32[24576]{0:T(1024)S(1)}, f32[24576]{0:T(1024)}, u32[]{:S(2)}) copy-start(f32[24576]{0:T(1024)} %param.3) | copy-start | bytes 294916
  13.4 145.1 %all-to-all-start = ((f32[4,6144,64]{1,2,0:T(8,128)}), f32[4,6144,64]{1,2,0:T(8,128)}, u32[]{:S(2)}, u32[]{:S(2)}) async-start(f32[4,6144,64]{1,2,0:T(8,128)} %bitcast.53), calls=%async_computation | async-start | bytes 12582912 | tf_op jit(solution)/shard_map/all_to_all | solution.py:14
  19.7 327.1 %all-reduce.3.cloned.1.call-start = ((), (), s32[]{:S(2)}) async-start(), calls=%async_computation.1 | async-start | bytes 524288 | tf_op jit(solution)/shard_map/psum | solution.py:8
  422.3 7.7 %copy-start.1 = (f32[256,256]{1,0:T(8,128)}, f32[256,256]{1,0:T(8,128)S(1)}, u32[]{:S(2)}) copy-start(f32[256,256]{1,0:T(8,128)S(1)} %fusion) | copy-start | bytes 786436
Sparse Core Ops, SparseCore 0:
  221.4 125.3 all-reduce.2
where the time goes:
time: 437 us
  waiting for transfers between devices  264 us (60%)
  other arithmetic  55.9 us (13%)
  matrix products  39 us (9%)
  blocking collectives  38.1 us (9%)
  local copies, waits for them, and re-layouts  17.8 us (4%)
  between operations  15.5 us (4%)
  starting transfers between devices  6.32 us (1%)
    all_to_all x1, waiting for transfers between devices, shards(): lax.all_to_all(snapshots, 'tm', split_axis=0, concat_axis=1, tiled=True)  139 us
    psum x1, waiting for transfers between devices, sum_moments(): lax.psum((first_part, second_part), ('tm', 'rows'))  126 us
    psum x1, blocking collectives, sum_moments(): lax.psum((first_part, second_part), ('tm', 'rows'))  38.1 us
    another operation x6, other arithmetic, shards(): lower_factor = jnp.linalg.cholesky(gram_matrix)  34 us
    another operation x2, other arithmetic, shards(): jax.scipy.linalg.solve_triangular(lower_factor, identity, lower=True)  19.9 us
    dot_general x1, matrix products, shards(): jnp.dot(local_rows.T, local_rows, precision=highest, preferred_element_ty...  17.7 us
    dot_general x1, matrix products, shards(): jnp.dot(local_rows, inverse.T, precision=highest, preferred_element_type=...  11.5 us
  transfers between devices with their start and end apart: 2, of which 2 were waited for; matrix products, arithmetic and copies ran while one was open for 0% of the time, Pallas kernels for 0%

commit v1 on v0

v1 whole, which is shorter than its diff:
```python
import jax
import jax.numpy as jnp
from jax import lax
from jax.sharding import PartitionSpec as P

AXES = ("tm", "rows")


def sum_all(rows):
    count = lax.axis_size("tm") * lax.axis_size("rows")
    held = rows.shape[0]
    each = -(-held // count)
    padded = jnp.pad(rows, ((0, each * count - held), (0, 0)))
    pieces = lax.all_to_all(padded.reshape(count, each, 128), AXES, 0, 0)
    total = jnp.sum(pieces, axis=0)
    spread = lax.all_to_all(
        jnp.broadcast_to(total[None], (count, each, 128)), AXES, 0, 0
    )
    return spread.reshape(count * each, 128)[:held]


def shards(snapshots, last_snapshot):
    highest = lax.Precision.HIGHEST
    own_cols = snapshots.shape[1]
    tail_own = jnp.dot(
        last_snapshot, snapshots, precision=highest, preferred_element_type=jnp.float32
    )
    local_rows = lax.all_to_all(snapshots, "tm", split_axis=0, concat_axis=1, tiled=True)
    row_count, col_count = local_rows.shape
    half = col_count // 2
    tail_part = lax.dynamic_update_slice_in_dim(
        jnp.zeros((col_count,), jnp.float32), tail_own, lax.axis_index("tm") * own_cols, 0
    )
    gram_part = jnp.dot(
        local_rows.T, local_rows, precision=highest, preferred_element_type=jnp.float32
    )
    samples = row_count * lax.axis_size("tm") * lax.axis_size("rows")
    packed = jnp.concatenate(
        [
            gram_part[:half, :half],
            gram_part[half:, :half],
            gram_part[half:, half:],
            tail_part.reshape(2, half),
        ],
        axis=0,
    )
    total = sum_all(packed) / samples
    low = total[half : 2 * half]
    gram_matrix = jnp.concatenate(
        [
            jnp.concatenate([total[:half], low.T], axis=1),
            jnp.concatenate([low, total[2 * half : 3 * half]], axis=1),
        ],
        axis=0,
    )
    tail_column = total[3 * half :].reshape(col_count)
    cross_matrix = jnp.concatenate([gram_matrix[:, 1:], tail_column[:, None]], axis=1)
    lower_factor = jnp.linalg.cholesky(gram_matrix)
    identity = jnp.eye(col_count, dtype=jnp.float32)
    inverse = jax.scipy.linalg.solve_triangular(lower_factor, identity, lower=True)
    factor = lower_factor.T
    basis_rows = jnp.dot(
        local_rows, inverse.T, precision=highest, preferred_element_type=jnp.float32
    )
    projected = jnp.dot(
        inverse, cross_matrix, precision=highest, preferred_element_type=jnp.float32
    )
    operator = jnp.dot(projected, inverse.T, precision=highest, preferred_element_type=jnp.float32)
    return (basis_rows.reshape(1, 1, row_count, col_count), factor, projected, operator)


def solution(mesh):
    in_specs = (P("rows", "tm"), P("rows"))
    out_specs = (P("rows", "tm", None, None), P(), P(), P())
    return jax.shard_map(shards, mesh=mesh, in_specs=in_specs, out_specs=out_specs, check_vma=False)
```

time: 437 us -> 280 us (0.64)
  waiting for transfers between devices: 264 us -> 142 us
  blocking collectives: 38.1 us -> 14.2 us
  between operations: 15.5 us -> 2.21 us
    psum x1 -> x0, waiting for transfers between devices: 126 us -> none  [sum_moments(): lax.psum((first_part, second_part), ('tm', 'rows'))]
    psum x1 -> x0, blocking collectives: 38.1 us -> none  [sum_moments(): lax.psum((first_part, second_part), ('tm', 'rows'))]
    all_to_all x0 -> x1, blocking collectives: none -> 14.2 us  [sum_all(): pieces = lax.all_to_all(padded.reshape(count, each, 128), AXES, 0, 0)]
    all_to_all x0 -> x1, waiting for transfers between devices: none -> 10.4 us  [sum_all(): lax.all_to_all(jnp.broadcast_to(total[None], (count, each, 128)), AXES, 0...]
    all_to_all x1, waiting for transfers between devices: 139 us -> 132 us  [shards(): lax.all_to_all(snapshots, 'tm', split_axis=0, concat_axis=1, tiled=True)]
  transfers between devices with their start and end apart: 2 -> 2, of which waited for: 2 -> 2; matrix products, arithmetic and copies ran while one was open for 0% -> 3% of each run, Pallas kernels for 0% -> 0%
where the time goes in v1:
time: 280 us; the launch traced here: 279 us
  waiting for transfers between devices  142 us (51%)
  other arithmetic  54.1 us (19%)
  matrix products  38.4 us (14%)
  local copies, waits for them, and re-layouts  19.2 us (7%)
  blocking collectives  14.2 us (5%)
  starting transfers between devices  9.08 us (3%)
    all_to_all x1, waiting for transfers between devices, shards(): lax.all_to_all(snapshots, 'tm', split_axis=0, concat_axis=1, tiled=True)  132 us
    another operation x6, other arithmetic, shards(): lower_factor = jnp.linalg.cholesky(gram_matrix)  34 us
    another operation x2, other arithmetic, shards(): jax.scipy.linalg.solve_triangular(lower_factor, identity, lower=True)  19.9 us
    dot_general x1, matrix products, shards(): jnp.dot(local_rows.T, local_rows, precision=highest, preferred_element_ty...  17.1 us
    all_to_all x1, blocking collectives, sum_all(): pieces = lax.all_to_all(padded.reshape(count, each, 128), AXES, 0, 0)  14.2 us
    dot_general x1, matrix products, shards(): jnp.dot(local_rows, inverse.T, precision=highest, preferred_element_type=...  11.5 us
    all_to_all x1, waiting for transfers between devices, sum_all(): lax.all_to_all(jnp.broadcast_to(total[None], (count, each, 128)), AXES, 0...  10.4 us
    unnamed x8, local copies, waits for them, and re-layouts  7.63 us
  transfers between devices with their start and end apart: 2, of which 2 were waited for; matrix products, arithmetic and copies ran while one was open for 3% of the time, Pallas kernels for 0%

profile of v1, /device:TPU:0, one launch (start us, length us, event | category | flops | bytes accessed | tf_op | source)
XLA Modules:
  0.0 279.1 jit_solution(17141766697177694038)
XLA Ops:
  0.6 0.0 copy-start
  0.6 6.2 %copy.39 = f32[8,4,8,6144]{3,2,0,1:T(8,128)} copy(f32[8,4,8,6144]{3,2,1,0:T(8,128)} %bitcast.58) | data formatting | bytes 12582912 | tf_op jit(solution)/shard_map/all_to_all | solution.py:28
  6.8 6.3 %all-to-all-start = ((f32[4,6144,64]{1,2,0:T(8,128)}), f32[4,6144,64]{1,2,0:T(8,128)}, u32[]{:S(2)}, u32[]{:S(2)}) async-start(f32[4,6144,64]{1,2,0:T(8,128)} %bitcast.59), calls=%async_computation | async-start | bytes 12582912 | tf_op jit(solution)/shard_map/all_to_all | solution.py:28
  13.2 0.0 copy-done
  13.2 7.0 %convolution_bitcast_fusion.1 = f32[64]{0:T(128)S(1)} fusion(f32[24576,1]{0,1:T(1,128)S(1)} %bitcast.57, f32[24576,64]{0,1:T(8,128)} %param.2), kind=kOutput, calls=%fused_computation.6 | convolution fusion | flops 18874368 | bytes 6390016 | tf_op jit(solution)/shard_map/dot_general | solution.py:25
  20.1 0.2 dynamic_update_slice.3
  20.4 131.5 %all-to-all-done = f32[4,6144,64]{1,2,0:T(8,128)} async-done(((f32[4,6144,64]{1,2,0:T(8,128)}), f32[4,6144,64]{1,2,0:T(8,128)}, u32[]{:S(2)}, u32[]{:S(2)}) %all-to-all-start) | async-done | bytes 6291488 | tf_op jit(solution)/shard_map/all_to_all | solution.py:28
  151.9 17.1 %fusion.20 = f32[256,256]{1,0:T(8,128)S(1)} fusion(f32[6144,256]{0,1:T(8,128)} %bitcast.1), kind=kOutput, calls=%fused_computation.51 | convolution fusion | flops 4831838208 | bytes 6553600 | tf_op jit(solution)/shard_map/dot_general | solution.py:34
  169.1 14.2 %all_to_all.29 = f32[32,13,128]{2,1,0:T(8,128)S(1)} all-to-all(f32[32,13,128]{2,1,0:T(8,128)S(1)} %reshape.44), channel_id=1, replica_groups=mesh['tm'=4,'rows'=8] {'tm','rows'}, dimensions={0} | all-to-all | bytes 425984 | tf_op jit(solution)/shard_map/all_to_all | solution.py:14
  183.3 0.7 broadcast_in_dim.12
  184.0 2.8 all-to-all-start.2
  186.9 10.4 %all-to-all-done.2 = f32[32,13,128]{2,1,0:T(8,128)S(1)} async-done(((f32[32,13,128]{2,1,0:T(8,128)}), f32[32,13,128]{2,1,0:T(8,128)S(1)}, u32[]{:S(2)}, u32[]{:S(2)}) %all-to-all-start.2) | async-done | bytes 213024 | tf_op jit(solution)/shard_map/all_to_all | solution.py:16
  197.3 0.1 copy.35
  197.5 0.1 copy.36
  197.6 0.1 copy.30
  197.7 0.1 copy.31
  197.9 11.7 %cholesky.50 = f32[128,128]{1,0:T(8,128)S(1)} custom-call(f32[128,128]{1,0:T(8,128)S(1)} %cholesky.118), custom_call_target="Cholesky" | custom-call | tf_op jit(solution)/shard_map/jit(cholesky)/cholesky | solution.py:58
  209.7 0.1 copy.32
  209.8 9.8 %custom-call.15 = f32[1,128,128]{1,2,0:T(8,128)S(1)} custom-call(f32[1,128,128]{2,1,0:T(8,128)S(1)} %get-tuple-element.47), custom_call_target="InvertDiagBlocksLowerTriangular" | custom-call | tf_op jit(solution)/shard_map/jit(cholesky)/cholesky | solution.py:58
  219.6 0.2 constant_dynamic-update-slice_fusion.1
  219.8 0.3 convolution_subtract_fusion.1
  220.1 11.7 %cholesky.105 = f32[128,128]{1,0:T(8,128)S(1)} custom-call(f32[128,128]{1,0:T(8,128)S(1)} %convolution_subtract_fusion.1), custom_call_target="Cholesky" | custom-call | tf_op jit(solution)/shard_map/jit(cholesky)/cholesky | solution.py:58
  231.8 0.6 compare_reduce_fusion
  233.8 0.8 copy.34
  234.7 0.1 triangular_solve.63
  234.7 4.0 %while.1 = (s32[]{:T(128)}, f32[256,256]{1,0:T(8,128)S(1)}, s32[2,2]{1,0:T(2,128)S(1)}, f32[2,128,128]{2,1,0:T(8,128)S(1)}, s32[]{:T(128)}) while((s32[]{:T(128)}, f32[256,256]{1,0:T(8,128)S(1)}, s32[2,2]{1,0:T(2,128)S(1)}, f32[2,128,128]{2,1,0:T(8,128)S(1)}, s32[]{:T(128)}) %tuple.35), condition=%wide.while_cond, body=%wide.while_body.sunk | while | flops 2 | bytes 131189 | solution.py:60
  234.8 0.6 fusion.32
  235.3 1.4 bitcast_dynamic-update-slice_fusion.2
  236.8 0.6 fusion.32
  237.3 1.4 bitcast_dynamic-update-slice_fusion.2
  238.7 19.9 %custom-call.16 = f32[2,128,128]{1,2,0:T(8,128)S(1)} custom-call(f32[2,128,128]{2,1,0:T(8,128)S(1)} %get-tuple-element.11), custom_call_target="InvertDiagBlocksLowerTriangular" | custom-call | tf_op jit(solution)/shard_map/jit(_solve_triangular)/triangular_solve | solution.py:60
  258.6 0.3 fusion.8
  258.9 0.3 convolution_subtract_fusion
  259.2 0.3 fusion.11
  259.5 11.5 %convolution_bitcast_fusion = f32[1,1,6144,256]{2,3,1,0:T(8,128)} fusion(f32[6144,256]{0,1:T(8,128)} %bitcast.1, f32[128,256]{1,0:T(8,128)S(1)} %fusion.11, f32[128,256]{1,0:T(8,128)S(1)} %fusion.8), kind=kOutput, calls=%fused_computation.2 | convolution fusion | flops 4831903744 | bytes 12845056 | tf_op jit(solution)/shard_map/dot_general | solution.py:62
  271.0 0.4 fusion
  271.4 0.0 copy-start.1
  271.4 1.1 fusion.7
  272.6 6.6 %copy.33 = f32[1,1,6144,256]{3,2,1,0:T(8,128)} copy(f32[1,1,6144,256]{2,3,1,0:T(8,128)} %convolution_bitcast_fusion) | data formatting | bytes 12582912
  279.1 0.0 copy-done.1
  (25 shorter events, 0.5 us)
Async XLA Ops:
  0.6 12.5 %copy-start = (f32[24576]{0:T(1024)S(1)}, f32[24576]{0:T(1024)}, u32[]{:S(2)}) copy-start(f32[24576]{0:T(1024)} %param.3) | copy-start | bytes 294916
  6.8 145.1 %all-to-all-start = ((f32[4,6144,64]{1,2,0:T(8,128)}), f32[4,6144,64]{1,2,0:T(8,128)}, u32[]{:S(2)}, u32[]{:S(2)}) async-start(f32[4,6144,64]{1,2,0:T(8,128)} %bitcast.59), calls=%async_computation | async-start | bytes 12582912 | tf_op jit(solution)/shard_map/all_to_all | solution.py:28
  184.0 13.2 %all-to-all-start.2 = ((f32[32,13,128]{2,1,0:T(8,128)}), f32[32,13,128]{2,1,0:T(8,128)S(1)}, u32[]{:S(2)}, u32[]{:S(2)}) async-start(f32[32,13,128]{2,1,0:T(8,128)} %broadcast_in_dim.12), calls=%async_computation.2 | async-start | bytes 524288 | tf_op jit(solution)/shard_map/all_to_all | solution.py:16
  271.4 7.7 %copy-start.1 = (f32[256,256]{1,0:T(8,128)}, f32[256,256]{1,0:T(8,128)S(1)}, u32[]{:S(2)}) copy-start(f32[256,256]{1,0:T(8,128)S(1)} %fusion) | copy-start | bytes 786436

commit v2 on v0

v2 whole, which is shorter than its diff:
```python
import functools

import jax
import jax.numpy as jnp
from jax import lax
from jax.experimental import pallas as pl
from jax.experimental.pallas import tpu as pltpu
from jax.sharding import PartitionSpec as P

AXES = ("tm", "rows")
HIGHEST = lax.Precision.HIGHEST
LANES = 128
PANEL = 32
BASIS_TILE = 512
VMEM_LIMIT = 48 * 1024 * 1024


def iota(shape, dim):
    return lax.broadcasted_iota(jnp.int32, shape, dim)


def split(values):
    first = values.astype(jnp.bfloat16)
    second = (values - first.astype(jnp.float32)).astype(jnp.bfloat16)
    return first, second


def dot(left, right, dims=((1,), (0,)), precision=None):
    return lax.dot_general(
        left, right, (dims, ((), ())), precision=precision, preferred_element_type=jnp.float32
    )


def chunk_kernel(*refs, peers, packed_rows):
    pieces = refs[:peers]
    sum_ref, tail_ref, out_ref, high_ref, low_ref, cols_ref = refs[peers:]
    width, depth = pieces[0].shape
    count = width * peers
    me = lax.axis_index("tm")
    for offset, piece in enumerate(pieces):
        start = pl.multiple_of(jnp.bitwise_xor(me, offset) * width, width)
        cols_ref[pl.ds(start, width), :] = piece[...]
    total = None
    step = 2 * LANES if depth % (2 * LANES) == 0 else LANES
    for at in range(0, depth, step):
        cols = cols_ref[:, at : at + step]
        rows = cols.T
        high, low = split(rows)
        high_ref[at : at + step, :] = high
        low_ref[at : at + step, :] = low
        part = dot(cols, rows, precision=HIGHEST)
        total = part if total is None else total + part
    half = count // 2
    blocks = [total[:half, :half], total[:half, half:], total[half:, half:]]
    for index, block in enumerate(blocks):
        at = index * half
        out_ref[at : at + half, :] = sum_ref[at : at + half, :] + block
    pad = jnp.zeros((packed_rows - 3 * half - 8, LANES), jnp.float32)
    out_ref[3 * half : 3 * half + 8, :] = tail_ref[...]
    out_ref[3 * half + 8 :, :] = pad


def add_chunk(pieces, running, tail):
    peers = len(pieces)
    width, depth = pieces[0].shape
    count = width * peers
    packed_rows = running.shape[0]
    vmem = pl.BlockSpec(memory_space=pltpu.VMEM)
    return pl.pallas_call(
        functools.partial(chunk_kernel, peers=peers, packed_rows=packed_rows),
        out_shape=(
            jax.ShapeDtypeStruct((packed_rows, LANES), jnp.float32),
            jax.ShapeDtypeStruct((depth, count), jnp.bfloat16),
            jax.ShapeDtypeStruct((depth, count), jnp.bfloat16),
        ),
        in_specs=[vmem] * (peers + 2),
        out_specs=(vmem,) * 3,
        scratch_shapes=[pltpu.VMEM((count, depth), jnp.float32)],
        compiler_params=pltpu.CompilerParams(vmem_limit_bytes=VMEM_LIMIT),
        cost_estimate=pl.CostEstimate(
            flops=12 * count * count * depth,
            bytes_accessed=8 * count * depth,
            transcendentals=0,
        ),
        name="gram_chunk",
    )(*pieces, running, tail)


def eliminate(rows, at):
    n, count = rows.shape
    sub = iota((n, LANES), 0)
    block = rows[:, at : at + n]
    columns = [jnp.broadcast_to(block[:, k : k + 1], (n, LANES)) for k in range(n)]
    lane, sub_all = iota((n, count), 1), iota((n, count), 0)
    own = (lane >= at) & (lane < at + n)
    rows = jnp.where(own, jnp.where(lane - at == sub_all, 1.0, 0.0), rows)
    halves = [rows[:, h : h + LANES] for h in range(0, count, LANES)]
    pivots = jnp.ones((n, LANES), jnp.float32)
    inverses = jnp.zeros((n, LANES), jnp.float32)
    for k in range(n):
        pivot = columns[k][k : k + 1, :]
        inverse = 1.0 / pivot
        pivots = jnp.where(sub == k, jnp.broadcast_to(pivot, (n, LANES)), pivots)
        inverses = jnp.where(sub == k, jnp.broadcast_to(inverse, (n, LANES)), inverses)
        factor = jnp.where(sub > k, columns[k] * inverse, 0.0)
        for j in range(k + 1, n):
            columns[j] = columns[j] - factor * columns[j][k : k + 1, :]
        halves = [half - factor * half[k : k + 1, :] for half in halves]
    upper = jnp.zeros((n, LANES), jnp.float32)
    lane_here = iota((n, LANES), 1) + at // LANES * LANES
    for k in range(n):
        upper = jnp.where(lane_here == at + k, columns[k], upper)
    return halves, upper, pivots, inverses


def factorize(work, factor_ref, inverse_ref):
    count = work.shape[0]
    n = PANEL
    lane, sub = iota((n, LANES), 1), iota((n, LANES), 0)
    for at in range(0, count, n):
        below = at + n
        halves, upper, pivots, inverses = eliminate(work[at:below, :], at)
        root = lax.rsqrt(pivots)
        root = root * (1.5 - 0.5 * pivots * root * root)
        scaled = []
        for h, half in enumerate(halves):
            column = lane + h * LANES
            mixed = jnp.where((column >= at) & (column < below), upper, half)
            cut = slice(h * LANES, (h + 1) * LANES)
            factor_ref[at:below, cut] = jnp.where(column >= sub + at, mixed * root, 0.0)
            inverse_ref[at:below, cut] = jnp.where(column <= sub + at, half * root, 0.0)
            scaled.append(jnp.where(column >= below, half * inverses, 0.0))
        if below == count:
            break
        skip = below // LANES
        multiplier = jnp.concatenate(scaled[skip:], axis=1)
        update = dot(
            multiplier, jnp.concatenate(halves, axis=1), dims=((0,), (0,)), precision=HIGHEST
        )
        wide = iota((count - below, count), 1)
        old = jnp.where((wide >= at) & (wide < below), 0.0, work[below:, :])
        work[below:, :] = old - update[below - skip * LANES :, :]


def finish_kernel(*refs, chunks, samples):
    total_ref = refs[0]
    high_in, low_in = refs[1 : 1 + chunks], refs[1 + chunks : 1 + 2 * chunks]
    basis_ref, factor_ref, projected_ref, operator_ref = refs[1 + 2 * chunks : 5 + 2 * chunks]
    work, inverse_ref, high_ref, low_ref, rows_ref, in_sem, out_sem = refs[5 + 2 * chunks :]
    count = work.shape[0]
    half = count // 2
    depth = rows_ref.shape[0]

    loads = []
    at = 0
    for index in range(chunks):
        size = high_in[index].shape[0]
        for source, target, lane in ((high_in, high_ref, 0), (low_in, low_ref, 1)):
            copy = pltpu.make_async_copy(
                source[index], target.at[pl.ds(at, size)], in_sem.at[2 * index + lane]
            )
            copy.start()
            loads.append(copy)
        at += size

    scale = 1.0 / samples
    work[:half, :half] = total_ref[:half, :] * scale
    work[:half, half:] = total_ref[half : 2 * half, :] * scale
    work[half:, :half] = jnp.zeros((half, half), jnp.float32)
    work[half:, half:] = total_ref[2 * half : 3 * half, :] * scale
    factorize(work, factor_ref, inverse_ref)

    inverse = inverse_ref[...]
    turned_high, turned_low = split(inverse.T)
    for copy in loads:
        copy.wait()
    stores = []
    for index, at in enumerate(range(0, depth, BASIS_TILE)):
        tile = pl.ds(at, BASIS_TILE)
        high, low = high_ref[tile, :], low_ref[tile, :]
        rows_ref[tile, :] = (
            dot(high, turned_high) + (dot(high, turned_low) + dot(low, turned_high))
        )
        copy = pltpu.make_async_copy(
            rows_ref.at[tile], basis_ref.at[tile], out_sem.at[index]
        )
        copy.start()
        stores.append(copy)

    tail = [total_ref[3 * half + r : 3 * half + r + 1, :] * scale for r in range(2)]
    column = jnp.sum(inverse * jnp.concatenate(tail, axis=1), axis=1, keepdims=True)
    shifted = pltpu.roll(factor_ref[...], count - 1, 1)
    projected = jnp.where(iota((count, count), 1) == count - 1, column, shifted)
    projected_ref[...] = projected
    operator_ref[...] = dot(projected, inverse, dims=((1,), (1,)), precision=HIGHEST)
    for copy in stores:
        copy.wait()


def finish(total, highs, lows, samples):
    chunks = len(highs)
    count = highs[0].shape[1]
    depth = sum(h.shape[0] for h in highs)
    square = jax.ShapeDtypeStruct((count, count), jnp.float32)
    vmem = pl.BlockSpec(memory_space=pltpu.VMEM)
    far = pl.BlockSpec(memory_space=pl.ANY)
    return pl.pallas_call(
        functools.partial(finish_kernel, chunks=chunks, samples=samples),
        out_shape=(jax.ShapeDtypeStruct((depth, count), jnp.float32), square, square, square),
        in_specs=[vmem] + [far] * (2 * chunks),
        out_specs=(far, vmem, vmem, vmem),
        scratch_shapes=[
            pltpu.VMEM((count, count), jnp.float32),
            pltpu.VMEM((count, count), jnp.float32),
            pltpu.VMEM((depth, count), jnp.bfloat16),
            pltpu.VMEM((depth, count), jnp.bfloat16),
            pltpu.VMEM((depth, count), jnp.float32),
            pltpu.SemaphoreType.DMA((2 * chunks,)),
            pltpu.SemaphoreType.DMA((depth // BASIS_TILE,)),
        ],
        compiler_params=pltpu.CompilerParams(vmem_limit_bytes=VMEM_LIMIT),
        name="factor_and_basis",
    )(total, *highs, *lows)


def sum_all(packed):
    devices = lax.axis_size("tm") * lax.axis_size("rows")
    each = packed.shape[0] // devices
    pieces = lax.all_to_all(packed.reshape(devices, each, LANES), AXES, 0, 0)
    total = jnp.sum(pieces, axis=0)
    spread = lax.all_to_all(
        jnp.broadcast_to(total[None], (devices, each, LANES)), AXES, 0, 0
    )
    return spread.reshape(devices * each, LANES)


def shards(snapshots, last_snapshot):
    peers = lax.axis_size("tm")
    devices = peers * lax.axis_size("rows")
    me = lax.axis_index("tm")
    own_cols = snapshots.shape[1]
    count = own_cols * peers
    depth = snapshots.shape[0] // peers
    columns = snapshots.T

    small = depth // 8
    large = (depth - small) // (3 * LANES) * LANES
    sizes = [large, large, depth - small - 2 * large, small]

    chunks = []
    start = 0
    for size in sizes:
        pieces = []
        for offset in range(peers):
            target = jnp.bitwise_xor(me, offset)
            piece = lax.dynamic_slice(columns, (0, target * depth + start), (own_cols, size))
            if offset:
                pairs = [(i, i ^ offset) for i in range(peers)]
                piece = lax.ppermute(piece, "tm", pairs)
            pieces.append(piece)
        chunks.append(pieces)
        start += size

    tail_own = jnp.dot(
        columns, last_snapshot, precision=HIGHEST, preferred_element_type=jnp.float32
    )
    tail = lax.dynamic_update_slice_in_dim(
        jnp.zeros((8 * LANES,), jnp.float32), tail_own, me * own_cols, 0
    ).reshape(8, LANES)

    rows_needed = 3 * (count // 2) + 8
    each = -(-rows_needed // (8 * devices)) * 8
    running = jnp.zeros((each * devices, LANES), jnp.float32)
    highs, lows = [], []
    for pieces in chunks:
        running, high, low = add_chunk(pieces, running, tail)
        highs.append(high)
        lows.append(low)
    total = sum_all(running)
    samples = depth * devices
    basis, factor, projected, operator = finish(total, highs, lows, samples)
    return (basis.reshape(1, 1, depth, count), factor, projected, operator)


def solution(mesh):
    in_specs = (P("rows", "tm"), P("rows"))
    out_specs = (P("rows", "tm", None, None), P(), P(), P())
    return jax.shard_map(shards, mesh=mesh, in_specs=in_specs, out_specs=out_specs, check_vma=False)
```

time: 437 us -> 195 us (0.45)
  waiting for transfers between devices: 264 us -> 40.4 us
  starting transfers between devices: 6.32 us -> 76 us
  other arithmetic: 55.9 us -> 0.04 us
  matrix products: 39 us -> 4.97 us
  Pallas kernels: 0 us -> 26.2 us
  between operations: 15.5 us -> 1.06 us
  blocking collectives: 38.1 us -> 27.9 us
    all_to_all x1 -> x0, waiting for transfers between devices: 139 us -> none  [shards(): lax.all_to_all(snapshots, 'tm', split_axis=0, concat_axis=1, tiled=True)]
    psum x1 -> x0, waiting for transfers between devices: 126 us -> none  [sum_moments(): lax.psum((first_part, second_part), ('tm', 'rows'))]
    ppermute x0 -> x12, starting transfers between devices: none -> 76 us  [shards(): piece = lax.ppermute(piece, 'tm', pairs)]
    another operation x8 -> x0, other arithmetic: 53.9 us -> none  [the longest x6 34 us: shards(): lower_factor = jnp.linalg.cholesky(gram_matrix)]
    ppermute x0 -> x12, waiting for transfers between devices: none -> 40.4 us  [shards(): piece = lax.ppermute(piece, 'tm', pairs)]
    psum x1 -> x0, blocking collectives: 38.1 us -> none  [sum_moments(): lax.psum((first_part, second_part), ('tm', 'rows'))]
    dot_general x5 -> x1, matrix products: 37.7 us -> 4.97 us  [shards(): jnp.dot(columns, last_snapshot, precision=HIGHEST, preferred_element_type...]
    all_to_all x0 -> x2, blocking collectives: none -> 27.9 us  [the longest x1 15.1 us: sum_all(): pieces = lax.all_to_all(packed.reshape(devices, each, LANES), AXES, 0, 0)]
  transfers between devices with their start and end apart: 2 -> 12, of which waited for: 2 -> 4; matrix products, arithmetic and copies ran while one was open for 0% -> 3% of each run, Pallas kernels for 0% -> 4%
where the time goes in v2:
time: 195 us
  starting transfers between devices  76 us (39%)
  waiting for transfers between devices  40.4 us (21%)
  blocking collectives  27.9 us (14%)
  Pallas kernels  26.2 us (13%)
  local copies, waits for them, and re-layouts  18.1 us (9%)
  matrix products  4.97 us (3%)
    ppermute x12, starting transfers between devices, shards(): piece = lax.ppermute(piece, 'tm', pairs)  76 us
    ppermute x12, waiting for transfers between devices, shards(): piece = lax.ppermute(piece, 'tm', pairs)  40.4 us
    pallas_call x1, Pallas kernels, finish(): pl.pallas_call(functools.partial(finish_kernel, chunks=chunks, samples=sa...  16.3 us
    all_to_all x1, blocking collectives, sum_all(): pieces = lax.all_to_all(packed.reshape(devices, each, LANES), AXES, 0, 0)  15.1 us
    all_to_all x1, blocking collectives, sum_all(): lax.all_to_all(jnp.broadcast_to(total[None], (devices, each, LANES)), AXE...  12.8 us
    unnamed x36, local copies, waits for them, and re-layouts  12 us
    pallas_call x4, Pallas kernels, add_chunk(): pl.pallas_call(functools.partial(chunk_kernel, peers=peers, packed_rows=p...  9.83 us
    dynamic_slice x2, local copies, waits for them, and re-layouts, shards(): lax.dynamic_slice(columns, (0, target * depth + start), (own_cols, size))  5.71 us
  transfers between devices with their start and end apart: 12, of which 4 were waited for; matrix products, arithmetic and copies ran while one was open for 3% of the time, Pallas kernels for 4%

profile of v2, /device:TPU:0, one launch (start us, length us, event | category | flops | bytes accessed | tf_op | source)
XLA Modules:
  0.0 194.7 jit_solution(8578235979348108193)
XLA Ops:
  0.6 0.0 copy-start
  0.7 0.0 copy-start.17
  0.7 4.4 %dynamic-slice_bitcast_fusion = (f32[64,1792]{1,0:T(8,128)S(1)}, f32[64,1792]{1,0:T(8,128)S(1)}, f32[64,1792]{1,0:T(8,128)S(1)}, f32[64,1792]{1,0:T(8,128)S(1)},...) fusion(f32[24576,64]{0,1:T(8,128)} %param.2, ...), kind=kLoop, calls=%fused_computation.3 | loop fusion | bytes 11010096 | tf_op jit(solution)/shard_map/dynamic_slice | solution.py:256
  5.2 5.0 %collective-permute-start.11 = (f32[64,1792]{1,0:T(8,128)S(1)}, f32[64,1792]{1,0:T(8,128)S(1)}, u32[]{:S(2)}, u32[]{:S(2)}) collective-permute-start(f32[64,1792]{1,0:T(8,128)S(1)} %get-tuple-element.36), channel_id=1, source_target_pairs={{0,24},{8,16},{16,8},{24,0},{1,25},{9,17},{17,9},{25,1},{2,26},{10... | collective-permute-start | bytes 1376264 | tf_op jit(solution)/shard_map/ppermute | solution.py:259
  10.2 0.0 collective-permute-start.10
  10.2 0.6 collective-permute-start.9
  10.8 3.8 %collective-permute-start.8 = (f32[64,1792]{1,0:T(8,128)S(1)}, f32[64,1792]{1,0:T(8,128)S(1)}, u32[]{:S(2)}, u32[]{:S(2)}) collective-permute-start(f32[64,1792]{1,0:T(8,128)S(1)} %get-tuple-element.40), channel_id=1, source_target_pairs={{0,24},{8,16},{16,8},{24,0},{1,25},{9,17},{17,9},{25,1},{2,26},{10... | collective-permute-start | bytes 1376264 | tf_op jit(solution)/shard_map/ppermute | solution.py:259
  14.6 0.0 collective-permute-start.7
  14.6 7.1 %collective-permute-done.11.refs_3_ = f32[64,1792]{1,0:T(8,128)S(1)} collective-permute-done((f32[64,1792]{1,0:T(8,128)S(1)}, f32[64,1792]{1,0:T(8,128)S(1)}, u32[]{:S(2)}, u32[]{:S(2)}) %collective-permute-start.11) | collective-permute-done | bytes 458784 | tf_op jit(solution)/shard_map/ppermute | solution.py:259
  21.7 0.0 copy-start.11
  21.7 20.2 %collective-permute-start.6 = (f32[64,1792]{1,0:T(8,128)}, f32[64,1792]{1,0:T(8,128)}, u32[]{:S(2)}, u32[]{:S(2)}) collective-permute-start(f32[64,1792]{1,0:T(8,128)} %get-tuple-element.42), channel_id=1, source_target_pairs={{0,8},{8,0},{16,24},{24,16},{1,9},{9,1},{17,25},{25,17},{2,10},{10... | collective-permute-start | bytes 1376264 | tf_op jit(solution)/shard_map/ppermute | solution.py:259
  41.9 28.1 %collective-permute-done.10.refs_2_ = f32[64,1792]{1,0:T(8,128)S(1)} collective-permute-done((f32[64,1792]{1,0:T(8,128)S(1)}, f32[64,1792]{1,0:T(8,128)S(1)}, u32[]{:S(2)}, u32[]{:S(2)}) %collective-permute-start.10) | collective-permute-done | bytes 458784 | tf_op jit(solution)/shard_map/ppermute | solution.py:259
  70.0 0.0 copy-start.13
  70.0 2.7 %collective-permute-start.5 = (f32[64,1792]{1,0:T(8,128)}, f32[64,1792]{1,0:T(8,128)}, u32[]{:S(2)}, u32[]{:S(2)}) collective-permute-start(f32[64,1792]{1,0:T(8,128)} %get-tuple-element.44), channel_id=1, source_target_pairs={{0,24},{8,16},{16,8},{24,0},{1,25},{9,17},{17,9},{25,1},{2,26},{10... | collective-permute-start | bytes 1376264 | tf_op jit(solution)/shard_map/ppermute | solution.py:259
  72.7 0.0 collective-permute-done.9.refs_1_
  72.7 0.0 copy-start.15
  72.7 0.0 collective-permute-start.4
  72.7 0.0 collective-permute-done.8.refs_3_
  72.7 0.0 copy-start.9
  72.7 27.4 %collective-permute-start.3 = (f32[64,1792]{1,0:T(8,128)}, f32[64,1792]{1,0:T(8,128)}, u32[]{:S(2)}, u32[]{:S(2)}) collective-permute-start(f32[64,1792]{1,0:T(8,128)} %get-tuple-element.46), channel_id=1, source_target_pairs={{0,8},{8,0},{16,24},{24,16},{1,9},{9,1},{17,25},{25,17},{2,10},{10... | collective-permute-start | bytes 1376264 | tf_op jit(solution)/shard_map/ppermute | solution.py:259
  100.1 0.0 copy-done
  100.1 0.0 copy-done.17
  100.1 5.0 %fusion.2 = f32[64]{0:T(128)S(1)} fusion(f32[24576,1]{0,1:T(1,128)S(1)} %bitcast.45, f32[24576,64]{0,1:T(8,128)S(1)} %copy-done.17), kind=kOutput, calls=%fused_computation.2 | convolution fusion | flops 18874368 | bytes 6390016 | tf_op jit(solution)/shard_map/dot_general | solution.py:264
  105.0 0.4 dynamic_update_slice.3
  105.4 1.3 dynamic-slice_bitcast_fusion.12
  106.7 0.0 copy-done.11
  106.7 0.0 copy-done.13
  106.7 0.0 copy-done.15
  106.7 0.0 copy-start.12
  106.8 1.0 copy-done.12
  107.8 0.0 copy-start.14
  107.8 1.0 copy-done.14
  108.8 1.0 copy-done.16
  109.8 2.1 %gram_chunk.4 = (f32[512,128]{1,0:T(8,128)S(1)}, bf16[1792,256]{1,0:T(8,128)(2,1)S(1)}, bf16[1792,256]{1,0:T(8,128)(2,1)S(1)}) custom-call(f32[64,1792]{1,0:T(8,128)S(1)} %get-tuple-element.39.refs_0_, f32[64,1792]{1,0:T(8,128)S(1)} %copy-done.16, f32[64,1792]{1,0:T(8,128)S(1)} %copy-done.14, f32[64,1792]{1,0:T(8,128)S(1)} %copy-done.12, ...), custom_call_target="tpu_custom_call" | custom-call | flops 1409286144 | bytes 3670016 | tf_op jit(solution)/shard_map/gram_chunk/pallas_call | solution.py:69
  111.9 0.0 copy-done.9
  111.9 0.0 collective-permute-done.7.refs_2_
  111.9 2.7 %collective-permute-start.2 = (f32[64,768]{1,0:T(8,128)S(1)}, f32[64,768]{1,0:T(8,128)S(1)}, u32[]{:S(2)}, u32[]{:S(2)}) collective-permute-start(f32[64,768]{1,0:T(8,128)S(1)} %get-tuple-element.48), channel_id=1, source_target_pairs={{0,24},{8,16},{16,8},{24,0},{1,25},{9,17},{17,9},{25,1},{2,26},{10... | collective-permute-start | bytes 589832 | tf_op jit(solution)/shard_map/ppermute | solution.py:259
  114.7 0.0 collective-permute-done.6.refs_1_
  114.7 0.0 collective-permute-start.1
  114.7 0.0 collective-permute-done.5.refs_3_
  114.7 13.6 %collective-permute-start = (f32[64,768]{1,0:T(8,128)S(1)}, f32[64,768]{1,0:T(8,128)S(1)}, u32[]{:S(2)}, u32[]{:S(2)}) collective-permute-start(f32[64,768]{1,0:T(8,128)S(1)} %get-tuple-element.50), channel_id=1, source_target_pairs={{0,8},{8,0},{16,24},{24,16},{1,9},{9,1},{17,25},{25,17},{2,10},{10... | collective-permute-start | bytes 589832 | tf_op jit(solution)/shard_map/ppermute | solution.py:259
  128.3 1.0 copy-done.6
  129.3 1.0 copy-done.10
  130.3 3.3 %gram_chunk.5 = (f32[512,128]{1,0:T(8,128)S(1)}, bf16[1792,256]{1,0:T(8,128)(2,1)S(1)}, bf16[1792,256]{1,0:T(8,128)(2,1)S(1)}) custom-call(f32[64,1792]{1,0:T(8,128)S(1)} %copy-done.6, f32[64,1792]{1,0:T(8,128)} %collective-permute-done.6.refs_1_, f32[64,1792]{1,0:T(8,128)} %collective-permute-done.7.refs_2_, f32[64,1792]{1,0:T(8,128)S(1)} %copy-done.10, ...), custom_call_target="tpu_custom_call" | custom-call | flops 1409286144 | bytes 3670016 | tf_op jit(solution)/shard_map/gram_chunk/pallas_call | solution.py:69
  133.6 0.0 copy-start.1
  133.6 0.9 copy-done.1
  134.5 3.1 %collective-permute-done.4.refs_2_ = f32[64,1792]{1,0:T(8,128)} collective-permute-done((f32[64,1792]{1,0:T(8,128)}, f32[64,1792]{1,0:T(8,128)}, u32[]{:S(2)}, u32[]{:S(2)}) %collective-permute-start.4) | collective-permute-done | bytes 458784 | tf_op jit(solution)/shard_map/ppermute | solution.py:259
  137.6 0.0 collective-permute-done.3.refs_1_
  137.6 3.4 %gram_chunk.6 = (f32[512,128]{1,0:T(8,128)S(1)}, bf16[1792,256]{1,0:T(8,128)(2,1)S(1)}, bf16[1792,256]{1,0:T(8,128)(2,1)S(1)}) custom-call(f32[64,1792]{1,0:T(8,128)S(1)} %get-tuple-element.47.refs_0_, f32[64,1792]{1,0:T(8,128)} %collective-permute-done.3.refs_1_, f32[64,1792]{1,0:T(8,128)} %collective-permute-done.4.refs_2_, ...), custom_call_target="tpu_custom_call" | custom-call | flops 1409286144 | bytes 3670016 | tf_op jit(solution)/shard_map/gram_chunk/pallas_call | solution.py:69
  141.0 0.0 copy-start.3
  141.0 0.9 copy-done.3
  141.9 0.9 copy-done.5
  142.9 0.0 collective-permute-done.2.refs_3_
  142.9 2.1 %collective-permute-done.1.refs_2_ = f32[64,768]{1,0:T(8,128)S(1)} collective-permute-done((f32[64,768]{1,0:T(8,128)S(1)}, f32[64,768]{1,0:T(8,128)S(1)}, u32[]{:S(2)}, u32[]{:S(2)}) %collective-permute-start.1) | collective-permute-done | bytes 196640 | tf_op jit(solution)/shard_map/ppermute | solution.py:259
  145.0 0.0 collective-permute-done.refs_1_
  145.0 1.1 gram_chunk.7
  146.0 0.0 copy-start.7
  146.1 0.7 copy-done.7
  146.8 15.1 %all_to_all.10 = f32[32,16,128]{2,1,0:T(8,128)S(1)} all-to-all(f32[32,16,128]{2,1,0:T(8,128)S(1)} %bitcast.47), channel_id=1, replica_groups=mesh['tm'=4,'rows'=8] {'tm','rows'}, dimensions={0} | all-to-all | bytes 524288 | tf_op jit(solution)/shard_map/all_to_all | solution.py:229
  162.0 12.8 %all_to_all.11 = f32[32,16,128]{2,1,0:T(8,128)S(1)} all-to-all(f32[32,16,128]{2,1,0:T(8,128)S(1)} %broadcast_in_dim.14), channel_id=1, replica_groups=mesh['tm'=4,'rows'=8] {'tm','rows'}, dimensions={0} | all-to-all | bytes 524288 | tf_op jit(solution)/shard_map/all_to_all | solution.py:231
  174.8 1.2 copy-done.2
  176.0 1.2 copy-done.4
  177.2 1.0 copy-done.8
  178.1 16.3 %factor_and_basis.1 = (f32[6144,256]{1,0:T(8,128)}, f32[256,256]{1,0:T(8,128)}, f32[256,256]{1,0:T(8,128)}, f32[256,256]{1,0:T(8,128)}) custom-call(f32[512,128]{1,0:T(8,128)S(1)} %bitcast.46, bf16[1792,256]{1,0:T(8,128)(2,1)S(1)} %get-tuple-element.24.refs_1_, bf16[1792,256]{1,0:T(8,128)(2,1)S(1)} %get-tuple-element.25.refs_2_, ...), custom_call_target="tpu_custom_call" | custom-call | tf_op jit(solution)/shard_map/factor_and_basis/pallas_call | solution.py:207
  (11 shorter events, 0.1 us)
Async XLA Ops:
  0.6 99.4 %copy-start = (f32[24576]{0:T(1024)S(1)}, f32[24576]{0:T(1024)}, u32[]{:S(2)}) copy-start(f32[24576]{0:T(1024)} %param.3) | copy-start | bytes 294916
  0.7 99.3 %copy-start.17 = (f32[24576,64]{0,1:T(8,128)S(1)}, f32[24576,64]{0,1:T(8,128)}, u32[]{:S(2)}) copy-start(f32[24576,64]{0,1:T(8,128)} %param.2) | copy-start | bytes 18874372
  5.2 16.5 %collective-permute-start.11 = (f32[64,1792]{1,0:T(8,128)S(1)}, f32[64,1792]{1,0:T(8,128)S(1)}, u32[]{:S(2)}, u32[]{:S(2)}) collective-permute-start(f32[64,1792]{1,0:T(8,128)S(1)} %get-tuple-element.36), channel_id=1, source_target_pairs={{0,24},{8,16},{16,8},{24,0},{1,25},{9,17},{17,9},{25,1},{2,26},{10... | collective-permute-start | bytes 1376264 | tf_op jit(solution)/shard_map/ppermute | solution.py:259
  10.2 59.8 %collective-permute-start.10 = (f32[64,1792]{1,0:T(8,128)S(1)}, f32[64,1792]{1,0:T(8,128)S(1)}, u32[]{:S(2)}, u32[]{:S(2)}) collective-permute-start(f32[64,1792]{1,0:T(8,128)S(1)} %get-tuple-element.37), channel_id=1, source_target_pairs={{0,16},{8,24},{16,0},{24,8},{1,17},{9,25},{17,1},{25,9},{2,18},{10... | collective-permute-start | bytes 1376264 | tf_op jit(solution)/shard_map/ppermute | solution.py:259
  10.2 62.4 %collective-permute-start.9 = (f32[64,1792]{1,0:T(8,128)S(1)}, f32[64,1792]{1,0:T(8,128)S(1)}, u32[]{:S(2)}, u32[]{:S(2)}) collective-permute-start(f32[64,1792]{1,0:T(8,128)S(1)} %get-tuple-element.38), channel_id=1, source_target_pairs={{0,8},{8,0},{16,24},{24,16},{1,9},{9,1},{17,25},{25,17},{2,10},{10... | collective-permute-start | bytes 1376264 | tf_op jit(solution)/shard_map/ppermute | solution.py:259
  10.8 61.8 %collective-permute-start.8 = (f32[64,1792]{1,0:T(8,128)S(1)}, f32[64,1792]{1,0:T(8,128)S(1)}, u32[]{:S(2)}, u32[]{:S(2)}) collective-permute-start(f32[64,1792]{1,0:T(8,128)S(1)} %get-tuple-element.40), channel_id=1, source_target_pairs={{0,24},{8,16},{16,8},{24,0},{1,25},{9,17},{17,9},{25,1},{2,26},{10... | collective-permute-start | bytes 1376264 | tf_op jit(solution)/shard_map/ppermute | solution.py:259
  14.6 97.3 %collective-permute-start.7 = (f32[64,1792]{1,0:T(8,128)}, f32[64,1792]{1,0:T(8,128)}, u32[]{:S(2)}, u32[]{:S(2)}) collective-permute-start(f32[64,1792]{1,0:T(8,128)} %get-tuple-element.41), channel_id=1, source_target_pairs={{0,16},{8,24},{16,0},{24,8},{1,17},{9,25},{17,1},{25,9},{2,18},{10... | collective-permute-start | bytes 1376264 | tf_op jit(solution)/shard_map/ppermute | solution.py:259
  21.7 85.0 %copy-start.11 = (f32[64,1792]{1,0:T(8,128)}, f32[64,1792]{1,0:T(8,128)S(1)}, u32[]{:S(2)}) copy-start(f32[64,1792]{1,0:T(8,128)S(1)} %collective-permute-done.11.refs_3_) | copy-start | bytes 1376260
  21.7 93.0 %collective-permute-start.6 = (f32[64,1792]{1,0:T(8,128)}, f32[64,1792]{1,0:T(8,128)}, u32[]{:S(2)}, u32[]{:S(2)}) collective-permute-start(f32[64,1792]{1,0:T(8,128)} %get-tuple-element.42), channel_id=1, source_target_pairs={{0,8},{8,0},{16,24},{24,16},{1,9},{9,1},{17,25},{25,17},{2,10},{10... | collective-permute-start | bytes 1376264 | tf_op jit(solution)/shard_map/ppermute | solution.py:259
  70.0 36.7 %copy-start.13 = (f32[64,1792]{1,0:T(8,128)}, f32[64,1792]{1,0:T(8,128)S(1)}, u32[]{:S(2)}) copy-start(f32[64,1792]{1,0:T(8,128)S(1)} %collective-permute-done.10.refs_2_) | copy-start | bytes 1376260
  70.0 44.7 %collective-permute-start.5 = (f32[64,1792]{1,0:T(8,128)}, f32[64,1792]{1,0:T(8,128)}, u32[]{:S(2)}, u32[]{:S(2)}) collective-permute-start(f32[64,1792]{1,0:T(8,128)} %get-tuple-element.44), channel_id=1, source_target_pairs={{0,24},{8,16},{16,8},{24,0},{1,25},{9,17},{17,9},{25,1},{2,26},{10... | collective-permute-start | bytes 1376264 | tf_op jit(solution)/shard_map/ppermute | solution.py:259
  72.7 34.0 %copy-start.15 = (f32[64,1792]{1,0:T(8,128)}, f32[64,1792]{1,0:T(8,128)S(1)}, u32[]{:S(2)}) copy-start(f32[64,1792]{1,0:T(8,128)S(1)} %collective-permute-done.9.refs_1_) | copy-start | bytes 1376260
  72.7 64.9 %collective-permute-start.4 = (f32[64,1792]{1,0:T(8,128)}, f32[64,1792]{1,0:T(8,128)}, u32[]{:S(2)}, u32[]{:S(2)}) collective-permute-start(f32[64,1792]{1,0:T(8,128)} %get-tuple-element.45), channel_id=1, source_target_pairs={{0,16},{8,24},{16,0},{24,8},{1,17},{9,25},{17,1},{25,9},{2,18},{10... | collective-permute-start | bytes 1376264 | tf_op jit(solution)/shard_map/ppermute | solution.py:259
  72.7 39.2 %copy-start.9 = (f32[64,1792]{1,0:T(8,128)}, f32[64,1792]{1,0:T(8,128)S(1)}, u32[]{:S(2)}) copy-start(f32[64,1792]{1,0:T(8,128)S(1)} %collective-permute-done.8.refs_3_) | copy-start | bytes 1376260
  72.7 64.9 %collective-permute-start.3 = (f32[64,1792]{1,0:T(8,128)}, f32[64,1792]{1,0:T(8,128)}, u32[]{:S(2)}, u32[]{:S(2)}) collective-permute-start(f32[64,1792]{1,0:T(8,128)} %get-tuple-element.46), channel_id=1, source_target_pairs={{0,8},{8,0},{16,24},{24,16},{1,9},{9,1},{17,25},{25,17},{2,10},{10... | collective-permute-start | bytes 1376264 | tf_op jit(solution)/shard_map/ppermute | solution.py:259
  106.7 1.0 copy-start.12
  107.8 1.0 copy-start.14
  108.8 1.0 copy-start.16
  111.9 30.9 %collective-permute-start.2 = (f32[64,768]{1,0:T(8,128)S(1)}, f32[64,768]{1,0:T(8,128)S(1)}, u32[]{:S(2)}, u32[]{:S(2)}) collective-permute-start(f32[64,768]{1,0:T(8,128)S(1)} %get-tuple-element.48), channel_id=1, source_target_pairs={{0,24},{8,16},{16,8},{24,0},{1,25},{9,17},{17,9},{25,1},{2,26},{10... | collective-permute-start | bytes 589832 | tf_op jit(solution)/shard_map/ppermute | solution.py:259
  114.7 30.3 %collective-permute-start.1 = (f32[64,768]{1,0:T(8,128)S(1)}, f32[64,768]{1,0:T(8,128)S(1)}, u32[]{:S(2)}, u32[]{:S(2)}) collective-permute-start(f32[64,768]{1,0:T(8,128)S(1)} %get-tuple-element.49), channel_id=1, source_target_pairs={{0,16},{8,24},{16,0},{24,8},{1,17},{9,25},{17,1},{25,9},{2,18},{10... | collective-permute-start | bytes 589832 | tf_op jit(solution)/shard_map/ppermute | solution.py:259
  114.7 30.3 %collective-permute-start = (f32[64,768]{1,0:T(8,128)S(1)}, f32[64,768]{1,0:T(8,128)S(1)}, u32[]{:S(2)}, u32[]{:S(2)}) collective-permute-start(f32[64,768]{1,0:T(8,128)S(1)} %get-tuple-element.50), channel_id=1, source_target_pairs={{0,8},{8,0},{16,24},{24,16},{1,9},{9,1},{17,25},{25,17},{2,10},{10... | collective-permute-start | bytes 589832 | tf_op jit(solution)/shard_map/ppermute | solution.py:259
  128.3 1.0 copy-start.6
  129.3 1.0 copy-start.10
  133.6 0.9 copy-start.1
  141.0 0.9 copy-start.3
  141.9 0.9 copy-start.5
  146.0 0.7 copy-start.7
  174.8 1.2 copy-start.2
  176.0 1.2 copy-start.4
  177.1 1.0 copy-start.8

commit v3 on v2

v3 whole, which is shorter than its diff:
```python
import functools

import jax
import jax.numpy as jnp
from jax import lax
from jax.experimental import pallas as pl
from jax.experimental.pallas import tpu as pltpu
from jax.sharding import PartitionSpec as P

HIGHEST = lax.Precision.HIGHEST
LANES = 128
PANEL = 32
BASIS_TILE = 512
VMEM_LIMIT = 24 * 1024 * 1024


def iota(shape, dim):
    return lax.broadcasted_iota(jnp.int32, shape, dim)


def split(values):
    first = values.astype(jnp.bfloat16)
    second = (values - first.astype(jnp.float32)).astype(jnp.bfloat16)
    return first, second


def dot(left, right, dims=((1,), (0,)), precision=None):
    return lax.dot_general(
        left, right, (dims, ((), ())), precision=precision, preferred_element_type=jnp.float32
    )


def widen(pieces, cols_ref):
    width = pieces[0].shape[0]
    me = lax.axis_index("tm")
    for offset, piece in enumerate(pieces):
        start = pl.multiple_of(jnp.bitwise_xor(me, offset) * width, width)
        cols_ref[pl.ds(start, width), :] = piece[...]


def gram_of(cols_ref, high_ref, low_ref):
    depth = cols_ref.shape[1]
    total = None
    step = 2 * LANES if depth % (2 * LANES) == 0 else LANES
    for at in range(0, depth, step):
        cols = cols_ref[:, at : at + step]
        rows = cols.T
        high, low = split(rows)
        high_ref[at : at + step, :] = high
        low_ref[at : at + step, :] = low
        part = dot(cols, rows, precision=HIGHEST)
        total = part if total is None else total + part
    half = total.shape[0] // 2
    return total[:half, :half], total[:half, half:], total[half:, half:]


def first_kernel(*refs, peers):
    out_ref, high_ref, low_ref, cols_ref = refs[peers:]
    widen(refs[:peers], cols_ref)
    for index, block in enumerate(gram_of(cols_ref, high_ref, low_ref)):
        out_ref[index] = block


def middle_kernel(*refs, peers):
    sum_ref, out_ref, high_ref, low_ref, cols_ref = refs[peers:]
    widen(refs[:peers], cols_ref)
    for index, block in enumerate(gram_of(cols_ref, high_ref, low_ref)):
        out_ref[index] = sum_ref[index] + block


def last_kernel(*refs, peers):
    sum_ref, tail_ref, keep_ref, send_ref, high_ref, low_ref, cols_ref, pack_ref = refs[peers:]
    widen(refs[:peers], cols_ref)
    first, cross, second = (
        sum_ref[index] + block
        for index, block in enumerate(gram_of(cols_ref, high_ref, low_ref))
    )
    size = first.shape[0]
    row, col = iota(first.shape, 0), iota(first.shape, 1)
    pack_ref[:size, :] = jnp.where(col >= row, first, second)
    pack_ref[size : 2 * size, :] = cross
    pack_ref[2 * size :, :] = jnp.zeros((pack_ref.shape[0] - 2 * size, LANES), jnp.float32)
    pack_ref[2 * size : 2 * size + 1, :] = jnp.sum(
        jnp.where(col == row, second, 0.0), axis=0, keepdims=True
    )
    pack_ref[2 * size + 1 : 2 * size + 3, :] = tail_ref[...]
    rows = keep_ref.shape[0]
    core = jnp.bitwise_and(lax.axis_index("rows"), 1)
    keep_ref[...] = pack_ref[pl.ds(pl.multiple_of(core * rows, 8), rows), :]
    send_ref[...] = pack_ref[pl.ds(pl.multiple_of((1 - core) * rows, 8), rows), :]


def add_chunk(pieces, running, tail):
    peers = len(pieces)
    width, depth = pieces[0].shape
    count = width * peers
    half = count // 2
    vmem = pl.BlockSpec(memory_space=pltpu.VMEM)
    terms = (jax.ShapeDtypeStruct((depth, count), jnp.bfloat16),) * 2
    scratch = [pltpu.VMEM((count, depth), jnp.float32)]
    if tail is None:
        sums = (jax.ShapeDtypeStruct((3, half, half), jnp.float32),)
        args = (*pieces,) if running is None else (*pieces, running)
        body = first_kernel if running is None else middle_kernel
    else:
        rows = (2 * half + 3 + 15) // 16 * 8
        sums = (jax.ShapeDtypeStruct((rows, LANES), jnp.float32),) * 2
        args = (*pieces, running, tail)
        body = last_kernel
        scratch.append(pltpu.VMEM((2 * rows, LANES), jnp.float32))
    return pl.pallas_call(
        functools.partial(body, peers=peers),
        out_shape=sums + terms,
        in_specs=[vmem] * len(args),
        out_specs=(vmem,) * (len(sums) + 2),
        scratch_shapes=scratch,
        compiler_params=pltpu.CompilerParams(vmem_limit_bytes=VMEM_LIMIT),
        cost_estimate=pl.CostEstimate(
            flops=12 * count * count * depth,
            bytes_accessed=8 * count * depth,
            transcendentals=0,
        ),
        name="gram_chunk",
    )(*args)


def eliminate(rows, at):
    n, count = rows.shape
    sub = iota((n, LANES), 0)
    block = rows[:, at : at + n]
    columns = [jnp.broadcast_to(block[:, k : k + 1], (n, LANES)) for k in range(n)]
    lane, sub_all = iota((n, count), 1), iota((n, count), 0)
    own = (lane >= at) & (lane < at + n)
    rows = jnp.where(own, jnp.where(lane - at == sub_all, 1.0, 0.0), rows)
    halves = [rows[:, h : h + LANES] for h in range(0, count, LANES)]
    pivots = jnp.ones((n, LANES), jnp.float32)
    inverses = jnp.zeros((n, LANES), jnp.float32)
    for k in range(n):
        pivot = columns[k][k : k + 1, :]
        inverse = 1.0 / pivot
        pivots = jnp.where(sub == k, jnp.broadcast_to(pivot, (n, LANES)), pivots)
        inverses = jnp.where(sub == k, jnp.broadcast_to(inverse, (n, LANES)), inverses)
        factor = jnp.where(sub > k, columns[k] * inverse, 0.0)
        for j in range(k + 1, n):
            columns[j] = columns[j] - factor * columns[j][k : k + 1, :]
        halves = [half - factor * half[k : k + 1, :] for half in halves]
    upper = jnp.zeros((n, LANES), jnp.float32)
    lane_here = iota((n, LANES), 1) + at // LANES * LANES
    for k in range(n):
        upper = jnp.where(lane_here == at + k, columns[k], upper)
    return halves, upper, pivots, inverses


def factorize(work, factor_ref, inverse_ref):
    count = work.shape[0]
    n = PANEL
    lane, sub = iota((n, LANES), 1), iota((n, LANES), 0)
    for at in range(0, count, n):
        below = at + n
        halves, upper, pivots, inverses = eliminate(work[at:below, :], at)
        root = lax.rsqrt(pivots)
        root = root * (1.5 - 0.5 * pivots * root * root)
        scaled = []
        for h, half in enumerate(halves):
            column = lane + h * LANES
            mixed = jnp.where((column >= at) & (column < below), upper, half)
            cut = slice(h * LANES, (h + 1) * LANES)
            factor_ref[at:below, cut] = jnp.where(column >= sub + at, mixed * root, 0.0)
            inverse_ref[at:below, cut] = jnp.where(column <= sub + at, half * root, 0.0)
            scaled.append(jnp.where(column >= below, half * inverses, 0.0))
        if below == count:
            break
        skip = below // LANES
        multiplier = jnp.concatenate(scaled[skip:], axis=1)
        update = dot(
            multiplier, jnp.concatenate(halves, axis=1), dims=((0,), (0,)), precision=HIGHEST
        )
        wide = iota((count - below, count), 1)
        old = jnp.where((wide >= at) & (wide < below), 0.0, work[below:, :])
        work[below:, :] = old - update[below - skip * LANES :, :]


def finish_kernel(*refs, chunks, samples):
    own_ref, other_ref = refs[:2]
    highs, lows = refs[2 : 2 + chunks], refs[2 + chunks : 2 + 2 * chunks]
    basis_ref, factor_ref, projected_ref, operator_ref = refs[2 + 2 * chunks : 6 + 2 * chunks]
    pack_ref, work, inverse_ref, rows_ref, out_sem = refs[6 + 2 * chunks :]
    count = work.shape[0]
    half = count // 2

    scale = 1.0 / samples
    rows = own_ref.shape[0]
    core = jnp.bitwise_and(lax.axis_index("rows"), 1)
    pack_ref[pl.ds(pl.multiple_of(core * rows, 8), rows), :] = own_ref[...] * scale
    pack_ref[pl.ds(pl.multiple_of((1 - core) * rows, 8), rows), :] = other_ref[...] * scale
    mixed = pack_ref[:half, :]
    row, col = iota((half, half), 0), iota((half, half), 1)
    diagonal = pack_ref[2 * half : 2 * half + 1, :]
    turned = mixed.T
    work[:half, :half] = jnp.where(col >= row, mixed, turned)
    work[:half, half:] = pack_ref[half : 2 * half, :]
    work[half:, :half] = jnp.zeros((half, half), jnp.float32)
    work[half:, half:] = jnp.where(col > row, turned, jnp.where(col == row, diagonal, mixed))
    factorize(work, factor_ref, inverse_ref)

    inverse = inverse_ref[...]
    turned_high, turned_low = split(inverse.T)
    stores = []
    done = 0
    for high_ref, low_ref in zip(highs, lows):
        for at in range(0, high_ref.shape[0], BASIS_TILE):
            size = min(BASIS_TILE, high_ref.shape[0] - at)
            high, low = high_ref[at : at + size, :], low_ref[at : at + size, :]
            tile = pl.ds(done, size)
            rows_ref[tile, :] = (
                dot(high, turned_high) + (dot(high, turned_low) + dot(low, turned_high))
            )
            copy = pltpu.make_async_copy(
                rows_ref.at[tile], basis_ref.at[tile], out_sem.at[len(stores)]
            )
            copy.start()
            stores.append(copy)
            done += size

    tail = [pack_ref[2 * half + r : 2 * half + r + 1, :] for r in (1, 2)]
    column = jnp.sum(inverse * jnp.concatenate(tail, axis=1), axis=1, keepdims=True)
    shifted = pltpu.roll(factor_ref[...], count - 1, 1)
    projected = jnp.where(iota((count, count), 1) == count - 1, column, shifted)
    projected_ref[...] = projected
    operator_ref[...] = dot(projected, inverse, dims=((1,), (1,)), precision=HIGHEST)
    for copy in stores:
        copy.wait()


def finish(own, other, highs, lows, samples):
    chunks = len(highs)
    count = highs[0].shape[1]
    depth = sum(h.shape[0] for h in highs)
    tiles = sum(-(-h.shape[0] // BASIS_TILE) for h in highs)
    square = jax.ShapeDtypeStruct((count, count), jnp.float32)
    vmem = pl.BlockSpec(memory_space=pltpu.VMEM)
    far = pl.BlockSpec(memory_space=pl.ANY)
    return pl.pallas_call(
        functools.partial(finish_kernel, chunks=chunks, samples=samples),
        out_shape=(jax.ShapeDtypeStruct((depth, count), jnp.float32), square, square, square),
        in_specs=[vmem] * (2 + 2 * chunks),
        out_specs=(far, vmem, vmem, vmem),
        scratch_shapes=[
            pltpu.VMEM((2 * own.shape[0], LANES), jnp.float32),
            pltpu.VMEM((count, count), jnp.float32),
            pltpu.VMEM((count, count), jnp.float32),
            pltpu.VMEM((depth, count), jnp.float32),
            pltpu.SemaphoreType.DMA((tiles,)),
        ],
        compiler_params=pltpu.CompilerParams(vmem_limit_bytes=VMEM_LIMIT),
        name="factor_and_basis",
    )(own, other, *highs, *lows)


def swap(values, axis, step):
    size = lax.axis_size(axis)
    return lax.ppermute(values, axis, [(i, i ^ step) for i in range(size)])


def sum_halves(keep, send):
    keep = keep + swap(send, "rows", 1)
    for axis, step in (("rows", 2), ("tm", 1)):
        while step < lax.axis_size(axis):
            keep = keep + swap(keep, axis, step)
            step *= 2
    return keep, swap(keep, "rows", 1)


def shards(snapshots, last_snapshot):
    peers = lax.axis_size("tm")
    devices = peers * lax.axis_size("rows")
    me = lax.axis_index("tm")
    own_cols = snapshots.shape[1]
    count = own_cols * peers
    depth = snapshots.shape[0] // peers
    columns = snapshots.T

    small = depth // 8
    first = depth // 4
    large = (depth - small - first) // (4 * LANES) * (2 * LANES)
    sizes = [first, depth - small - first - large, large, small]

    chunks = []
    start = 0
    for size in sizes:
        pieces = []
        for offset in range(peers):
            target = jnp.bitwise_xor(me, offset)
            pieces.append(
                lax.dynamic_slice(columns, (0, target * depth + start), (own_cols, size))
            )
        if not chunks:
            columns, *pieces = lax.optimization_barrier((columns, *pieces))
            tail_own = jnp.dot(
                columns, last_snapshot, precision=HIGHEST, preferred_element_type=jnp.float32
            )
            columns, tail_own = lax.optimization_barrier((columns, tail_own))
        chunks.append(
            [swap(piece, "tm", offset) if offset else piece for offset, piece in enumerate(pieces)]
        )
        start += size

    tail = lax.dynamic_update_slice_in_dim(
        jnp.zeros((count,), jnp.float32), tail_own, me * own_cols, 0
    ).reshape(count // LANES, LANES)

    running = None
    highs, lows = [], []
    for index, pieces in enumerate(chunks):
        ending = index == len(chunks) - 1
        *running, high, low = add_chunk(pieces, running, tail if ending else None)
        running = running if ending else running[0]
        highs.append(high)
        lows.append(low)
    own, other = sum_halves(*running)
    basis, factor, projected, operator = finish(own, other, highs, lows, depth * devices)
    return (basis.reshape(1, 1, depth, count), factor, projected, operator)


def solution(mesh):
    in_specs = (P("rows", "tm"), P("rows"))
    out_specs = (P("rows", "tm", None, None), P(), P(), P())
    return jax.shard_map(shards, mesh=mesh, in_specs=in_specs, out_specs=out_specs, check_vma=False)
```

time: 195 us -> 183 us (0.938)
  waiting for transfers between devices: 40.4 us -> 86.6 us
  blocking collectives: 27.9 us -> 0 us
  starting transfers between devices: 76 us -> 50.1 us
  local copies, waits for them, and re-layouts: 18.1 us -> 12.8 us
  matrix products: 4.97 us -> 6.97 us
    ppermute x12 -> x18, waiting for transfers between devices: 40.4 us -> 86.6 us  [swap(): return lax.ppermute(values, axis, [(i, i ^ step) for i in range(size)])]
    all_to_all x2 -> x0, blocking collectives: 27.9 us -> none  [the longest x1 15.1 us: sum_all(): pieces = lax.all_to_all(packed.reshape(devices, each, LANES), AXES, 0, 0)]
    ppermute x12 -> x18, starting transfers between devices: 76 us -> 50.1 us  [swap(): return lax.ppermute(values, axis, [(i, i ^ step) for i in range(size)])]
    unnamed x36 -> x10, local copies, waits for them, and re-layouts: 12 us -> 3.5 us
    dynamic_slice x2 -> x4, local copies, waits for them, and re-layouts: 5.71 us -> 8.98 us  [shards(): lax.dynamic_slice(columns, (0, target * depth + start), (own_cols, size))]
    dot_general x1, matrix products: 4.97 us -> 6.97 us  [shards(): jnp.dot(columns, last_snapshot, precision=HIGHEST, preferred_element_type...]
  transfers between devices with their start and end apart: 12 -> 18, of which waited for: 4 -> 10; matrix products, arithmetic and copies ran while one was open for 3% -> 8% of each run, Pallas kernels for 4% -> 5%
where the time goes in v3:
time: 183 us; the launch traced here: 182 us
  waiting for transfers between devices  86.6 us (47%)
  starting transfers between devices  50.1 us (27%)
  Pallas kernels  24.7 us (13%)
  local copies, waits for them, and re-layouts  12.8 us (7%)
  matrix products  6.97 us (4%)
    ppermute x18, waiting for transfers between devices, swap(): return lax.ppermute(values, axis, [(i, i ^ step) for i in range(size)])  86.6 us
    ppermute x18, starting transfers between devices, swap(): return lax.ppermute(values, axis, [(i, i ^ step) for i in range(size)])  50.1 us
    pallas_call x1, Pallas kernels, finish(): pl.pallas_call(functools.partial(finish_kernel, chunks=chunks, samples=sa...  15.1 us
    pallas_call x4, Pallas kernels, add_chunk(): pl.pallas_call(functools.partial(body, peers=peers), out_shape=sums + ter...  9.59 us
    dynamic_slice x4, local copies, waits for them, and re-layouts, shards(): lax.dynamic_slice(columns, (0, target * depth + start), (own_cols, size))  8.98 us
    dot_general x1, matrix products, shards(): jnp.dot(columns, last_snapshot, precision=HIGHEST, preferred_element_type...  6.97 us
  transfers between devices with their start and end apart: 18, of which 10 were waited for; matrix products, arithmetic and copies ran while one was open for 8% of the time, Pallas kernels for 5%

profile of v3, /device:TPU:0, one launch (start us, length us, event | category | flops | bytes accessed | tf_op | source)
XLA Modules:
  0.0 182.2 jit_solution(6125268044349450091)
XLA Ops:
  0.6 0.0 copy-start
  0.7 2.4 %dynamic-slice_bitcast_fusion = (f32[64,1536]{1,0:T(8,128)}, f32[64,1536]{1,0:T(8,128)}, f32[64,1536]{1,0:T(8,128)S(1)}, f32[64,1536]{1,0:T(8,128)}) fusion(f32[24576,64]{0,1:T(8,128)} %param.2, s32[]{:T(128)S(6)} %select_n.54, s32[]{:T(128)S(6)} %select_n.52, s32[]{:T(128)S(6)} %select_n.51, s32[]{:T(128)S(6)} %select_n.53), kind=kLoop, calls=%fused_computation.1 | loop fusion | bytes 3145744 | tf_op jit(solution)/shard_map/dynamic_slice | solution.py:295
  3.1 3.0 %collective-permute-start.9 = (f32[64,1536]{1,0:T(8,128)}, f32[64,1536]{1,0:T(8,128)S(1)}, u32[]{:S(2)}, u32[]{:S(2)}) collective-permute-start(f32[64,1536]{1,0:T(8,128)} %get-tuple-element.31), channel_id=1, source_target_pairs={{0,8},{8,0},{16,24},{24,16},{1,9},{9,1},{17,25},{25,17},{2,10},{10... | collective-permute-start | bytes 1179656 | tf_op jit(solution)/shard_map/ppermute | solution.py:262
  6.1 2.6 %collective-permute-start.10 = (f32[64,1536]{1,0:T(8,128)}, f32[64,1536]{1,0:T(8,128)S(1)}, u32[]{:S(2)}, u32[]{:S(2)}) collective-permute-start(f32[64,1536]{1,0:T(8,128)} %get-tuple-element.32), channel_id=1, source_target_pairs={{0,16},{8,24},{16,0},{24,8},{1,17},{9,25},{17,1},{25,9},{2,18},{10... | collective-permute-start | bytes 1179656 | tf_op jit(solution)/shard_map/ppermute | solution.py:262
  8.7 0.0 collective-permute-start.11
  8.7 0.0 copy-done
  8.7 7.0 %convolution_bitcast_fusion = f32[64]{0:T(128)S(1)} fusion(f32[64,24576]{1,0:T(8,128)} %bitcast.18, f32[24576,1]{0,1:T(1,128)S(1)} %bitcast.16), kind=kOutput, calls=%fused_computation | convolution fusion | flops 18874368 | bytes 6390016 | tf_op jit(solution)/shard_map/dot_general | solution.py:299
  15.7 2.6 %constant_dynamic-slice_fusion.4 = (f32[64,1792]{1,0:T(8,128)}, f32[64,1792]{1,0:T(8,128)}, f32[64,1792]{1,0:T(8,128)}, f32[64,1792]{1,0:T(8,128)S(1)}) fusion(f32[64,24576]{1,0:T(8,128)} %bitcast.19, s32[]{:T(128)S(6)} %select_n.62, s32[]{:T(128)S(6)} %select_n.61, s32[]{:T(128)S(6)} %select_n.60, s32[]{:T(128)S(6)} %select_n.59), kind=kLoop, calls=%fused_computation.9 | loop fusion | bytes 3670032 | tf_op jit(solution)/shard_map/dynamic_slice | solution.py:295
  18.2 3.8 %collective-permute-start.5 = (f32[64,1792]{1,0:T(8,128)}, f32[64,1792]{1,0:T(8,128)S(1)}, u32[]{:S(2)}, u32[]{:S(2)}) collective-permute-start(f32[64,1792]{1,0:T(8,128)} %get-tuple-element.56), channel_id=1, source_target_pairs={{0,24},{8,16},{16,8},{24,0},{1,25},{9,17},{17,9},{25,1},{2,26},{10... | collective-permute-start | bytes 1376264 | tf_op jit(solution)/shard_map/ppermute | solution.py:262
  22.1 2.7 %constant_dynamic-slice_fusion = (f32[64,2048]{1,0:T(8,128)}, f32[64,2048]{1,0:T(8,128)}, f32[64,2048]{1,0:T(8,128)}, f32[64,2048]{1,0:T(8,128)S(1)}) fusion(f32[64,24576]{1,0:T(8,128)} %bitcast.20, s32[]{:T(128)S(6)} %select_n.66, s32[]{:T(128)S(6)} %select_n.65, s32[]{:T(128)S(6)} %select_n.64, s32[]{:T(128)S(6)} %select_n.63), kind=kLoop, calls=%fused_computation.5 | loop fusion | bytes 4194320 | tf_op jit(solution)/shard_map/dynamic_slice | solution.py:295
  24.8 0.0 collective-permute-start.8
  24.8 0.0 collective-permute-done.9.refs_1_
  24.8 0.0 copy-start.1
  24.8 0.7 copy-done.1
  25.5 0.1 collective-permute-start.7
  25.6 42.8 %collective-permute-done.10.refs_2_ = f32[64,1536]{1,0:T(8,128)S(1)} collective-permute-done((f32[64,1536]{1,0:T(8,128)}, f32[64,1536]{1,0:T(8,128)S(1)}, u32[]{:S(2)}, u32[]{:S(2)}) %collective-permute-start.10) | collective-permute-done | bytes 393248 | tf_op jit(solution)/shard_map/ppermute | solution.py:262
  68.4 0.0 copy-start.3
  68.4 0.8 copy-done.3
  69.2 0.0 collective-permute-start.6
  69.2 0.0 collective-permute-done.11.refs_3_
  69.2 9.3 %collective-permute-start.4 = (f32[64,1792]{1,0:T(8,128)}, f32[64,1792]{1,0:T(8,128)}, u32[]{:S(2)}, u32[]{:S(2)}) collective-permute-start(f32[64,1792]{1,0:T(8,128)} %get-tuple-element.57), channel_id=1, source_target_pairs={{0,16},{8,24},{16,0},{24,8},{1,17},{9,25},{17,1},{25,9},{2,18},{10... | collective-permute-start | bytes 1376264 | tf_op jit(solution)/shard_map/ppermute | solution.py:262
  78.6 0.0 collective-permute-done.5.refs_3_
  78.6 18.5 %collective-permute-start.3 = (f32[64,1792]{1,0:T(8,128)}, f32[64,1792]{1,0:T(8,128)}, u32[]{:S(2)}, u32[]{:S(2)}) collective-permute-start(f32[64,1792]{1,0:T(8,128)} %get-tuple-element.58), channel_id=1, source_target_pairs={{0,8},{8,0},{16,24},{24,16},{1,9},{9,1},{17,25},{25,17},{2,10},{10... | collective-permute-start | bytes 1376264 | tf_op jit(solution)/shard_map/ppermute | solution.py:262
  97.1 0.3 dynamic_update_slice.3
  97.4 1.3 constant_dynamic-slice_fusion.8
  98.7 0.0 copy-start.2
  98.7 1.0 copy-done.2
  99.7 0.0 copy-start.4
  99.7 1.0 copy-done.4
  100.7 2.9 %gram_chunk.4 = (f32[3,128,128]{2,1,0:T(8,128)S(1)}, bf16[1536,256]{1,0:T(8,128)(2,1)S(1)}, bf16[1536,256]{1,0:T(8,128)(2,1)S(1)}) custom-call(f32[64,1536]{1,0:T(8,128)S(1)} %get-tuple-element.30.refs_0_, f32[64,1536]{1,0:T(8,128)S(1)} %copy-done.2, f32[64,1536]{1,0:T(8,128)S(1)} %copy-done.4, f32[64,1536]{1,0:T(8,128)} %collective-permute-done.11.refs_3_), custom_call_target="tpu_custom_call" | custom-call | flops 1207959552 | bytes 3145728 | tf_op jit(solution)/shard_map/gram_chunk/pallas_call | solution.py:111
  103.6 0.0 collective-permute-done.8.refs_3_
  103.6 2.5 %collective-permute-start.2 = (f32[64,768]{1,0:T(8,128)S(1)}, f32[64,768]{1,0:T(8,128)S(1)}, u32[]{:S(2)}, u32[]{:S(2)}) collective-permute-start(f32[64,768]{1,0:T(8,128)S(1)} %get-tuple-element.60), channel_id=1, source_target_pairs={{0,24},{8,16},{16,8},{24,0},{1,25},{9,17},{17,9},{25,1},{2,26},{10... | collective-permute-start | bytes 589832 | tf_op jit(solution)/shard_map/ppermute | solution.py:262
  106.2 17.1 %collective-permute-done.7.refs_2_ = f32[64,2048]{1,0:T(8,128)S(1)} collective-permute-done((f32[64,2048]{1,0:T(8,128)}, f32[64,2048]{1,0:T(8,128)S(1)}, u32[]{:S(2)}, u32[]{:S(2)}) %collective-permute-start.7) | collective-permute-done | bytes 524320 | tf_op jit(solution)/shard_map/ppermute | solution.py:262
  123.2 0.0 collective-permute-start.1
  123.2 0.0 collective-permute-done.6.refs_1_
  123.2 5.2 %collective-permute-start = (f32[64,768]{1,0:T(8,128)S(1)}, f32[64,768]{1,0:T(8,128)S(1)}, u32[]{:S(2)}, u32[]{:S(2)}) collective-permute-start(f32[64,768]{1,0:T(8,128)S(1)} %get-tuple-element.62), channel_id=1, source_target_pairs={{0,8},{8,0},{16,24},{24,16},{1,9},{9,1},{17,25},{25,17},{2,10},{10... | collective-permute-start | bytes 589832 | tf_op jit(solution)/shard_map/ppermute | solution.py:262
  128.5 2.4 %gram_chunk.5 = (f32[3,128,128]{2,1,0:T(8,128)S(1)}, bf16[2048,256]{1,0:T(8,128)(2,1)S(1)}, bf16[2048,256]{1,0:T(8,128)(2,1)S(1)}) custom-call(f32[64,2048]{1,0:T(8,128)S(1)} %get-tuple-element.55.refs_0_, f32[64,2048]{1,0:T(8,128)S(1)} %collective-permute-done.6.refs_1_, f32[64,2048]{1,0:T(8,128)S(1)} %collective-permute-done.7.refs_2_, ...), custom_call_target="tpu_custom_call" | custom-call | flops 1610612736 | bytes 4194304 | tf_op jit(solution)/shard_map/gram_chunk/pallas_call | solution.py:111
  130.8 6.6 %collective-permute-done.4.refs_2_ = f32[64,1792]{1,0:T(8,128)} collective-permute-done((f32[64,1792]{1,0:T(8,128)}, f32[64,1792]{1,0:T(8,128)}, u32[]{:S(2)}, u32[]{:S(2)}) %collective-permute-start.4) | collective-permute-done | bytes 458784 | tf_op jit(solution)/shard_map/ppermute | solution.py:262
  137.5 0.0 collective-permute-done.3.refs_1_
  137.5 3.3 %gram_chunk.6 = (f32[3,128,128]{2,1,0:T(8,128)S(1)}, bf16[1792,256]{1,0:T(8,128)(2,1)S(1)}, bf16[1792,256]{1,0:T(8,128)(2,1)S(1)}) custom-call(f32[64,1792]{1,0:T(8,128)S(1)} %get-tuple-element.59.refs_0_, f32[64,1792]{1,0:T(8,128)} %collective-permute-done.3.refs_1_, f32[64,1792]{1,0:T(8,128)} %collective-permute-done.4.refs_2_, ...), custom_call_target="tpu_custom_call" | custom-call | flops 1409286144 | bytes 3670016 | tf_op jit(solution)/shard_map/gram_chunk/pallas_call | solution.py:111
  140.7 0.0 collective-permute-done.2.refs_3_
  140.7 3.6 %collective-permute-done.1.refs_2_ = f32[64,768]{1,0:T(8,128)S(1)} collective-permute-done((f32[64,768]{1,0:T(8,128)S(1)}, f32[64,768]{1,0:T(8,128)S(1)}, u32[]{:S(2)}, u32[]{:S(2)}) %collective-permute-start.1) | collective-permute-done | bytes 196640 | tf_op jit(solution)/shard_map/ppermute | solution.py:262
  144.4 0.0 collective-permute-done.refs_1_
  144.4 1.1 gram_chunk.7
  145.5 0.1 collective-permute-start.12
  145.5 1.2 collective-permute-done.12
  146.8 1.6 collective-permute-start.13
  148.4 2.8 %collective-permute-done.13 = f32[136,128]{1,0:T(8,128)S(1)} collective-permute-done((f32[136,128]{1,0:T(8,128)S(1)}, f32[136,128]{1,0:T(8,128)S(1)}, u32[]{:S(2)}, u32[]{:S(2)}) %collective-permute-start.13) | collective-permute-done | bytes 69664 | tf_op jit(solution)/shard_map/ppermute | solution.py:262
  151.2 1.6 collective-permute-start.14
  152.8 2.8 %collective-permute-done.14 = f32[136,128]{1,0:T(8,128)S(1)} collective-permute-done((f32[136,128]{1,0:T(8,128)S(1)}, f32[136,128]{1,0:T(8,128)S(1)}, u32[]{:S(2)}, u32[]{:S(2)}) %collective-permute-start.14) | collective-permute-done | bytes 69664 | tf_op jit(solution)/shard_map/ppermute | solution.py:262
  155.6 0.1 collective-permute-start.15
  155.7 4.3 %collective-permute-done.15 = f32[136,128]{1,0:T(8,128)S(1)} collective-permute-done((f32[136,128]{1,0:T(8,128)S(1)}, f32[136,128]{1,0:T(8,128)S(1)}, u32[]{:S(2)}, u32[]{:S(2)}) %collective-permute-start.15) | collective-permute-done | bytes 69664 | tf_op jit(solution)/shard_map/ppermute | solution.py:262
  160.0 1.5 collective-permute-start.16
  161.5 4.1 %collective-permute-done.16 = f32[136,128]{1,0:T(8,128)S(1)} collective-permute-done((f32[136,128]{1,0:T(8,128)S(1)}, f32[136,128]{1,0:T(8,128)S(1)}, u32[]{:S(2)}, u32[]{:S(2)}) %collective-permute-start.16) | collective-permute-done | bytes 69664 | tf_op jit(solution)/shard_map/ppermute | solution.py:262
  165.6 0.1 collective-permute-start.17
  165.6 1.2 collective-permute-done.17.refs_1_
  166.9 15.1 %factor_and_basis.1 = (f32[6144,256]{1,0:T(8,128)}, f32[256,256]{1,0:T(8,128)}, f32[256,256]{1,0:T(8,128)}, f32[256,256]{1,0:T(8,128)}) custom-call(f32[136,128]{1,0:T(8,128)S(1)} %add.159.refs_0_, f32[136,128]{1,0:T(8,128)S(1)} %collective-permute-done.17.refs_1_, bf16[1536,256]{1,0:T(8,128)(2,1)S(1)} %get-tuple-element.40.refs_2_, ...), custom_call_target="tpu_custom_call" | custom-call | tf_op jit(solution)/shard_map/factor_and_basis/pallas_call | solution.py:243
  (6 shorter events, 0.1 us)
Async XLA Ops:
  0.6 8.1 %copy-start = (f32[24576]{0:T(1024)S(1)}, f32[24576]{0:T(1024)}, u32[]{:S(2)}) copy-start(f32[24576]{0:T(1024)} %param.3) | copy-start | bytes 294916
  3.1 21.7 %collective-permute-start.9 = (f32[64,1536]{1,0:T(8,128)}, f32[64,1536]{1,0:T(8,128)S(1)}, u32[]{:S(2)}, u32[]{:S(2)}) collective-permute-start(f32[64,1536]{1,0:T(8,128)} %get-tuple-element.31), channel_id=1, source_target_pairs={{0,8},{8,0},{16,24},{24,16},{1,9},{9,1},{17,25},{25,17},{2,10},{10... | collective-permute-start | bytes 1179656 | tf_op jit(solution)/shard_map/ppermute | solution.py:262
  6.1 62.3 %collective-permute-start.10 = (f32[64,1536]{1,0:T(8,128)}, f32[64,1536]{1,0:T(8,128)S(1)}, u32[]{:S(2)}, u32[]{:S(2)}) collective-permute-start(f32[64,1536]{1,0:T(8,128)} %get-tuple-element.32), channel_id=1, source_target_pairs={{0,16},{8,24},{16,0},{24,8},{1,17},{9,25},{17,1},{25,9},{2,18},{10... | collective-permute-start | bytes 1179656 | tf_op jit(solution)/shard_map/ppermute | solution.py:262
  8.7 60.5 %collective-permute-start.11 = (f32[64,1536]{1,0:T(8,128)}, f32[64,1536]{1,0:T(8,128)}, u32[]{:S(2)}, u32[]{:S(2)}) collective-permute-start(f32[64,1536]{1,0:T(8,128)} %get-tuple-element.33), channel_id=1, source_target_pairs={{0,24},{8,16},{16,8},{24,0},{1,25},{9,17},{17,9},{25,1},{2,26},{10... | collective-permute-start | bytes 1179656 | tf_op jit(solution)/shard_map/ppermute | solution.py:262
  18.2 60.3 %collective-permute-start.5 = (f32[64,1792]{1,0:T(8,128)}, f32[64,1792]{1,0:T(8,128)S(1)}, u32[]{:S(2)}, u32[]{:S(2)}) collective-permute-start(f32[64,1792]{1,0:T(8,128)} %get-tuple-element.56), channel_id=1, source_target_pairs={{0,24},{8,16},{16,8},{24,0},{1,25},{9,17},{17,9},{25,1},{2,26},{10... | collective-permute-start | bytes 1376264 | tf_op jit(solution)/shard_map/ppermute | solution.py:262
  24.8 78.8 %collective-permute-start.8 = (f32[64,2048]{1,0:T(8,128)}, f32[64,2048]{1,0:T(8,128)S(1)}, u32[]{:S(2)}, u32[]{:S(2)}) collective-permute-start(f32[64,2048]{1,0:T(8,128)} %get-tuple-element.52), channel_id=1, source_target_pairs={{0,24},{8,16},{16,8},{24,0},{1,25},{9,17},{17,9},{25,1},{2,26},{10... | collective-permute-start | bytes 1572872 | tf_op jit(solution)/shard_map/ppermute | solution.py:262
  24.8 0.8 copy-start.1
  25.5 97.7 %collective-permute-start.7 = (f32[64,2048]{1,0:T(8,128)}, f32[64,2048]{1,0:T(8,128)S(1)}, u32[]{:S(2)}, u32[]{:S(2)}) collective-permute-start(f32[64,2048]{1,0:T(8,128)} %get-tuple-element.53), channel_id=1, source_target_pairs={{0,16},{8,24},{16,0},{24,8},{1,17},{9,25},{17,1},{25,9},{2,18},{10... | collective-permute-start | bytes 1572872 | tf_op jit(solution)/shard_map/ppermute | solution.py:262
  68.4 0.8 copy-start.3
  69.2 54.0 %collective-permute-start.6 = (f32[64,2048]{1,0:T(8,128)}, f32[64,2048]{1,0:T(8,128)S(1)}, u32[]{:S(2)}, u32[]{:S(2)}) collective-permute-start(f32[64,2048]{1,0:T(8,128)} %get-tuple-element.54), channel_id=1, source_target_pairs={{0,8},{8,0},{16,24},{24,16},{1,9},{9,1},{17,25},{25,17},{2,10},{10... | collective-permute-start | bytes 1572872 | tf_op jit(solution)/shard_map/ppermute | solution.py:262
  69.2 68.2 %collective-permute-start.4 = (f32[64,1792]{1,0:T(8,128)}, f32[64,1792]{1,0:T(8,128)}, u32[]{:S(2)}, u32[]{:S(2)}) collective-permute-start(f32[64,1792]{1,0:T(8,128)} %get-tuple-element.57), channel_id=1, source_target_pairs={{0,16},{8,24},{16,0},{24,8},{1,17},{9,25},{17,1},{25,9},{2,18},{10... | collective-permute-start | bytes 1376264 | tf_op jit(solution)/shard_map/ppermute | solution.py:262
  78.6 58.9 %collective-permute-start.3 = (f32[64,1792]{1,0:T(8,128)}, f32[64,1792]{1,0:T(8,128)}, u32[]{:S(2)}, u32[]{:S(2)}) collective-permute-start(f32[64,1792]{1,0:T(8,128)} %get-tuple-element.58), channel_id=1, source_target_pairs={{0,8},{8,0},{16,24},{24,16},{1,9},{9,1},{17,25},{25,17},{2,10},{10... | collective-permute-start | bytes 1376264 | tf_op jit(solution)/shard_map/ppermute | solution.py:262
  98.7 1.0 copy-start.2
  99.7 1.0 copy-start.4
  103.6 37.1 %collective-permute-start.2 = (f32[64,768]{1,0:T(8,128)S(1)}, f32[64,768]{1,0:T(8,128)S(1)}, u32[]{:S(2)}, u32[]{:S(2)}) collective-permute-start(f32[64,768]{1,0:T(8,128)S(1)} %get-tuple-element.60), channel_id=1, source_target_pairs={{0,24},{8,16},{16,8},{24,0},{1,25},{9,17},{17,9},{25,1},{2,26},{10... | collective-permute-start | bytes 589832 | tf_op jit(solution)/shard_map/ppermute | solution.py:262
  123.2 21.1 %collective-permute-start.1 = (f32[64,768]{1,0:T(8,128)S(1)}, f32[64,768]{1,0:T(8,128)S(1)}, u32[]{:S(2)}, u32[]{:S(2)}) collective-permute-start(f32[64,768]{1,0:T(8,128)S(1)} %get-tuple-element.61), channel_id=1, source_target_pairs={{0,16},{8,24},{16,0},{24,8},{1,17},{9,25},{17,1},{25,9},{2,18},{10... | collective-permute-start | bytes 589832 | tf_op jit(solution)/shard_map/ppermute | solution.py:262
  123.2 21.1 %collective-permute-start = (f32[64,768]{1,0:T(8,128)S(1)}, f32[64,768]{1,0:T(8,128)S(1)}, u32[]{:S(2)}, u32[]{:S(2)}) collective-permute-start(f32[64,768]{1,0:T(8,128)S(1)} %get-tuple-element.62), channel_id=1, source_target_pairs={{0,8},{8,0},{16,24},{24,16},{1,9},{9,1},{17,25},{25,17},{2,10},{10... | collective-permute-start | bytes 589832 | tf_op jit(solution)/shard_map/ppermute | solution.py:262
  145.5 1.3 collective-permute-start.12
  146.8 4.4 %collective-permute-start.13 = (f32[136,128]{1,0:T(8,128)S(1)}, f32[136,128]{1,0:T(8,128)S(1)}, u32[]{:S(2)}, u32[]{:S(2)}) collective-permute-start(f32[136,128]{1,0:T(8,128)S(1)} %add.155), channel_id=1, source_target_pairs={{0,2},{1,3},{2,0},{3,1},{4,6},{5,7},{6,4},{7,5},{8,10},{9,11},{10,... | collective-permute-start | bytes 208904 | tf_op jit(solution)/shard_map/ppermute | solution.py:262
  151.2 4.4 %collective-permute-start.14 = (f32[136,128]{1,0:T(8,128)S(1)}, f32[136,128]{1,0:T(8,128)S(1)}, u32[]{:S(2)}, u32[]{:S(2)}) collective-permute-start(f32[136,128]{1,0:T(8,128)S(1)} %add.156), channel_id=1, source_target_pairs={{0,4},{1,5},{2,6},{3,7},{4,0},{5,1},{6,2},{7,3},{8,12},{9,13},{10,... | collective-permute-start | bytes 208904 | tf_op jit(solution)/shard_map/ppermute | solution.py:262
  155.6 4.4 %collective-permute-start.15 = (f32[136,128]{1,0:T(8,128)S(1)}, f32[136,128]{1,0:T(8,128)S(1)}, u32[]{:S(2)}, u32[]{:S(2)}) collective-permute-start(f32[136,128]{1,0:T(8,128)S(1)} %add.157), channel_id=1, source_target_pairs={{0,8},{8,0},{16,24},{24,16},{1,9},{9,1},{17,25},{25,17},{2,10},{10... | collective-permute-start | bytes 208904 | tf_op jit(solution)/shard_map/ppermute | solution.py:262
  160.0 5.6 %collective-permute-start.16 = (f32[136,128]{1,0:T(8,128)S(1)}, f32[136,128]{1,0:T(8,128)S(1)}, u32[]{:S(2)}, u32[]{:S(2)}) collective-permute-start(f32[136,128]{1,0:T(8,128)S(1)} %add.158), channel_id=1, source_target_pairs={{0,16},{8,24},{16,0},{24,8},{1,17},{9,25},{17,1},{25,9},{2,18},{10... | collective-permute-start | bytes 208904 | tf_op jit(solution)/shard_map/ppermute | solution.py:262
  165.6 1.3 collective-permute-start.17

commit v4 on v3

--- a/solution.py
+++ b/solution.py
@@ -9,7 +9,7 @@
 
 HIGHEST = lax.Precision.HIGHEST
 LANES = 128
-PANEL = 32
+PANEL = 16
 BASIS_TILE = 512
 VMEM_LIMIT = 24 * 1024 * 1024
 
@@ -124,15 +124,23 @@
     )(*args)
 
 
-def eliminate(rows, at):
+def eliminate(rows, following, at):
     n, count = rows.shape
     sub = iota((n, LANES), 0)
-    block = rows[:, at : at + n]
-    columns = [jnp.broadcast_to(block[:, k : k + 1], (n, LANES)) for k in range(n)]
     lane, sub_all = iota((n, count), 1), iota((n, count), 0)
     own = (lane >= at) & (lane < at + n)
-    rows = jnp.where(own, jnp.where(lane - at == sub_all, 1.0, 0.0), rows)
-    halves = [rows[:, h : h + LANES] for h in range(0, count, LANES)]
+
+    def spread(values):
+        return [jnp.broadcast_to(values[:, at + k : at + k + 1], (n, LANES)) for k in range(n)]
+
+    def cut(values):
+        return [values[:, h : h + LANES] for h in range(0, count, LANES)]
+
+    columns = spread(rows)
+    halves = cut(jnp.where(own, jnp.where(lane - at == sub_all, 1.0, 0.0), rows))
+    if following is not None:
+        next_columns = spread(following)
+        next_halves = cut(jnp.where(own, 0.0, following))
     pivots = jnp.ones((n, LANES), jnp.float32)
     inverses = jnp.zeros((n, LANES), jnp.float32)
     for k in range(n):
@@ -141,23 +149,35 @@
         pivots = jnp.where(sub == k, jnp.broadcast_to(pivot, (n, LANES)), pivots)
         inverses = jnp.where(sub == k, jnp.broadcast_to(inverse, (n, LANES)), inverses)
         factor = jnp.where(sub > k, columns[k] * inverse, 0.0)
+        if following is not None:
+            next_factor = next_columns[k] * inverse
         for j in range(k + 1, n):
-            columns[j] = columns[j] - factor * columns[j][k : k + 1, :]
-        halves = [half - factor * half[k : k + 1, :] for half in halves]
+            row = columns[j][k : k + 1, :]
+            columns[j] = columns[j] - factor * row
+            if following is not None:
+                next_columns[j] = next_columns[j] - next_factor * row
+        for h, half in enumerate(halves):
+            row = half[k : k + 1, :]
+            halves[h] = half - factor * row
+            if following is not None:
+                next_halves[h] = next_halves[h] - next_factor * row
     upper = jnp.zeros((n, LANES), jnp.float32)
     lane_here = iota((n, LANES), 1) + at // LANES * LANES
     for k in range(n):
         upper = jnp.where(lane_here == at + k, columns[k], upper)
-    return halves, upper, pivots, inverses
+    carried = None if following is None else jnp.concatenate(next_halves, axis=1)
+    return halves, upper, pivots, inverses, carried
 
 
 def factorize(work, factor_ref, inverse_ref):
     count = work.shape[0]
     n = PANEL
     lane, sub = iota((n, LANES), 1), iota((n, LANES), 0)
+    rows = work[:n, :]
     for at in range(0, count, n):
-        below = at + n
-        halves, upper, pivots, inverses = eliminate(work[at:below, :], at)
+        below, later = at + n, at + 2 * n
+        following = work[below:later, :] if below < count else None
+        halves, upper, pivots, inverses, rows = eliminate(rows, following, at)
         root = lax.rsqrt(pivots)
         root = root * (1.5 - 0.5 * pivots * root * root)
         scaled = []
@@ -167,17 +187,17 @@
             cut = slice(h * LANES, (h + 1) * LANES)
             factor_ref[at:below, cut] = jnp.where(column >= sub + at, mixed * root, 0.0)
             inverse_ref[at:below, cut] = jnp.where(column <= sub + at, half * root, 0.0)
-            scaled.append(jnp.where(column >= below, half * inverses, 0.0))
-        if below == count:
-            break
-        skip = below // LANES
+            scaled.append(jnp.where(column >= later, half * inverses, 0.0))
+        if later >= count:
+            continue
+        skip = later // LANES
         multiplier = jnp.concatenate(scaled[skip:], axis=1)
         update = dot(
             multiplier, jnp.concatenate(halves, axis=1), dims=((0,), (0,)), precision=HIGHEST
         )
-        wide = iota((count - below, count), 1)
-        old = jnp.where((wide >= at) & (wide < below), 0.0, work[below:, :])
-        work[below:, :] = old - update[below - skip * LANES :, :]
+        wide = iota((count - later, count), 1)
+        old = jnp.where((wide >= at) & (wide < below), 0.0, work[later:, :])
+        work[later:, :] = old - update[later - skip * LANES :, :]
 
 
 def finish_kernel(*refs, chunks, samples):
@@ -198,8 +218,9 @@
     diagonal = pack_ref[2 * half : 2 * half + 1, :]
     turned = mixed.T
     work[:half, :half] = jnp.where(col >= row, mixed, turned)
-    work[:half, half:] = pack_ref[half : 2 * half, :]
-    work[half:, :half] = jnp.zeros((half, half), jnp.float32)
+    cross = pack_ref[half : 2 * half, :]
+    work[:half, half:] = cross
+    work[half:, :half] = cross.T
     work[half:, half:] = jnp.where(col > row, turned, jnp.where(col == row, diagonal, mixed))
     factorize(work, factor_ref, inverse_ref)
 
@@ -281,28 +302,34 @@
     columns = snapshots.T
 
     small = depth // 8
-    first = depth // 4
+    first = depth // 6 // LANES * LANES
     large = (depth - small - first) // (4 * LANES) * (2 * LANES)
     sizes = [first, depth - small - first - large, large, small]
 
+    def cut(values, offset, start, size):
+        target = jnp.bitwise_xor(me, offset)
+        return lax.dynamic_slice(values, (0, target * depth + start), (own_cols, size))
+
+    far = range(2, peers)
+    columns, *early = lax.optimization_barrier(
+        (columns, *[cut(columns, offset, 0, first) for offset in far])
+    )
+    early = {offset: swap(piece, "tm", offset) for offset, piece in zip(far, early)}
+    tail_own = jnp.dot(
+        columns, last_snapshot, precision=HIGHEST, preferred_element_type=jnp.float32
+    )
+    columns, tail_own = lax.optimization_barrier((columns, tail_own))
     chunks = []
     start = 0
     for size in sizes:
         pieces = []
         for offset in range(peers):
-            target = jnp.bitwise_xor(me, offset)
-            pieces.append(
-                lax.dynamic_slice(columns, (0, target * depth + start), (own_cols, size))
-            )
-        if not chunks:
-            columns, *pieces = lax.optimization_barrier((columns, *pieces))
-            tail_own = jnp.dot(
-                columns, last_snapshot, precision=HIGHEST, preferred_element_type=jnp.float32
-            )
-            columns, tail_own = lax.optimization_barrier((columns, tail_own))
-        chunks.append(
-            [swap(piece, "tm", offset) if offset else piece for offset, piece in enumerate(pieces)]
-        )
+            if start == 0 and offset in early:
+                pieces.append(early[offset])
+                continue
+            piece = cut(columns, offset, start, size)
+            pieces.append(swap(piece, "tm", offset) if offset else piece)
+        chunks.append(pieces)
         start += size
 
     tail = lax.dynamic_update_slice_in_dim(

time: 183 us -> 178 us (0.973)
  waiting for transfers between devices: 86.6 us -> 60.7 us
  starting transfers between devices: 50.1 us -> 74.5 us
  Pallas kernels: 24.7 us -> 22.8 us
    ppermute x18, waiting for transfers between devices: 86.6 us -> 60.7 us  [swap(): return lax.ppermute(values, axis, [(i, i ^ step) for i in range(size)])]
    ppermute x18, starting transfers between devices: 50.1 us -> 74.5 us  [swap(): return lax.ppermute(values, axis, [(i, i ^ step) for i in range(size)])]
    pallas_call x1, Pallas kernels: 15.1 us -> 13 us  [finish(): pl.pallas_call(functools.partial(finish_kernel, chunks=chunks, samples=sa...]
    unnamed x10 -> x6, local copies, waits for them, and re-layouts: 3.5 us -> 1.66 us
    dynamic_slice x4 -> x5, local copies, waits for them, and re-layouts: 8.98 us -> 9.75 us  [cut(): lax.dynamic_slice(values, (0, target * depth + start), (own_cols, size))]
  transfers between devices with their start and end apart: 18 -> 18, of which waited for: 10 -> 9; matrix products, arithmetic and copies ran while one was open for 8% -> 9% of each run, Pallas kernels for 5% -> 5%
where the time goes in v4:
time: 178 us
  starting transfers between devices  74.5 us (42%)
  waiting for transfers between devices  60.7 us (34%)
  Pallas kernels  22.8 us (13%)
  local copies, waits for them, and re-layouts  11.7 us (7%)
  matrix products  6.97 us (4%)
    ppermute x18, starting transfers between devices, swap(): return lax.ppermute(values, axis, [(i, i ^ step) for i in range(size)])  74.5 us
    ppermute x18, waiting for transfers between devices, swap(): return lax.ppermute(values, axis, [(i, i ^ step) for i in range(size)])  60.7 us
    pallas_call x1, Pallas kernels, finish(): pl.pallas_call(functools.partial(finish_kernel, chunks=chunks, samples=sa...  13 us
    dynamic_slice x5, local copies, waits for them, and re-layouts, cut(): lax.dynamic_slice(values, (0, target * depth + start), (own_cols, size))  9.75 us
    pallas_call x4, Pallas kernels, add_chunk(): pl.pallas_call(functools.partial(body, peers=peers), out_shape=sums + ter...  9.75 us
    dot_general x1, matrix products, shards(): jnp.dot(columns, last_snapshot, precision=HIGHEST, preferred_element_type...  6.97 us
  transfers between devices with their start and end apart: 18, of which 9 were waited for; matrix products, arithmetic and copies ran while one was open for 9% of the time, Pallas kernels for 5%

profile of v4, /device:TPU:0, one launch (start us, length us, event | category | flops | bytes accessed | tf_op | source)
XLA Modules:
  0.0 177.7 jit_solution(12312613028355574466)
XLA Ops:
  0.6 0.0 copy-start
  0.7 1.1 dynamic-slice_bitcast_fusion
  1.8 4.1 %collective-permute-start.10 = (f32[64,1024]{1,0:T(8,128)S(1)}, f32[64,1024]{1,0:T(8,128)S(1)}, u32[]{:S(2)}, u32[]{:S(2)}) collective-permute-start(f32[64,1024]{1,0:T(8,128)S(1)} %get-tuple-element.28), channel_id=1, source_target_pairs={{0,16},{8,24},{16,0},{24,8},{1,17},{9,25},{17,1},{25,9},{2,18},{10... | collective-permute-start | bytes 786440 | tf_op jit(solution)/shard_map/ppermute | solution.py:283
  5.9 1.3 collective-permute-start.11
  7.2 0.0 copy-done
  7.2 7.0 %convolution_bitcast_fusion = f32[64]{0:T(128)S(1)} fusion(f32[64,24576]{1,0:T(8,128)} %bitcast.14, f32[24576,1]{0,1:T(1,128)S(1)} %bitcast.12), kind=kOutput, calls=%fused_computation | convolution fusion | flops 18874368 | bytes 6390016 | tf_op jit(solution)/shard_map/dot_general | solution.py:318
  14.2 1.8 %constant_dynamic-slice_fusion = (f32[64,1024]{1,0:T(8,128)}, f32[64,1024]{1,0:T(8,128)S(1)}) fusion(f32[64,24576]{1,0:T(8,128)} %bitcast.15, s32[]{:T(128)S(6)} %select_n.66, s32[]{:T(128)S(6)} %select_n.65), kind=kLoop, calls=%fused_computation.3 | loop fusion | bytes 1048584 | tf_op jit(solution)/shard_map/dynamic_slice | solution.py:311
  16.0 0.2 collective-permute-start.9
  16.2 2.7 %constant_dynamic-slice_fusion.6 = (f32[64,2048]{1,0:T(8,128)}, f32[64,2048]{1,0:T(8,128)}, f32[64,2048]{1,0:T(8,128)}, f32[64,2048]{1,0:T(8,128)S(1)}) fusion(f32[64,24576]{1,0:T(8,128)} %bitcast.16, s32[]{:T(128)S(6)} %select_n.60, s32[]{:T(128)S(6)} %select_n.59, s32[]{:T(128)S(6)} %select_n.58, s32[]{:T(128)S(6)} %select_n.57), kind=kLoop, calls=%fused_computation.9 | loop fusion | bytes 4194320 | tf_op jit(solution)/shard_map/dynamic_slice | solution.py:311
  18.9 2.9 %collective-permute-start.5 = (f32[64,2048]{1,0:T(8,128)}, f32[64,2048]{1,0:T(8,128)}, u32[]{:S(2)}, u32[]{:S(2)}) collective-permute-start(f32[64,2048]{1,0:T(8,128)} %get-tuple-element.54), channel_id=1, source_target_pairs={{0,24},{8,16},{16,8},{24,0},{1,25},{9,17},{17,9},{25,1},{2,26},{10... | collective-permute-start | bytes 1572872 | tf_op jit(solution)/shard_map/ppermute | solution.py:283
  21.9 2.8 %constant_dynamic-slice_fusion.2 = (f32[64,2304]{1,0:T(8,128)}, f32[64,2304]{1,0:T(8,128)}, f32[64,2304]{1,0:T(8,128)}, f32[64,2304]{1,0:T(8,128)S(1)}) fusion(f32[64,24576]{1,0:T(8,128)} %bitcast.17, s32[]{:T(128)S(6)} %select_n.64, s32[]{:T(128)S(6)} %select_n.63, s32[]{:T(128)S(6)} %select_n.62, s32[]{:T(128)S(6)} %select_n.61), kind=kLoop, calls=%fused_computation.5 | loop fusion | bytes 4718608 | tf_op jit(solution)/shard_map/dynamic_slice | solution.py:311
  24.7 0.9 collective-permute-start.8
  25.6 0.0 collective-permute-done.10.refs_2_
  25.6 1.0 collective-permute-start.7
  26.6 0.0 collective-permute-done.11.refs_3_
  26.6 0.0 copy-start.1
  26.6 0.7 copy-done.1
  27.3 40.4 %collective-permute-start.6 = (f32[64,2304]{1,0:T(8,128)}, f32[64,2304]{1,0:T(8,128)S(1)}, u32[]{:S(2)}, u32[]{:S(2)}) collective-permute-start(f32[64,2304]{1,0:T(8,128)} %get-tuple-element.52), channel_id=1, source_target_pairs={{0,8},{8,0},{16,24},{24,16},{1,9},{9,1},{17,25},{25,17},{2,10},{10... | collective-permute-start | bytes 1769480 | tf_op jit(solution)/shard_map/ppermute | solution.py:283
  67.7 0.0 collective-permute-done.9.refs_1_
  67.7 1.3 collective-permute-start.4
  69.0 0.0 collective-permute-done.5.refs_3_
  69.0 9.3 %collective-permute-start.3 = (f32[64,2048]{1,0:T(8,128)}, f32[64,2048]{1,0:T(8,128)}, u32[]{:S(2)}, u32[]{:S(2)}) collective-permute-start(f32[64,2048]{1,0:T(8,128)} %get-tuple-element.56), channel_id=1, source_target_pairs={{0,8},{8,0},{16,24},{24,16},{1,9},{9,1},{17,25},{25,17},{2,10},{10... | collective-permute-start | bytes 1572872 | tf_op jit(solution)/shard_map/ppermute | solution.py:283
  78.3 0.3 dynamic_update_slice.3
  78.6 1.3 constant_dynamic-slice_fusion.10
  80.0 0.0 copy-start.2
  80.0 0.9 copy-done.2
  80.9 2.3 %gram_chunk.4 = (f32[3,128,128]{2,1,0:T(8,128)S(1)}, bf16[1024,256]{1,0:T(8,128)(2,1)S(1)}, bf16[1024,256]{1,0:T(8,128)(2,1)S(1)}) custom-call(f32[64,1024]{1,0:T(8,128)S(1)} %get-tuple-element.49.refs_0_, f32[64,1024]{1,0:T(8,128)} %collective-permute-done.9.refs_1_, f32[64,1024]{1,0:T(8,128)S(1)} %collective-permute-done.10.refs_2_, f32[64,1024]{1,0:T(8,128)S(1)} %copy-done.2), custom_call_target="tpu_custom_call" | custom-call | flops 805306368 | bytes 2097152 | tf_op jit(solution)/shard_map/gram_chunk/pallas_call | solution.py:111
  83.2 0.0 collective-permute-done.8.refs_3_
  83.2 2.9 %collective-permute-start.2 = (f32[64,768]{1,0:T(8,128)S(1)}, f32[64,768]{1,0:T(8,128)S(1)}, u32[]{:S(2)}, u32[]{:S(2)}) collective-permute-start(f32[64,768]{1,0:T(8,128)S(1)} %get-tuple-element.58), channel_id=1, source_target_pairs={{0,24},{8,16},{16,8},{24,0},{1,25},{9,17},{17,9},{25,1},{2,26},{10... | collective-permute-start | bytes 589832 | tf_op jit(solution)/shard_map/ppermute | solution.py:283
  86.1 32.3 %collective-permute-done.7.refs_2_ = f32[64,2304]{1,0:T(8,128)S(1)} collective-permute-done((f32[64,2304]{1,0:T(8,128)}, f32[64,2304]{1,0:T(8,128)S(1)}, u32[]{:S(2)}, u32[]{:S(2)}) %collective-permute-start.7) | collective-permute-done | bytes 589856 | tf_op jit(solution)/shard_map/ppermute | solution.py:283
  118.4 0.0 collective-permute-start.1
  118.4 0.0 collective-permute-done.6.refs_1_
  118.4 3.4 %collective-permute-start = (f32[64,768]{1,0:T(8,128)S(1)}, f32[64,768]{1,0:T(8,128)S(1)}, u32[]{:S(2)}, u32[]{:S(2)}) collective-permute-start(f32[64,768]{1,0:T(8,128)S(1)} %get-tuple-element.60), channel_id=1, source_target_pairs={{0,8},{8,0},{16,24},{24,16},{1,9},{9,1},{17,25},{25,17},{2,10},{10... | collective-permute-start | bytes 589832 | tf_op jit(solution)/shard_map/ppermute | solution.py:283
  121.8 2.6 %gram_chunk.5 = (f32[3,128,128]{2,1,0:T(8,128)S(1)}, bf16[2304,256]{1,0:T(8,128)(2,1)S(1)}, bf16[2304,256]{1,0:T(8,128)(2,1)S(1)}) custom-call(f32[64,2304]{1,0:T(8,128)S(1)} %get-tuple-element.53.refs_0_, f32[64,2304]{1,0:T(8,128)S(1)} %collective-permute-done.6.refs_1_, f32[64,2304]{1,0:T(8,128)S(1)} %collective-permute-done.7.refs_2_, ...), custom_call_target="tpu_custom_call" | custom-call | flops 1811939328 | bytes 4718592 | tf_op jit(solution)/shard_map/gram_chunk/pallas_call | solution.py:111
  124.4 9.6 %collective-permute-done.4.refs_2_ = f32[64,2048]{1,0:T(8,128)} collective-permute-done((f32[64,2048]{1,0:T(8,128)}, f32[64,2048]{1,0:T(8,128)}, u32[]{:S(2)}, u32[]{:S(2)}) %collective-permute-start.4) | collective-permute-done | bytes 524320 | tf_op jit(solution)/shard_map/ppermute | solution.py:283
  134.0 0.0 collective-permute-done.3.refs_1_
  134.0 3.7 %gram_chunk.6 = (f32[3,128,128]{2,1,0:T(8,128)S(1)}, bf16[2048,256]{1,0:T(8,128)(2,1)S(1)}, bf16[2048,256]{1,0:T(8,128)(2,1)S(1)}) custom-call(f32[64,2048]{1,0:T(8,128)S(1)} %get-tuple-element.57.refs_0_, f32[64,2048]{1,0:T(8,128)} %collective-permute-done.3.refs_1_, f32[64,2048]{1,0:T(8,128)} %collective-permute-done.4.refs_2_, ...), custom_call_target="tpu_custom_call" | custom-call | flops 1610612736 | bytes 4194304 | tf_op jit(solution)/shard_map/gram_chunk/pallas_call | solution.py:111
  137.7 0.0 collective-permute-done.2.refs_3_
  137.7 3.8 %collective-permute-done.1.refs_2_ = f32[64,768]{1,0:T(8,128)S(1)} collective-permute-done((f32[64,768]{1,0:T(8,128)S(1)}, f32[64,768]{1,0:T(8,128)S(1)}, u32[]{:S(2)}, u32[]{:S(2)}) %collective-permute-start.1) | collective-permute-done | bytes 196640 | tf_op jit(solution)/shard_map/ppermute | solution.py:283
  141.5 0.0 collective-permute-done.refs_1_
  141.5 1.1 gram_chunk.7
  142.6 0.1 collective-permute-start.12
  142.7 1.2 collective-permute-done.12
  143.9 1.6 collective-permute-start.13
  145.5 2.8 %collective-permute-done.13 = f32[136,128]{1,0:T(8,128)S(1)} collective-permute-done((f32[136,128]{1,0:T(8,128)S(1)}, f32[136,128]{1,0:T(8,128)S(1)}, u32[]{:S(2)}, u32[]{:S(2)}) %collective-permute-start.13) | collective-permute-done | bytes 69664 | tf_op jit(solution)/shard_map/ppermute | solution.py:283
  148.3 1.6 collective-permute-start.14
  149.9 2.7 %collective-permute-done.14 = f32[136,128]{1,0:T(8,128)S(1)} collective-permute-done((f32[136,128]{1,0:T(8,128)S(1)}, f32[136,128]{1,0:T(8,128)S(1)}, u32[]{:S(2)}, u32[]{:S(2)}) %collective-permute-start.14) | collective-permute-done | bytes 69664 | tf_op jit(solution)/shard_map/ppermute | solution.py:283
  152.7 0.8 collective-permute-start.15
  153.5 3.6 %collective-permute-done.15 = f32[136,128]{1,0:T(8,128)S(1)} collective-permute-done((f32[136,128]{1,0:T(8,128)S(1)}, f32[136,128]{1,0:T(8,128)S(1)}, u32[]{:S(2)}, u32[]{:S(2)}) %collective-permute-start.15) | collective-permute-done | bytes 69664 | tf_op jit(solution)/shard_map/ppermute | solution.py:283
  157.1 2.6 %collective-permute-start.16 = (f32[136,128]{1,0:T(8,128)S(1)}, f32[136,128]{1,0:T(8,128)S(1)}, u32[]{:S(2)}, u32[]{:S(2)}) collective-permute-start(f32[136,128]{1,0:T(8,128)S(1)} %add.158), channel_id=1, source_target_pairs={{0,16},{8,24},{16,0},{24,8},{1,17},{9,25},{17,1},{25,9},{2,18},{10... | collective-permute-start | bytes 208904 | tf_op jit(solution)/shard_map/ppermute | solution.py:283
  159.7 3.5 %collective-permute-done.16 = f32[136,128]{1,0:T(8,128)S(1)} collective-permute-done((f32[136,128]{1,0:T(8,128)S(1)}, f32[136,128]{1,0:T(8,128)S(1)}, u32[]{:S(2)}, u32[]{:S(2)}) %collective-permute-start.16) | collective-permute-done | bytes 69664 | tf_op jit(solution)/shard_map/ppermute | solution.py:283
  163.1 0.1 collective-permute-start.17
  163.2 1.2 collective-permute-done.17.refs_1_
  164.4 13.0 %factor_and_basis.1 = (f32[6144,256]{1,0:T(8,128)}, f32[256,256]{1,0:T(8,128)}, f32[256,256]{1,0:T(8,128)}, f32[256,256]{1,0:T(8,128)}) custom-call(f32[136,128]{1,0:T(8,128)S(1)} %add.159.refs_0_, f32[136,128]{1,0:T(8,128)S(1)} %collective-permute-done.17.refs_1_, bf16[1024,256]{1,0:T(8,128)(2,1)S(1)} %get-tuple-element.36.refs_2_, ...), custom_call_target="tpu_custom_call" | custom-call | tf_op jit(solution)/shard_map/factor_and_basis/pallas_call | solution.py:264
  (6 shorter events, 0.0 us)
Async XLA Ops:
  0.6 6.6 %copy-start = (f32[24576]{0:T(1024)S(1)}, f32[24576]{0:T(1024)}, u32[]{:S(2)}) copy-start(f32[24576]{0:T(1024)} %param.3) | copy-start | bytes 294916
  1.8 23.8 %collective-permute-start.10 = (f32[64,1024]{1,0:T(8,128)S(1)}, f32[64,1024]{1,0:T(8,128)S(1)}, u32[]{:S(2)}, u32[]{:S(2)}) collective-permute-start(f32[64,1024]{1,0:T(8,128)S(1)} %get-tuple-element.28), channel_id=1, source_target_pairs={{0,16},{8,24},{16,0},{24,8},{1,17},{9,25},{17,1},{25,9},{2,18},{10... | collective-permute-start | bytes 786440 | tf_op jit(solution)/shard_map/ppermute | solution.py:283
  5.9 20.8 %collective-permute-start.11 = (f32[64,1024]{1,0:T(8,128)S(1)}, f32[64,1024]{1,0:T(8,128)S(1)}, u32[]{:S(2)}, u32[]{:S(2)}) collective-permute-start(f32[64,1024]{1,0:T(8,128)S(1)} %get-tuple-element.29), channel_id=1, source_target_pairs={{0,24},{8,16},{16,8},{24,0},{1,25},{9,17},{17,9},{25,1},{2,26},{10... | collective-permute-start | bytes 786440 | tf_op jit(solution)/shard_map/ppermute | solution.py:283
  16.0 51.7 %collective-permute-start.9 = (f32[64,1024]{1,0:T(8,128)}, f32[64,1024]{1,0:T(8,128)}, u32[]{:S(2)}, u32[]{:S(2)}) collective-permute-start(f32[64,1024]{1,0:T(8,128)} %get-tuple-element.48), channel_id=1, source_target_pairs={{0,8},{8,0},{16,24},{24,16},{1,9},{9,1},{17,25},{25,17},{2,10},{10... | collective-permute-start | bytes 786440 | tf_op jit(solution)/shard_map/ppermute | solution.py:283
  18.9 50.1 %collective-permute-start.5 = (f32[64,2048]{1,0:T(8,128)}, f32[64,2048]{1,0:T(8,128)}, u32[]{:S(2)}, u32[]{:S(2)}) collective-permute-start(f32[64,2048]{1,0:T(8,128)} %get-tuple-element.54), channel_id=1, source_target_pairs={{0,24},{8,16},{16,8},{24,0},{1,25},{9,17},{17,9},{25,1},{2,26},{10... | collective-permute-start | bytes 1572872 | tf_op jit(solution)/shard_map/ppermute | solution.py:283
  24.7 58.5 %collective-permute-start.8 = (f32[64,2304]{1,0:T(8,128)}, f32[64,2304]{1,0:T(8,128)S(1)}, u32[]{:S(2)}, u32[]{:S(2)}) collective-permute-start(f32[64,2304]{1,0:T(8,128)} %get-tuple-element.50), channel_id=1, source_target_pairs={{0,24},{8,16},{16,8},{24,0},{1,25},{9,17},{17,9},{25,1},{2,26},{10... | collective-permute-start | bytes 1769480 | tf_op jit(solution)/shard_map/ppermute | solution.py:283
  25.6 92.8 %collective-permute-start.7 = (f32[64,2304]{1,0:T(8,128)}, f32[64,2304]{1,0:T(8,128)S(1)}, u32[]{:S(2)}, u32[]{:S(2)}) collective-permute-start(f32[64,2304]{1,0:T(8,128)} %get-tuple-element.51), channel_id=1, source_target_pairs={{0,16},{8,24},{16,0},{24,8},{1,17},{9,25},{17,1},{25,9},{2,18},{10... | collective-permute-start | bytes 1769480 | tf_op jit(solution)/shard_map/ppermute | solution.py:283
  26.6 0.7 copy-start.1
  27.3 91.1 %collective-permute-start.6 = (f32[64,2304]{1,0:T(8,128)}, f32[64,2304]{1,0:T(8,128)S(1)}, u32[]{:S(2)}, u32[]{:S(2)}) collective-permute-start(f32[64,2304]{1,0:T(8,128)} %get-tuple-element.52), channel_id=1, source_target_pairs={{0,8},{8,0},{16,24},{24,16},{1,9},{9,1},{17,25},{25,17},{2,10},{10... | collective-permute-start | bytes 1769480 | tf_op jit(solution)/shard_map/ppermute | solution.py:283
  67.7 66.3 %collective-permute-start.4 = (f32[64,2048]{1,0:T(8,128)}, f32[64,2048]{1,0:T(8,128)}, u32[]{:S(2)}, u32[]{:S(2)}) collective-permute-start(f32[64,2048]{1,0:T(8,128)} %get-tuple-element.55), channel_id=1, source_target_pairs={{0,16},{8,24},{16,0},{24,8},{1,17},{9,25},{17,1},{25,9},{2,18},{10... | collective-permute-start | bytes 1572872 | tf_op jit(solution)/shard_map/ppermute | solution.py:283
  69.0 64.9 %collective-permute-start.3 = (f32[64,2048]{1,0:T(8,128)}, f32[64,2048]{1,0:T(8,128)}, u32[]{:S(2)}, u32[]{:S(2)}) collective-permute-start(f32[64,2048]{1,0:T(8,128)} %get-tuple-element.56), channel_id=1, source_target_pairs={{0,8},{8,0},{16,24},{24,16},{1,9},{9,1},{17,25},{25,17},{2,10},{10... | collective-permute-start | bytes 1572872 | tf_op jit(solution)/shard_map/ppermute | solution.py:283
  80.0 1.0 copy-start.2
  83.2 54.5 %collective-permute-start.2 = (f32[64,768]{1,0:T(8,128)S(1)}, f32[64,768]{1,0:T(8,128)S(1)}, u32[]{:S(2)}, u32[]{:S(2)}) collective-permute-start(f32[64,768]{1,0:T(8,128)S(1)} %get-tuple-element.58), channel_id=1, source_target_pairs={{0,24},{8,16},{16,8},{24,0},{1,25},{9,17},{17,9},{25,1},{2,26},{10... | collective-permute-start | bytes 589832 | tf_op jit(solution)/shard_map/ppermute | solution.py:283
  118.4 23.1 %collective-permute-start.1 = (f32[64,768]{1,0:T(8,128)S(1)}, f32[64,768]{1,0:T(8,128)S(1)}, u32[]{:S(2)}, u32[]{:S(2)}) collective-permute-start(f32[64,768]{1,0:T(8,128)S(1)} %get-tuple-element.59), channel_id=1, source_target_pairs={{0,16},{8,24},{16,0},{24,8},{1,17},{9,25},{17,1},{25,9},{2,18},{10... | collective-permute-start | bytes 589832 | tf_op jit(solution)/shard_map/ppermute | solution.py:283
  118.4 23.1 %collective-permute-start = (f32[64,768]{1,0:T(8,128)S(1)}, f32[64,768]{1,0:T(8,128)S(1)}, u32[]{:S(2)}, u32[]{:S(2)}) collective-permute-start(f32[64,768]{1,0:T(8,128)S(1)} %get-tuple-element.60), channel_id=1, source_target_pairs={{0,8},{8,0},{16,24},{24,16},{1,9},{9,1},{17,25},{25,17},{2,10},{10... | collective-permute-start | bytes 589832 | tf_op jit(solution)/shard_map/ppermute | solution.py:283
  142.6 1.3 collective-permute-start.12
  143.9 4.4 %collective-permute-start.13 = (f32[136,128]{1,0:T(8,128)S(1)}, f32[136,128]{1,0:T(8,128)S(1)}, u32[]{:S(2)}, u32[]{:S(2)}) collective-permute-start(f32[136,128]{1,0:T(8,128)S(1)} %add.155), channel_id=1, source_target_pairs={{0,2},{1,3},{2,0},{3,1},{4,6},{5,7},{6,4},{7,5},{8,10},{9,11},{10,... | collective-permute-start | bytes 208904 | tf_op jit(solution)/shard_map/ppermute | solution.py:283
  148.3 4.4 %collective-permute-start.14 = (f32[136,128]{1,0:T(8,128)S(1)}, f32[136,128]{1,0:T(8,128)S(1)}, u32[]{:S(2)}, u32[]{:S(2)}) collective-permute-start(f32[136,128]{1,0:T(8,128)S(1)} %add.156), channel_id=1, source_target_pairs={{0,4},{1,5},{2,6},{3,7},{4,0},{5,1},{6,2},{7,3},{8,12},{9,13},{10,... | collective-permute-start | bytes 208904 | tf_op jit(solution)/shard_map/ppermute | solution.py:283
  152.7 4.4 %collective-permute-start.15 = (f32[136,128]{1,0:T(8,128)S(1)}, f32[136,128]{1,0:T(8,128)S(1)}, u32[]{:S(2)}, u32[]{:S(2)}) collective-permute-start(f32[136,128]{1,0:T(8,128)S(1)} %add.157), channel_id=1, source_target_pairs={{0,8},{8,0},{16,24},{24,16},{1,9},{9,1},{17,25},{25,17},{2,10},{10... | collective-permute-start | bytes 208904 | tf_op jit(solution)/shard_map/ppermute | solution.py:283
  157.1 6.0 %collective-permute-start.16 = (f32[136,128]{1,0:T(8,128)S(1)}, f32[136,128]{1,0:T(8,128)S(1)}, u32[]{:S(2)}, u32[]{:S(2)}) collective-permute-start(f32[136,128]{1,0:T(8,128)S(1)} %add.158), channel_id=1, source_target_pairs={{0,16},{8,24},{16,0},{24,8},{1,17},{9,25},{17,1},{25,9},{2,18},{10... | collective-permute-start | bytes 208904 | tf_op jit(solution)/shard_map/ppermute | solution.py:283
  163.1 1.3 collective-permute-start.17

commit v5 on v4

--- a/solution.py
+++ b/solution.py
@@ -191,13 +191,16 @@
         if later >= count:
             continue
         skip = later // LANES
-        multiplier = jnp.concatenate(scaled[skip:], axis=1)
-        update = dot(
-            multiplier, jnp.concatenate(halves, axis=1), dims=((0,), (0,)), precision=HIGHEST
-        )
-        wide = iota((count - later, count), 1)
-        old = jnp.where((wide >= at) & (wide < below), 0.0, work[later:, :])
-        work[later:, :] = old - update[later - skip * LANES :, :]
+        multiplier = jnp.concatenate([part.T for part in scaled[skip:]], axis=0)
+        finished = jnp.concatenate(halves, axis=1)
+        for top, end in ((later, later + n), (later + n, count)):
+            if top >= end:
+                continue
+            from_row = skip * LANES
+            update = dot(multiplier[top - from_row : end - from_row], finished, precision=HIGHEST)
+            wide = iota((end - top, count), 1)
+            old = jnp.where((wide >= at) & (wide < below), 0.0, work[top:end, :])
+            work[top:end, :] = old - update
 
 
 def finish_kernel(*refs, chunks, samples):
@@ -286,9 +289,16 @@
 def sum_halves(keep, send):
     keep = keep + swap(send, "rows", 1)
     for axis, step in (("rows", 2), ("tm", 1)):
-        while step < lax.axis_size(axis):
-            keep = keep + swap(keep, axis, step)
-            step *= 2
+        size = lax.axis_size(axis)
+        while step < size:
+            if 2 * step < size:
+                far = swap(keep, axis, 3 * step)
+                near = swap(keep, axis, step)
+                other = swap(keep, axis, 2 * step)
+                keep = (keep + near) + (other + far)
+            else:
+                keep = keep + swap(keep, axis, step)
+            step *= 4
     return keep, swap(keep, "rows", 1)
 
 

time: 178 us -> 175 us (0.983)
  waiting for transfers between devices: 60.7 us -> 56.8 us
    ppermute x18 -> x20, waiting for transfers between devices: 60.7 us -> 56.8 us  [swap(): return lax.ppermute(values, axis, [(i, i ^ step) for i in range(size)])]
    ppermute x18 -> x20, starting transfers between devices: 74.5 us -> 75.9 us  [swap(): return lax.ppermute(values, axis, [(i, i ^ step) for i in range(size)])]
  transfers between devices with their start and end apart: 18 -> 20, of which waited for: 9 -> 11; matrix products, arithmetic and copies ran while one was open for 9% -> 9% of each run, Pallas kernels for 5% -> 5%
where the time goes in v5:
time: 175 us; the launch traced here: 174 us
  starting transfers between devices  75.9 us (43%)
  waiting for transfers between devices  56.8 us (32%)
  Pallas kernels  21.8 us (12%)
  local copies, waits for them, and re-layouts  11.7 us (7%)
  matrix products  6.97 us (4%)
    ppermute x20, starting transfers between devices, swap(): return lax.ppermute(values, axis, [(i, i ^ step) for i in range(size)])  75.9 us
    ppermute x20, waiting for transfers between devices, swap(): return lax.ppermute(values, axis, [(i, i ^ step) for i in range(size)])  56.8 us
    pallas_call x1, Pallas kernels, finish(): pl.pallas_call(functools.partial(finish_kernel, chunks=chunks, samples=sa...  12.1 us
    dynamic_slice x5, local copies, waits for them, and re-layouts, cut(): lax.dynamic_slice(values, (0, target * depth + start), (own_cols, size))  9.75 us
    pallas_call x4, Pallas kernels, add_chunk(): pl.pallas_call(functools.partial(body, peers=peers), out_shape=sums + ter...  9.75 us
    dot_general x1, matrix products, shards(): jnp.dot(columns, last_snapshot, precision=HIGHEST, preferred_element_type...  6.97 us
  transfers between devices with their start and end apart: 20, of which 11 were waited for; matrix products, arithmetic and copies ran while one was open for 9% of the time, Pallas kernels for 5%

profile of v5, /device:TPU:0, one launch (start us, length us, event | category | flops | bytes accessed | tf_op | source)
XLA Modules:
  0.0 174.2 jit_solution(1211009286551914258)
XLA Ops:
  0.6 0.0 copy-start
  0.7 1.1 dynamic-slice_bitcast_fusion
  1.8 4.1 %collective-permute-start.10 = (f32[64,1024]{1,0:T(8,128)S(1)}, f32[64,1024]{1,0:T(8,128)S(1)}, u32[]{:S(2)}, u32[]{:S(2)}) collective-permute-start(f32[64,1024]{1,0:T(8,128)S(1)} %get-tuple-element.28), channel_id=1, source_target_pairs={{0,16},{8,24},{16,0},{24,8},{1,17},{9,25},{17,1},{25,9},{2,18},{10... | collective-permute-start | bytes 786440 | tf_op jit(solution)/shard_map/ppermute | solution.py:286
  5.9 1.3 collective-permute-start.11
  7.2 0.0 copy-done
  7.2 7.0 %convolution_bitcast_fusion = f32[64]{0:T(128)S(1)} fusion(f32[64,24576]{1,0:T(8,128)} %bitcast.14, f32[24576,1]{0,1:T(1,128)S(1)} %bitcast.12), kind=kOutput, calls=%fused_computation | convolution fusion | flops 18874368 | bytes 6390016 | tf_op jit(solution)/shard_map/dot_general | solution.py:328
  14.2 1.8 %constant_dynamic-slice_fusion = (f32[64,1024]{1,0:T(8,128)}, f32[64,1024]{1,0:T(8,128)S(1)}) fusion(f32[64,24576]{1,0:T(8,128)} %bitcast.15, s32[]{:T(128)S(6)} %select_n.66, s32[]{:T(128)S(6)} %select_n.65), kind=kLoop, calls=%fused_computation.5 | loop fusion | bytes 1048584 | tf_op jit(solution)/shard_map/dynamic_slice | solution.py:321
  16.0 0.2 collective-permute-start.9
  16.2 2.7 %constant_dynamic-slice_fusion.6 = (f32[64,2048]{1,0:T(8,128)}, f32[64,2048]{1,0:T(8,128)}, f32[64,2048]{1,0:T(8,128)}, f32[64,2048]{1,0:T(8,128)S(1)}) fusion(f32[64,24576]{1,0:T(8,128)} %bitcast.16, s32[]{:T(128)S(6)} %select_n.60, s32[]{:T(128)S(6)} %select_n.59, s32[]{:T(128)S(6)} %select_n.58, s32[]{:T(128)S(6)} %select_n.57), kind=kLoop, calls=%fused_computation.11 | loop fusion | bytes 4194320 | tf_op jit(solution)/shard_map/dynamic_slice | solution.py:321
  18.9 2.9 %collective-permute-start.5 = (f32[64,2048]{1,0:T(8,128)}, f32[64,2048]{1,0:T(8,128)}, u32[]{:S(2)}, u32[]{:S(2)}) collective-permute-start(f32[64,2048]{1,0:T(8,128)} %get-tuple-element.54), channel_id=1, source_target_pairs={{0,24},{8,16},{16,8},{24,0},{1,25},{9,17},{17,9},{25,1},{2,26},{10... | collective-permute-start | bytes 1572872 | tf_op jit(solution)/shard_map/ppermute | solution.py:286
  21.9 2.9 %constant_dynamic-slice_fusion.2 = (f32[64,2304]{1,0:T(8,128)}, f32[64,2304]{1,0:T(8,128)}, f32[64,2304]{1,0:T(8,128)}, f32[64,2304]{1,0:T(8,128)S(1)}) fusion(f32[64,24576]{1,0:T(8,128)} %bitcast.17, s32[]{:T(128)S(6)} %select_n.64, s32[]{:T(128)S(6)} %select_n.63, s32[]{:T(128)S(6)} %select_n.62, s32[]{:T(128)S(6)} %select_n.61), kind=kLoop, calls=%fused_computation.7 | loop fusion | bytes 4718608 | tf_op jit(solution)/shard_map/dynamic_slice | solution.py:321
  24.7 0.9 collective-permute-start.8
  25.6 0.0 collective-permute-done.10.refs_2_
  25.6 1.0 collective-permute-start.7
  26.6 0.0 collective-permute-done.11.refs_3_
  26.6 0.0 copy-start.1
  26.6 0.7 copy-done.1
  27.3 40.4 %collective-permute-start.6 = (f32[64,2304]{1,0:T(8,128)}, f32[64,2304]{1,0:T(8,128)S(1)}, u32[]{:S(2)}, u32[]{:S(2)}) collective-permute-start(f32[64,2304]{1,0:T(8,128)} %get-tuple-element.52), channel_id=1, source_target_pairs={{0,8},{8,0},{16,24},{24,16},{1,9},{9,1},{17,25},{25,17},{2,10},{10... | collective-permute-start | bytes 1769480 | tf_op jit(solution)/shard_map/ppermute | solution.py:286
  67.7 0.0 collective-permute-done.9.refs_1_
  67.7 1.3 collective-permute-start.4
  69.0 0.0 collective-permute-done.5.refs_3_
  69.0 9.3 %collective-permute-start.3 = (f32[64,2048]{1,0:T(8,128)}, f32[64,2048]{1,0:T(8,128)}, u32[]{:S(2)}, u32[]{:S(2)}) collective-permute-start(f32[64,2048]{1,0:T(8,128)} %get-tuple-element.56), channel_id=1, source_target_pairs={{0,8},{8,0},{16,24},{24,16},{1,9},{9,1},{17,25},{25,17},{2,10},{10... | collective-permute-start | bytes 1572872 | tf_op jit(solution)/shard_map/ppermute | solution.py:286
  78.3 0.3 dynamic_update_slice.3
  78.6 1.3 constant_dynamic-slice_fusion.10
  80.0 0.0 copy-start.2
  80.0 0.9 copy-done.2
  80.9 2.3 %gram_chunk.4 = (f32[3,128,128]{2,1,0:T(8,128)S(1)}, bf16[1024,256]{1,0:T(8,128)(2,1)S(1)}, bf16[1024,256]{1,0:T(8,128)(2,1)S(1)}) custom-call(f32[64,1024]{1,0:T(8,128)S(1)} %get-tuple-element.49.refs_0_, f32[64,1024]{1,0:T(8,128)} %collective-permute-done.9.refs_1_, f32[64,1024]{1,0:T(8,128)S(1)} %collective-permute-done.10.refs_2_, f32[64,1024]{1,0:T(8,128)S(1)} %copy-done.2), custom_call_target="tpu_custom_call" | custom-call | flops 805306368 | bytes 2097152 | tf_op jit(solution)/shard_map/gram_chunk/pallas_call | solution.py:111
  83.2 0.0 collective-permute-done.8.refs_3_
  83.2 2.9 %collective-permute-start.2 = (f32[64,768]{1,0:T(8,128)S(1)}, f32[64,768]{1,0:T(8,128)S(1)}, u32[]{:S(2)}, u32[]{:S(2)}) collective-permute-start(f32[64,768]{1,0:T(8,128)S(1)} %get-tuple-element.58), channel_id=1, source_target_pairs={{0,24},{8,16},{16,8},{24,0},{1,25},{9,17},{17,9},{25,1},{2,26},{10... | collective-permute-start | bytes 589832 | tf_op jit(solution)/shard_map/ppermute | solution.py:286
  86.1 32.3 %collective-permute-done.7.refs_2_ = f32[64,2304]{1,0:T(8,128)S(1)} collective-permute-done((f32[64,2304]{1,0:T(8,128)}, f32[64,2304]{1,0:T(8,128)S(1)}, u32[]{:S(2)}, u32[]{:S(2)}) %collective-permute-start.7) | collective-permute-done | bytes 589856 | tf_op jit(solution)/shard_map/ppermute | solution.py:286
  118.4 0.0 collective-permute-start.1
  118.4 0.0 collective-permute-done.6.refs_1_
  118.4 3.4 %collective-permute-start = (f32[64,768]{1,0:T(8,128)S(1)}, f32[64,768]{1,0:T(8,128)S(1)}, u32[]{:S(2)}, u32[]{:S(2)}) collective-permute-start(f32[64,768]{1,0:T(8,128)S(1)} %get-tuple-element.60), channel_id=1, source_target_pairs={{0,8},{8,0},{16,24},{24,16},{1,9},{9,1},{17,25},{25,17},{2,10},{10... | collective-permute-start | bytes 589832 | tf_op jit(solution)/shard_map/ppermute | solution.py:286
  121.8 2.6 %gram_chunk.5 = (f32[3,128,128]{2,1,0:T(8,128)S(1)}, bf16[2304,256]{1,0:T(8,128)(2,1)S(1)}, bf16[2304,256]{1,0:T(8,128)(2,1)S(1)}) custom-call(f32[64,2304]{1,0:T(8,128)S(1)} %get-tuple-element.53.refs_0_, f32[64,2304]{1,0:T(8,128)S(1)} %collective-permute-done.6.refs_1_, f32[64,2304]{1,0:T(8,128)S(1)} %collective-permute-done.7.refs_2_, ...), custom_call_target="tpu_custom_call" | custom-call | flops 1811939328 | bytes 4718592 | tf_op jit(solution)/shard_map/gram_chunk/pallas_call | solution.py:111
  124.4 9.6 %collective-permute-done.4.refs_2_ = f32[64,2048]{1,0:T(8,128)} collective-permute-done((f32[64,2048]{1,0:T(8,128)}, f32[64,2048]{1,0:T(8,128)}, u32[]{:S(2)}, u32[]{:S(2)}) %collective-permute-start.4) | collective-permute-done | bytes 524320 | tf_op jit(solution)/shard_map/ppermute | solution.py:286
  134.0 0.0 collective-permute-done.3.refs_1_
  134.0 3.7 %gram_chunk.6 = (f32[3,128,128]{2,1,0:T(8,128)S(1)}, bf16[2048,256]{1,0:T(8,128)(2,1)S(1)}, bf16[2048,256]{1,0:T(8,128)(2,1)S(1)}) custom-call(f32[64,2048]{1,0:T(8,128)S(1)} %get-tuple-element.57.refs_0_, f32[64,2048]{1,0:T(8,128)} %collective-permute-done.3.refs_1_, f32[64,2048]{1,0:T(8,128)} %collective-permute-done.4.refs_2_, ...), custom_call_target="tpu_custom_call" | custom-call | flops 1610612736 | bytes 4194304 | tf_op jit(solution)/shard_map/gram_chunk/pallas_call | solution.py:111
  137.7 0.0 collective-permute-done.2.refs_3_
  137.7 3.8 %collective-permute-done.1.refs_2_ = f32[64,768]{1,0:T(8,128)S(1)} collective-permute-done((f32[64,768]{1,0:T(8,128)S(1)}, f32[64,768]{1,0:T(8,128)S(1)}, u32[]{:S(2)}, u32[]{:S(2)}) %collective-permute-start.1) | collective-permute-done | bytes 196640 | tf_op jit(solution)/shard_map/ppermute | solution.py:286
  141.5 0.0 collective-permute-done.refs_1_
  141.5 1.1 gram_chunk.7
  142.6 0.1 collective-permute-start.12
  142.7 1.2 collective-permute-done.12
  143.9 2.6 %collective-permute-start.15 = (f32[136,128]{1,0:T(8,128)S(1)}, f32[136,128]{1,0:T(8,128)S(1)}, u32[]{:S(2)}, u32[]{:S(2)}) collective-permute-start(f32[136,128]{1,0:T(8,128)S(1)} %add.161), channel_id=1, source_target_pairs={{0,6},{1,7},{2,4},{3,5},{4,2},{5,3},{6,0},{7,1},{8,14},{9,15},{10,... | collective-permute-start | bytes 208904 | tf_op jit(solution)/shard_map/ppermute | solution.py:286
  146.5 0.5 collective-permute-start.14
  147.0 0.5 collective-permute-start.13
  147.5 1.7 collective-permute-done.15
  149.2 1.6 collective-permute-done.14
  150.8 0.5 collective-permute-done.13
  151.3 3.6 %collective-permute-start.18 = (f32[136,128]{1,0:T(8,128)S(1)}, f32[136,128]{1,0:T(8,128)S(1)}, u32[]{:S(2)}, u32[]{:S(2)}) collective-permute-start(f32[136,128]{1,0:T(8,128)S(1)} %add_add_fusion.1), channel_id=1, source_target_pairs={{0,24},{8,16},{16,8},{24,0},{1,25},{9,17},{17,9},{25,1},{2,26},{10... | collective-permute-start | bytes 208904 | tf_op jit(solution)/shard_map/ppermute | solution.py:286
  154.9 0.0 collective-permute-start.17
  154.9 0.9 collective-permute-start.16
  155.8 1.8 %collective-permute-done.18 = f32[136,128]{1,0:T(8,128)S(1)} collective-permute-done((f32[136,128]{1,0:T(8,128)S(1)}, f32[136,128]{1,0:T(8,128)S(1)}, u32[]{:S(2)}, u32[]{:S(2)}) %collective-permute-start.18) | collective-permute-done | bytes 69664 | tf_op jit(solution)/shard_map/ppermute | solution.py:286
  157.6 2.5 %collective-permute-done.17 = f32[136,128]{1,0:T(8,128)S(1)} collective-permute-done((f32[136,128]{1,0:T(8,128)S(1)}, f32[136,128]{1,0:T(8,128)S(1)}, u32[]{:S(2)}, u32[]{:S(2)}) %collective-permute-start.17) | collective-permute-done | bytes 69664 | tf_op jit(solution)/shard_map/ppermute | solution.py:286
  160.1 0.5 collective-permute-done.16
  160.6 0.1 collective-permute-start.19
  160.7 1.2 collective-permute-done.19.refs_1_
  162.0 12.1 %factor_and_basis.1 = (f32[6144,256]{1,0:T(8,128)}, f32[256,256]{1,0:T(8,128)}, f32[256,256]{1,0:T(8,128)}, f32[256,256]{1,0:T(8,128)}) custom-call(f32[136,128]{1,0:T(8,128)S(1)} %add_add_fusion.refs_0_, f32[136,128]{1,0:T(8,128)S(1)} %collective-permute-done.19.refs_1_, bf16[1024,256]{1,0:T(8,128)(2,1)S(1)} %get-tuple-element.36.refs_2_, ...), custom_call_target="tpu_custom_call" | custom-call | tf_op jit(solution)/shard_map/factor_and_basis/pallas_call | solution.py:267
  (4 shorter events, 0.0 us)
Async XLA Ops:
  0.6 6.6 %copy-start = (f32[24576]{0:T(1024)S(1)}, f32[24576]{0:T(1024)}, u32[]{:S(2)}) copy-start(f32[24576]{0:T(1024)} %param.3) | copy-start | bytes 294916
  1.8 23.8 %collective-permute-start.10 = (f32[64,1024]{1,0:T(8,128)S(1)}, f32[64,1024]{1,0:T(8,128)S(1)}, u32[]{:S(2)}, u32[]{:S(2)}) collective-permute-start(f32[64,1024]{1,0:T(8,128)S(1)} %get-tuple-element.28), channel_id=1, source_target_pairs={{0,16},{8,24},{16,0},{24,8},{1,17},{9,25},{17,1},{25,9},{2,18},{10... | collective-permute-start | bytes 786440 | tf_op jit(solution)/shard_map/ppermute | solution.py:286
  5.9 20.8 %collective-permute-start.11 = (f32[64,1024]{1,0:T(8,128)S(1)}, f32[64,1024]{1,0:T(8,128)S(1)}, u32[]{:S(2)}, u32[]{:S(2)}) collective-permute-start(f32[64,1024]{1,0:T(8,128)S(1)} %get-tuple-element.29), channel_id=1, source_target_pairs={{0,24},{8,16},{16,8},{24,0},{1,25},{9,17},{17,9},{25,1},{2,26},{10... | collective-permute-start | bytes 786440 | tf_op jit(solution)/shard_map/ppermute | solution.py:286
  16.0 51.7 %collective-permute-start.9 = (f32[64,1024]{1,0:T(8,128)}, f32[64,1024]{1,0:T(8,128)}, u32[]{:S(2)}, u32[]{:S(2)}) collective-permute-start(f32[64,1024]{1,0:T(8,128)} %get-tuple-element.48), channel_id=1, source_target_pairs={{0,8},{8,0},{16,24},{24,16},{1,9},{9,1},{17,25},{25,17},{2,10},{10... | collective-permute-start | bytes 786440 | tf_op jit(solution)/shard_map/ppermute | solution.py:286
  18.9 50.1 %collective-permute-start.5 = (f32[64,2048]{1,0:T(8,128)}, f32[64,2048]{1,0:T(8,128)}, u32[]{:S(2)}, u32[]{:S(2)}) collective-permute-start(f32[64,2048]{1,0:T(8,128)} %get-tuple-element.54), channel_id=1, source_target_pairs={{0,24},{8,16},{16,8},{24,0},{1,25},{9,17},{17,9},{25,1},{2,26},{10... | collective-permute-start | bytes 1572872 | tf_op jit(solution)/shard_map/ppermute | solution.py:286
  24.7 58.5 %collective-permute-start.8 = (f32[64,2304]{1,0:T(8,128)}, f32[64,2304]{1,0:T(8,128)S(1)}, u32[]{:S(2)}, u32[]{:S(2)}) collective-permute-start(f32[64,2304]{1,0:T(8,128)} %get-tuple-element.50), channel_id=1, source_target_pairs={{0,24},{8,16},{16,8},{24,0},{1,25},{9,17},{17,9},{25,1},{2,26},{10... | collective-permute-start | bytes 1769480 | tf_op jit(solution)/shard_map/ppermute | solution.py:286
  25.6 92.8 %collective-permute-start.7 = (f32[64,2304]{1,0:T(8,128)}, f32[64,2304]{1,0:T(8,128)S(1)}, u32[]{:S(2)}, u32[]{:S(2)}) collective-permute-start(f32[64,2304]{1,0:T(8,128)} %get-tuple-element.51), channel_id=1, source_target_pairs={{0,16},{8,24},{16,0},{24,8},{1,17},{9,25},{17,1},{25,9},{2,18},{10... | collective-permute-start | bytes 1769480 | tf_op jit(solution)/shard_map/ppermute | solution.py:286
  26.6 0.7 copy-start.1
  27.3 91.1 %collective-permute-start.6 = (f32[64,2304]{1,0:T(8,128)}, f32[64,2304]{1,0:T(8,128)S(1)}, u32[]{:S(2)}, u32[]{:S(2)}) collective-permute-start(f32[64,2304]{1,0:T(8,128)} %get-tuple-element.52), channel_id=1, source_target_pairs={{0,8},{8,0},{16,24},{24,16},{1,9},{9,1},{17,25},{25,17},{2,10},{10... | collective-permute-start | bytes 1769480 | tf_op jit(solution)/shard_map/ppermute | solution.py:286
  67.7 66.3 %collective-permute-start.4 = (f32[64,2048]{1,0:T(8,128)}, f32[64,2048]{1,0:T(8,128)}, u32[]{:S(2)}, u32[]{:S(2)}) collective-permute-start(f32[64,2048]{1,0:T(8,128)} %get-tuple-element.55), channel_id=1, source_target_pairs={{0,16},{8,24},{16,0},{24,8},{1,17},{9,25},{17,1},{25,9},{2,18},{10... | collective-permute-start | bytes 1572872 | tf_op jit(solution)/shard_map/ppermute | solution.py:286
  69.0 64.9 %collective-permute-start.3 = (f32[64,2048]{1,0:T(8,128)}, f32[64,2048]{1,0:T(8,128)}, u32[]{:S(2)}, u32[]{:S(2)}) collective-permute-start(f32[64,2048]{1,0:T(8,128)} %get-tuple-element.56), channel_id=1, source_target_pairs={{0,8},{8,0},{16,24},{24,16},{1,9},{9,1},{17,25},{25,17},{2,10},{10... | collective-permute-start | bytes 1572872 | tf_op jit(solution)/shard_map/ppermute | solution.py:286
  80.0 1.0 copy-start.2
  83.2 54.5 %collective-permute-start.2 = (f32[64,768]{1,0:T(8,128)S(1)}, f32[64,768]{1,0:T(8,128)S(1)}, u32[]{:S(2)}, u32[]{:S(2)}) collective-permute-start(f32[64,768]{1,0:T(8,128)S(1)} %get-tuple-element.58), channel_id=1, source_target_pairs={{0,24},{8,16},{16,8},{24,0},{1,25},{9,17},{17,9},{25,1},{2,26},{10... | collective-permute-start | bytes 589832 | tf_op jit(solution)/shard_map/ppermute | solution.py:286
  118.4 23.1 %collective-permute-start.1 = (f32[64,768]{1,0:T(8,128)S(1)}, f32[64,768]{1,0:T(8,128)S(1)}, u32[]{:S(2)}, u32[]{:S(2)}) collective-permute-start(f32[64,768]{1,0:T(8,128)S(1)} %get-tuple-element.59), channel_id=1, source_target_pairs={{0,16},{8,24},{16,0},{24,8},{1,17},{9,25},{17,1},{25,9},{2,18},{10... | collective-permute-start | bytes 589832 | tf_op jit(solution)/shard_map/ppermute | solution.py:286
  118.4 23.1 %collective-permute-start = (f32[64,768]{1,0:T(8,128)S(1)}, f32[64,768]{1,0:T(8,128)S(1)}, u32[]{:S(2)}, u32[]{:S(2)}) collective-permute-start(f32[64,768]{1,0:T(8,128)S(1)} %get-tuple-element.60), channel_id=1, source_target_pairs={{0,8},{8,0},{16,24},{24,16},{1,9},{9,1},{17,25},{25,17},{2,10},{10... | collective-permute-start | bytes 589832 | tf_op jit(solution)/shard_map/ppermute | solution.py:286
  142.6 1.3 collective-permute-start.12
  143.9 5.3 %collective-permute-start.15 = (f32[136,128]{1,0:T(8,128)S(1)}, f32[136,128]{1,0:T(8,128)S(1)}, u32[]{:S(2)}, u32[]{:S(2)}) collective-permute-start(f32[136,128]{1,0:T(8,128)S(1)} %add.161), channel_id=1, source_target_pairs={{0,6},{1,7},{2,4},{3,5},{4,2},{5,3},{6,0},{7,1},{8,14},{9,15},{10,... | collective-permute-start | bytes 208904 | tf_op jit(solution)/shard_map/ppermute | solution.py:286
  146.5 4.3 %collective-permute-start.14 = (f32[136,128]{1,0:T(8,128)S(1)}, f32[136,128]{1,0:T(8,128)S(1)}, u32[]{:S(2)}, u32[]{:S(2)}) collective-permute-start(f32[136,128]{1,0:T(8,128)S(1)} %add.161), channel_id=1, source_target_pairs={{0,4},{1,5},{2,6},{3,7},{4,0},{5,1},{6,2},{7,3},{8,12},{9,13},{10,... | collective-permute-start | bytes 208904 | tf_op jit(solution)/shard_map/ppermute | solution.py:286
  147.0 4.3 %collective-permute-start.13 = (f32[136,128]{1,0:T(8,128)S(1)}, f32[136,128]{1,0:T(8,128)S(1)}, u32[]{:S(2)}, u32[]{:S(2)}) collective-permute-start(f32[136,128]{1,0:T(8,128)S(1)} %add.161), channel_id=1, source_target_pairs={{0,2},{1,3},{2,0},{3,1},{4,6},{5,7},{6,4},{7,5},{8,10},{9,11},{10,... | collective-permute-start | bytes 208904 | tf_op jit(solution)/shard_map/ppermute | solution.py:286
  151.3 6.3 %collective-permute-start.18 = (f32[136,128]{1,0:T(8,128)S(1)}, f32[136,128]{1,0:T(8,128)S(1)}, u32[]{:S(2)}, u32[]{:S(2)}) collective-permute-start(f32[136,128]{1,0:T(8,128)S(1)} %add_add_fusion.1), channel_id=1, source_target_pairs={{0,24},{8,16},{16,8},{24,0},{1,25},{9,17},{17,9},{25,1},{2,26},{10... | collective-permute-start | bytes 208904 | tf_op jit(solution)/shard_map/ppermute | solution.py:286
  154.9 5.3 %collective-permute-start.17 = (f32[136,128]{1,0:T(8,128)S(1)}, f32[136,128]{1,0:T(8,128)S(1)}, u32[]{:S(2)}, u32[]{:S(2)}) collective-permute-start(f32[136,128]{1,0:T(8,128)S(1)} %add_add_fusion.1), channel_id=1, source_target_pairs={{0,16},{8,24},{16,0},{24,8},{1,17},{9,25},{17,1},{25,9},{2,18},{10... | collective-permute-start | bytes 208904 | tf_op jit(solution)/shard_map/ppermute | solution.py:286
  154.9 5.7 %collective-permute-start.16 = (f32[136,128]{1,0:T(8,128)S(1)}, f32[136,128]{1,0:T(8,128)S(1)}, u32[]{:S(2)}, u32[]{:S(2)}) collective-permute-start(f32[136,128]{1,0:T(8,128)S(1)} %add_add_fusion.1), channel_id=1, source_target_pairs={{0,8},{8,0},{16,24},{24,16},{1,9},{9,1},{17,25},{25,17},{2,10},{10... | collective-permute-start | bytes 208904 | tf_op jit(solution)/shard_map/ppermute | solution.py:286
  160.6 1.3 collective-permute-start.19

commit v6 on v5

--- a/solution.py
+++ b/solution.py
@@ -10,7 +10,7 @@
 HIGHEST = lax.Precision.HIGHEST
 LANES = 128
 PANEL = 16
-BASIS_TILE = 512
+BASIS_TILE = 256
 VMEM_LIMIT = 24 * 1024 * 1024
 
 
@@ -206,8 +206,11 @@
 def finish_kernel(*refs, chunks, samples):
     own_ref, other_ref = refs[:2]
     highs, lows = refs[2 : 2 + chunks], refs[2 + chunks : 2 + 2 * chunks]
-    basis_ref, factor_ref, projected_ref, operator_ref = refs[2 + 2 * chunks : 6 + 2 * chunks]
-    pack_ref, work, inverse_ref, rows_ref, out_sem = refs[6 + 2 * chunks :]
+    basis_ref, *square_refs = refs[2 + 2 * chunks : 6 + 2 * chunks]
+    pack_ref, work, inverse_ref, rows_ref, out_sem, *own_squares, square_sem = refs[
+        6 + 2 * chunks :
+    ]
+    factor_ref, projected_ref, operator_ref = own_squares
     count = work.shape[0]
     half = count // 2
 
@@ -228,30 +231,36 @@
     factorize(work, factor_ref, inverse_ref)
 
     inverse = inverse_ref[...]
+    tail = [pack_ref[2 * half + r : 2 * half + r + 1, :] for r in (1, 2)]
+    column = jnp.sum(inverse * jnp.concatenate(tail, axis=1), axis=1, keepdims=True)
+    shifted = pltpu.roll(factor_ref[...], count - 1, 1)
+    projected = jnp.where(iota((count, count), 1) == count - 1, column, shifted)
+    projected_ref[...] = projected
+    operator_ref[...] = dot(projected, inverse, dims=((1,), (1,)), precision=HIGHEST)
+    stores = []
+    for index, (source, target) in enumerate(zip(own_squares, square_refs)):
+        copy = pltpu.make_async_copy(source, target, square_sem.at[index])
+        copy.start()
+        stores.append(copy)
+
     turned_high, turned_low = split(inverse.T)
-    stores = []
+    turned = jnp.concatenate([turned_high, turned_high, turned_low], axis=0)
+    tiles = 0
     done = 0
     for high_ref, low_ref in zip(highs, lows):
         for at in range(0, high_ref.shape[0], BASIS_TILE):
             size = min(BASIS_TILE, high_ref.shape[0] - at)
             high, low = high_ref[at : at + size, :], low_ref[at : at + size, :]
             tile = pl.ds(done, size)
-            rows_ref[tile, :] = (
-                dot(high, turned_high) + (dot(high, turned_low) + dot(low, turned_high))
-            )
+            rows_ref[tile, :] = dot(jnp.concatenate([high, low, high], axis=1), turned)
             copy = pltpu.make_async_copy(
-                rows_ref.at[tile], basis_ref.at[tile], out_sem.at[len(stores)]
+                rows_ref.at[tile], basis_ref.at[tile], out_sem.at[tiles]
             )
             copy.start()
             stores.append(copy)
+            tiles += 1
             done += size
 
-    tail = [pack_ref[2 * half + r : 2 * half + r + 1, :] for r in (1, 2)]
-    column = jnp.sum(inverse * jnp.concatenate(tail, axis=1), axis=1, keepdims=True)
-    shifted = pltpu.roll(factor_ref[...], count - 1, 1)
-    projected = jnp.where(iota((count, count), 1) == count - 1, column, shifted)
-    projected_ref[...] = projected
-    operator_ref[...] = dot(projected, inverse, dims=((1,), (1,)), precision=HIGHEST)
     for copy in stores:
         copy.wait()
 
@@ -268,13 +277,15 @@
         functools.partial(finish_kernel, chunks=chunks, samples=samples),
         out_shape=(jax.ShapeDtypeStruct((depth, count), jnp.float32), square, square, square),
         in_specs=[vmem] * (2 + 2 * chunks),
-        out_specs=(far, vmem, vmem, vmem),
+        out_specs=(far,) * 4,
         scratch_shapes=[
             pltpu.VMEM((2 * own.shape[0], LANES), jnp.float32),
             pltpu.VMEM((count, count), jnp.float32),
             pltpu.VMEM((count, count), jnp.float32),
             pltpu.VMEM((depth, count), jnp.float32),
             pltpu.SemaphoreType.DMA((tiles,)),
+            *[pltpu.VMEM((count, count), jnp.float32)] * 3,
+            pltpu.SemaphoreType.DMA((3,)),
         ],
         compiler_params=pltpu.CompilerParams(vmem_limit_bytes=VMEM_LIMIT),
         name="factor_and_basis",

time: 175 us -> 174 us (level)
  no operation moved by 1% of the time
where the time goes in v6:
time: 174 us
  starting transfers between devices  75.9 us (44%)
  waiting for transfers between devices  56.8 us (33%)
  Pallas kernels  21.4 us (12%)
  local copies, waits for them, and re-layouts  11.7 us (7%)
  matrix products  6.97 us (4%)
    ppermute x20, starting transfers between devices, swap(): return lax.ppermute(values, axis, [(i, i ^ step) for i in range(size)])  75.9 us
    ppermute x20, waiting for transfers between devices, swap(): return lax.ppermute(values, axis, [(i, i ^ step) for i in range(size)])  56.8 us
    pallas_call x1, Pallas kernels, finish(): pl.pallas_call(functools.partial(finish_kernel, chunks=chunks, samples=sa...  11.6 us
    dynamic_slice x5, local copies, waits for them, and re-layouts, cut(): lax.dynamic_slice(values, (0, target * depth + start), (own_cols, size))  9.75 us
    pallas_call x4, Pallas kernels, add_chunk(): pl.pallas_call(functools.partial(body, peers=peers), out_shape=sums + ter...  9.75 us
    dot_general x1, matrix products, shards(): jnp.dot(columns, last_snapshot, precision=HIGHEST, preferred_element_type...  6.97 us
  transfers between devices with their start and end apart: 20, of which 11 were waited for; matrix products, arithmetic and copies ran while one was open for 9% of the time, Pallas kernels for 5%

profile of v6, /device:TPU:0, one launch (start us, length us, event | category | flops | bytes accessed | tf_op | source)
XLA Modules:
  0.0 173.8 jit_solution(3418247974001761459)
XLA Ops:
  0.6 0.0 copy-start
  0.7 1.1 dynamic-slice_bitcast_fusion
  1.8 4.1 %collective-permute-start.10 = (f32[64,1024]{1,0:T(8,128)S(1)}, f32[64,1024]{1,0:T(8,128)S(1)}, u32[]{:S(2)}, u32[]{:S(2)}) collective-permute-start(f32[64,1024]{1,0:T(8,128)S(1)} %get-tuple-element.28), channel_id=1, source_target_pairs={{0,16},{8,24},{16,0},{24,8},{1,17},{9,25},{17,1},{25,9},{2,18},{10... | collective-permute-start | bytes 786440 | tf_op jit(solution)/shard_map/ppermute | solution.py:297
  5.9 1.3 collective-permute-start.11
  7.2 0.0 copy-done
  7.2 7.0 %convolution_bitcast_fusion = f32[64]{0:T(128)S(1)} fusion(f32[64,24576]{1,0:T(8,128)} %bitcast.14, f32[24576,1]{0,1:T(1,128)S(1)} %bitcast.12), kind=kOutput, calls=%fused_computation | convolution fusion | flops 18874368 | bytes 6390016 | tf_op jit(solution)/shard_map/dot_general | solution.py:339
  14.2 1.8 %constant_dynamic-slice_fusion = (f32[64,1024]{1,0:T(8,128)}, f32[64,1024]{1,0:T(8,128)S(1)}) fusion(f32[64,24576]{1,0:T(8,128)} %bitcast.15, s32[]{:T(128)S(6)} %select_n.66, s32[]{:T(128)S(6)} %select_n.65), kind=kLoop, calls=%fused_computation.5 | loop fusion | bytes 1048584 | tf_op jit(solution)/shard_map/dynamic_slice | solution.py:332
  16.0 0.2 collective-permute-start.9
  16.2 2.7 %constant_dynamic-slice_fusion.6 = (f32[64,2048]{1,0:T(8,128)}, f32[64,2048]{1,0:T(8,128)}, f32[64,2048]{1,0:T(8,128)}, f32[64,2048]{1,0:T(8,128)S(1)}) fusion(f32[64,24576]{1,0:T(8,128)} %bitcast.16, s32[]{:T(128)S(6)} %select_n.60, s32[]{:T(128)S(6)} %select_n.59, s32[]{:T(128)S(6)} %select_n.58, s32[]{:T(128)S(6)} %select_n.57), kind=kLoop, calls=%fused_computation.11 | loop fusion | bytes 4194320 | tf_op jit(solution)/shard_map/dynamic_slice | solution.py:332
  18.9 2.9 %collective-permute-start.5 = (f32[64,2048]{1,0:T(8,128)}, f32[64,2048]{1,0:T(8,128)}, u32[]{:S(2)}, u32[]{:S(2)}) collective-permute-start(f32[64,2048]{1,0:T(8,128)} %get-tuple-element.54), channel_id=1, source_target_pairs={{0,24},{8,16},{16,8},{24,0},{1,25},{9,17},{17,9},{25,1},{2,26},{10... | collective-permute-start | bytes 1572872 | tf_op jit(solution)/shard_map/ppermute | solution.py:297
  21.9 2.9 %constant_dynamic-slice_fusion.2 = (f32[64,2304]{1,0:T(8,128)}, f32[64,2304]{1,0:T(8,128)}, f32[64,2304]{1,0:T(8,128)}, f32[64,2304]{1,0:T(8,128)S(1)}) fusion(f32[64,24576]{1,0:T(8,128)} %bitcast.17, s32[]{:T(128)S(6)} %select_n.64, s32[]{:T(128)S(6)} %select_n.63, s32[]{:T(128)S(6)} %select_n.62, s32[]{:T(128)S(6)} %select_n.61), kind=kLoop, calls=%fused_computation.7 | loop fusion | bytes 4718608 | tf_op jit(solution)/shard_map/dynamic_slice | solution.py:332
  24.7 0.9 collective-permute-start.8
  25.6 0.0 collective-permute-done.10.refs_2_
  25.6 1.0 collective-permute-start.7
  26.6 0.0 collective-permute-done.11.refs_3_
  26.6 0.0 copy-start.1
  26.6 0.7 copy-done.1
  27.3 40.4 %collective-permute-start.6 = (f32[64,2304]{1,0:T(8,128)}, f32[64,2304]{1,0:T(8,128)S(1)}, u32[]{:S(2)}, u32[]{:S(2)}) collective-permute-start(f32[64,2304]{1,0:T(8,128)} %get-tuple-element.52), channel_id=1, source_target_pairs={{0,8},{8,0},{16,24},{24,16},{1,9},{9,1},{17,25},{25,17},{2,10},{10... | collective-permute-start | bytes 1769480 | tf_op jit(solution)/shard_map/ppermute | solution.py:297
  67.7 0.0 collective-permute-done.9.refs_1_
  67.7 1.3 collective-permute-start.4
  69.0 0.0 collective-permute-done.5.refs_3_
  69.0 9.3 %collective-permute-start.3 = (f32[64,2048]{1,0:T(8,128)}, f32[64,2048]{1,0:T(8,128)}, u32[]{:S(2)}, u32[]{:S(2)}) collective-permute-start(f32[64,2048]{1,0:T(8,128)} %get-tuple-element.56), channel_id=1, source_target_pairs={{0,8},{8,0},{16,24},{24,16},{1,9},{9,1},{17,25},{25,17},{2,10},{10... | collective-permute-start | bytes 1572872 | tf_op jit(solution)/shard_map/ppermute | solution.py:297
  78.3 0.3 dynamic_update_slice.3
  78.6 1.3 constant_dynamic-slice_fusion.10
  80.0 0.0 copy-start.2
  80.0 0.9 copy-done.2
  80.9 2.3 %gram_chunk.4 = (f32[3,128,128]{2,1,0:T(8,128)S(1)}, bf16[1024,256]{1,0:T(8,128)(2,1)S(1)}, bf16[1024,256]{1,0:T(8,128)(2,1)S(1)}) custom-call(f32[64,1024]{1,0:T(8,128)S(1)} %get-tuple-element.49.refs_0_, f32[64,1024]{1,0:T(8,128)} %collective-permute-done.9.refs_1_, f32[64,1024]{1,0:T(8,128)S(1)} %collective-permute-done.10.refs_2_, f32[64,1024]{1,0:T(8,128)S(1)} %copy-done.2), custom_call_target="tpu_custom_call" | custom-call | flops 805306368 | bytes 2097152 | tf_op jit(solution)/shard_map/gram_chunk/pallas_call | solution.py:111
  83.2 0.0 collective-permute-done.8.refs_3_
  83.2 2.9 %collective-permute-start.2 = (f32[64,768]{1,0:T(8,128)S(1)}, f32[64,768]{1,0:T(8,128)S(1)}, u32[]{:S(2)}, u32[]{:S(2)}) collective-permute-start(f32[64,768]{1,0:T(8,128)S(1)} %get-tuple-element.58), channel_id=1, source_target_pairs={{0,24},{8,16},{16,8},{24,0},{1,25},{9,17},{17,9},{25,1},{2,26},{10... | collective-permute-start | bytes 589832 | tf_op jit(solution)/shard_map/ppermute | solution.py:297
  86.1 32.3 %collective-permute-done.7.refs_2_ = f32[64,2304]{1,0:T(8,128)S(1)} collective-permute-done((f32[64,2304]{1,0:T(8,128)}, f32[64,2304]{1,0:T(8,128)S(1)}, u32[]{:S(2)}, u32[]{:S(2)}) %collective-permute-start.7) | collective-permute-done | bytes 589856 | tf_op jit(solution)/shard_map/ppermute | solution.py:297
  118.4 0.0 collective-permute-start.1
  118.4 0.0 collective-permute-done.6.refs_1_
  118.4 3.4 %collective-permute-start = (f32[64,768]{1,0:T(8,128)S(1)}, f32[64,768]{1,0:T(8,128)S(1)}, u32[]{:S(2)}, u32[]{:S(2)}) collective-permute-start(f32[64,768]{1,0:T(8,128)S(1)} %get-tuple-element.60), channel_id=1, source_target_pairs={{0,8},{8,0},{16,24},{24,16},{1,9},{9,1},{17,25},{25,17},{2,10},{10... | collective-permute-start | bytes 589832 | tf_op jit(solution)/shard_map/ppermute | solution.py:297
  121.8 2.6 %gram_chunk.5 = (f32[3,128,128]{2,1,0:T(8,128)S(1)}, bf16[2304,256]{1,0:T(8,128)(2,1)S(1)}, bf16[2304,256]{1,0:T(8,128)(2,1)S(1)}) custom-call(f32[64,2304]{1,0:T(8,128)S(1)} %get-tuple-element.53.refs_0_, f32[64,2304]{1,0:T(8,128)S(1)} %collective-permute-done.6.refs_1_, f32[64,2304]{1,0:T(8,128)S(1)} %collective-permute-done.7.refs_2_, ...), custom_call_target="tpu_custom_call" | custom-call | flops 1811939328 | bytes 4718592 | tf_op jit(solution)/shard_map/gram_chunk/pallas_call | solution.py:111
  124.4 9.6 %collective-permute-done.4.refs_2_ = f32[64,2048]{1,0:T(8,128)} collective-permute-done((f32[64,2048]{1,0:T(8,128)}, f32[64,2048]{1,0:T(8,128)}, u32[]{:S(2)}, u32[]{:S(2)}) %collective-permute-start.4) | collective-permute-done | bytes 524320 | tf_op jit(solution)/shard_map/ppermute | solution.py:297
  134.0 0.0 collective-permute-done.3.refs_1_
  134.0 3.7 %gram_chunk.6 = (f32[3,128,128]{2,1,0:T(8,128)S(1)}, bf16[2048,256]{1,0:T(8,128)(2,1)S(1)}, bf16[2048,256]{1,0:T(8,128)(2,1)S(1)}) custom-call(f32[64,2048]{1,0:T(8,128)S(1)} %get-tuple-element.57.refs_0_, f32[64,2048]{1,0:T(8,128)} %collective-permute-done.3.refs_1_, f32[64,2048]{1,0:T(8,128)} %collective-permute-done.4.refs_2_, ...), custom_call_target="tpu_custom_call" | custom-call | flops 1610612736 | bytes 4194304 | tf_op jit(solution)/shard_map/gram_chunk/pallas_call | solution.py:111
  137.7 0.0 collective-permute-done.2.refs_3_
  137.7 3.8 %collective-permute-done.1.refs_2_ = f32[64,768]{1,0:T(8,128)S(1)} collective-permute-done((f32[64,768]{1,0:T(8,128)S(1)}, f32[64,768]{1,0:T(8,128)S(1)}, u32[]{:S(2)}, u32[]{:S(2)}) %collective-permute-start.1) | collective-permute-done | bytes 196640 | tf_op jit(solution)/shard_map/ppermute | solution.py:297
  141.5 0.0 collective-permute-done.refs_1_
  141.5 1.1 gram_chunk.7
  142.6 0.1 collective-permute-start.12
  142.7 1.2 collective-permute-done.12
  143.9 2.6 %collective-permute-start.15 = (f32[136,128]{1,0:T(8,128)S(1)}, f32[136,128]{1,0:T(8,128)S(1)}, u32[]{:S(2)}, u32[]{:S(2)}) collective-permute-start(f32[136,128]{1,0:T(8,128)S(1)} %add.161), channel_id=1, source_target_pairs={{0,6},{1,7},{2,4},{3,5},{4,2},{5,3},{6,0},{7,1},{8,14},{9,15},{10,... | collective-permute-start | bytes 208904 | tf_op jit(solution)/shard_map/ppermute | solution.py:297
  146.5 0.5 collective-permute-start.14
  147.0 0.5 collective-permute-start.13
  147.5 1.7 %collective-permute-done.15 = f32[136,128]{1,0:T(8,128)S(1)} collective-permute-done((f32[136,128]{1,0:T(8,128)S(1)}, f32[136,128]{1,0:T(8,128)S(1)}, u32[]{:S(2)}, u32[]{:S(2)}) %collective-permute-start.15) | collective-permute-done | bytes 69664 | tf_op jit(solution)/shard_map/ppermute | solution.py:297
  149.2 1.6 collective-permute-done.14
  150.8 0.5 collective-permute-done.13
  151.3 3.6 %collective-permute-start.18 = (f32[136,128]{1,0:T(8,128)S(1)}, f32[136,128]{1,0:T(8,128)S(1)}, u32[]{:S(2)}, u32[]{:S(2)}) collective-permute-start(f32[136,128]{1,0:T(8,128)S(1)} %add_add_fusion.1), channel_id=1, source_target_pairs={{0,24},{8,16},{16,8},{24,0},{1,25},{9,17},{17,9},{25,1},{2,26},{10... | collective-permute-start | bytes 208904 | tf_op jit(solution)/shard_map/ppermute | solution.py:297
  154.9 0.0 collective-permute-start.17
  154.9 0.9 collective-permute-start.16
  155.8 1.8 %collective-permute-done.18 = f32[136,128]{1,0:T(8,128)S(1)} collective-permute-done((f32[136,128]{1,0:T(8,128)S(1)}, f32[136,128]{1,0:T(8,128)S(1)}, u32[]{:S(2)}, u32[]{:S(2)}) %collective-permute-start.18) | collective-permute-done | bytes 69664 | tf_op jit(solution)/shard_map/ppermute | solution.py:297
  157.6 2.5 %collective-permute-done.17 = f32[136,128]{1,0:T(8,128)S(1)} collective-permute-done((f32[136,128]{1,0:T(8,128)S(1)}, f32[136,128]{1,0:T(8,128)S(1)}, u32[]{:S(2)}, u32[]{:S(2)}) %collective-permute-start.17) | collective-permute-done | bytes 69664 | tf_op jit(solution)/shard_map/ppermute | solution.py:297
  160.1 0.5 collective-permute-done.16
  160.6 0.1 collective-permute-start.19
  160.7 1.2 collective-permute-done.19.refs_1_
  162.0 11.6 %factor_and_basis.1 = (f32[6144,256]{1,0:T(8,128)}, f32[256,256]{1,0:T(8,128)}, f32[256,256]{1,0:T(8,128)}, f32[256,256]{1,0:T(8,128)}) custom-call(f32[136,128]{1,0:T(8,128)S(1)} %add_add_fusion.refs_0_, f32[136,128]{1,0:T(8,128)S(1)} %collective-permute-done.19.refs_1_, bf16[1024,256]{1,0:T(8,128)(2,1)S(1)} %get-tuple-element.36.refs_2_, ...), custom_call_target="tpu_custom_call" | custom-call | tf_op jit(solution)/shard_map/factor_and_basis/pallas_call | solution.py:276
  (4 shorter events, 0.0 us)
Async XLA Ops:
  0.6 6.6 %copy-start = (f32[24576]{0:T(1024)S(1)}, f32[24576]{0:T(1024)}, u32[]{:S(2)}) copy-start(f32[24576]{0:T(1024)} %param.3) | copy-start | bytes 294916
  1.8 23.8 %collective-permute-start.10 = (f32[64,1024]{1,0:T(8,128)S(1)}, f32[64,1024]{1,0:T(8,128)S(1)}, u32[]{:S(2)}, u32[]{:S(2)}) collective-permute-start(f32[64,1024]{1,0:T(8,128)S(1)} %get-tuple-element.28), channel_id=1, source_target_pairs={{0,16},{8,24},{16,0},{24,8},{1,17},{9,25},{17,1},{25,9},{2,18},{10... | collective-permute-start | bytes 786440 | tf_op jit(solution)/shard_map/ppermute | solution.py:297
  5.9 20.8 %collective-permute-start.11 = (f32[64,1024]{1,0:T(8,128)S(1)}, f32[64,1024]{1,0:T(8,128)S(1)}, u32[]{:S(2)}, u32[]{:S(2)}) collective-permute-start(f32[64,1024]{1,0:T(8,128)S(1)} %get-tuple-element.29), channel_id=1, source_target_pairs={{0,24},{8,16},{16,8},{24,0},{1,25},{9,17},{17,9},{25,1},{2,26},{10... | collective-permute-start | bytes 786440 | tf_op jit(solution)/shard_map/ppermute | solution.py:297
  16.0 51.7 %collective-permute-start.9 = (f32[64,1024]{1,0:T(8,128)}, f32[64,1024]{1,0:T(8,128)}, u32[]{:S(2)}, u32[]{:S(2)}) collective-permute-start(f32[64,1024]{1,0:T(8,128)} %get-tuple-element.48), channel_id=1, source_target_pairs={{0,8},{8,0},{16,24},{24,16},{1,9},{9,1},{17,25},{25,17},{2,10},{10... | collective-permute-start | bytes 786440 | tf_op jit(solution)/shard_map/ppermute | solution.py:297
  18.9 50.1 %collective-permute-start.5 = (f32[64,2048]{1,0:T(8,128)}, f32[64,2048]{1,0:T(8,128)}, u32[]{:S(2)}, u32[]{:S(2)}) collective-permute-start(f32[64,2048]{1,0:T(8,128)} %get-tuple-element.54), channel_id=1, source_target_pairs={{0,24},{8,16},{16,8},{24,0},{1,25},{9,17},{17,9},{25,1},{2,26},{10... | collective-permute-start | bytes 1572872 | tf_op jit(solution)/shard_map/ppermute | solution.py:297
  24.7 58.5 %collective-permute-start.8 = (f32[64,2304]{1,0:T(8,128)}, f32[64,2304]{1,0:T(8,128)S(1)}, u32[]{:S(2)}, u32[]{:S(2)}) collective-permute-start(f32[64,2304]{1,0:T(8,128)} %get-tuple-element.50), channel_id=1, source_target_pairs={{0,24},{8,16},{16,8},{24,0},{1,25},{9,17},{17,9},{25,1},{2,26},{10... | collective-permute-start | bytes 1769480 | tf_op jit(solution)/shard_map/ppermute | solution.py:297
  25.6 92.8 %collective-permute-start.7 = (f32[64,2304]{1,0:T(8,128)}, f32[64,2304]{1,0:T(8,128)S(1)}, u32[]{:S(2)}, u32[]{:S(2)}) collective-permute-start(f32[64,2304]{1,0:T(8,128)} %get-tuple-element.51), channel_id=1, source_target_pairs={{0,16},{8,24},{16,0},{24,8},{1,17},{9,25},{17,1},{25,9},{2,18},{10... | collective-permute-start | bytes 1769480 | tf_op jit(solution)/shard_map/ppermute | solution.py:297
  26.6 0.7 copy-start.1
  27.3 91.1 %collective-permute-start.6 = (f32[64,2304]{1,0:T(8,128)}, f32[64,2304]{1,0:T(8,128)S(1)}, u32[]{:S(2)}, u32[]{:S(2)}) collective-permute-start(f32[64,2304]{1,0:T(8,128)} %get-tuple-element.52), channel_id=1, source_target_pairs={{0,8},{8,0},{16,24},{24,16},{1,9},{9,1},{17,25},{25,17},{2,10},{10... | collective-permute-start | bytes 1769480 | tf_op jit(solution)/shard_map/ppermute | solution.py:297
  67.7 66.3 %collective-permute-start.4 = (f32[64,2048]{1,0:T(8,128)}, f32[64,2048]{1,0:T(8,128)}, u32[]{:S(2)}, u32[]{:S(2)}) collective-permute-start(f32[64,2048]{1,0:T(8,128)} %get-tuple-element.55), channel_id=1, source_target_pairs={{0,16},{8,24},{16,0},{24,8},{1,17},{9,25},{17,1},{25,9},{2,18},{10... | collective-permute-start | bytes 1572872 | tf_op jit(solution)/shard_map/ppermute | solution.py:297
  69.0 64.9 %collective-permute-start.3 = (f32[64,2048]{1,0:T(8,128)}, f32[64,2048]{1,0:T(8,128)}, u32[]{:S(2)}, u32[]{:S(2)}) collective-permute-start(f32[64,2048]{1,0:T(8,128)} %get-tuple-element.56), channel_id=1, source_target_pairs={{0,8},{8,0},{16,24},{24,16},{1,9},{9,1},{17,25},{25,17},{2,10},{10... | collective-permute-start | bytes 1572872 | tf_op jit(solution)/shard_map/ppermute | solution.py:297
  80.0 1.0 copy-start.2
  83.2 54.5 %collective-permute-start.2 = (f32[64,768]{1,0:T(8,128)S(1)}, f32[64,768]{1,0:T(8,128)S(1)}, u32[]{:S(2)}, u32[]{:S(2)}) collective-permute-start(f32[64,768]{1,0:T(8,128)S(1)} %get-tuple-element.58), channel_id=1, source_target_pairs={{0,24},{8,16},{16,8},{24,0},{1,25},{9,17},{17,9},{25,1},{2,26},{10... | collective-permute-start | bytes 589832 | tf_op jit(solution)/shard_map/ppermute | solution.py:297
  118.4 23.1 %collective-permute-start.1 = (f32[64,768]{1,0:T(8,128)S(1)}, f32[64,768]{1,0:T(8,128)S(1)}, u32[]{:S(2)}, u32[]{:S(2)}) collective-permute-start(f32[64,768]{1,0:T(8,128)S(1)} %get-tuple-element.59), channel_id=1, source_target_pairs={{0,16},{8,24},{16,0},{24,8},{1,17},{9,25},{17,1},{25,9},{2,18},{10... | collective-permute-start | bytes 589832 | tf_op jit(solution)/shard_map/ppermute | solution.py:297
  118.4 23.1 %collective-permute-start = (f32[64,768]{1,0:T(8,128)S(1)}, f32[64,768]{1,0:T(8,128)S(1)}, u32[]{:S(2)}, u32[]{:S(2)}) collective-permute-start(f32[64,768]{1,0:T(8,128)S(1)} %get-tuple-element.60), channel_id=1, source_target_pairs={{0,8},{8,0},{16,24},{24,16},{1,9},{9,1},{17,25},{25,17},{2,10},{10... | collective-permute-start | bytes 589832 | tf_op jit(solution)/shard_map/ppermute | solution.py:297
  142.6 1.3 collective-permute-start.12
  143.9 5.3 %collective-permute-start.15 = (f32[136,128]{1,0:T(8,128)S(1)}, f32[136,128]{1,0:T(8,128)S(1)}, u32[]{:S(2)}, u32[]{:S(2)}) collective-permute-start(f32[136,128]{1,0:T(8,128)S(1)} %add.161), channel_id=1, source_target_pairs={{0,6},{1,7},{2,4},{3,5},{4,2},{5,3},{6,0},{7,1},{8,14},{9,15},{10,... | collective-permute-start | bytes 208904 | tf_op jit(solution)/shard_map/ppermute | solution.py:297
  146.5 4.3 %collective-permute-start.14 = (f32[136,128]{1,0:T(8,128)S(1)}, f32[136,128]{1,0:T(8,128)S(1)}, u32[]{:S(2)}, u32[]{:S(2)}) collective-permute-start(f32[136,128]{1,0:T(8,128)S(1)} %add.161), channel_id=1, source_target_pairs={{0,4},{1,5},{2,6},{3,7},{4,0},{5,1},{6,2},{7,3},{8,12},{9,13},{10,... | collective-permute-start | bytes 208904 | tf_op jit(solution)/shard_map/ppermute | solution.py:297
  147.0 4.3 %collective-permute-start.13 = (f32[136,128]{1,0:T(8,128)S(1)}, f32[136,128]{1,0:T(8,128)S(1)}, u32[]{:S(2)}, u32[]{:S(2)}) collective-permute-start(f32[136,128]{1,0:T(8,128)S(1)} %add.161), channel_id=1, source_target_pairs={{0,2},{1,3},{2,0},{3,1},{4,6},{5,7},{6,4},{7,5},{8,10},{9,11},{10,... | collective-permute-start | bytes 208904 | tf_op jit(solution)/shard_map/ppermute | solution.py:297
  151.3 6.3 %collective-permute-start.18 = (f32[136,128]{1,0:T(8,128)S(1)}, f32[136,128]{1,0:T(8,128)S(1)}, u32[]{:S(2)}, u32[]{:S(2)}) collective-permute-start(f32[136,128]{1,0:T(8,128)S(1)} %add_add_fusion.1), channel_id=1, source_target_pairs={{0,24},{8,16},{16,8},{24,0},{1,25},{9,17},{17,9},{25,1},{2,26},{10... | collective-permute-start | bytes 208904 | tf_op jit(solution)/shard_map/ppermute | solution.py:297
  154.9 5.3 %collective-permute-start.17 = (f32[136,128]{1,0:T(8,128)S(1)}, f32[136,128]{1,0:T(8,128)S(1)}, u32[]{:S(2)}, u32[]{:S(2)}) collective-permute-start(f32[136,128]{1,0:T(8,128)S(1)} %add_add_fusion.1), channel_id=1, source_target_pairs={{0,16},{8,24},{16,0},{24,8},{1,17},{9,25},{17,1},{25,9},{2,18},{10... | collective-permute-start | bytes 208904 | tf_op jit(solution)/shard_map/ppermute | solution.py:297
  154.9 5.7 %collective-permute-start.16 = (f32[136,128]{1,0:T(8,128)S(1)}, f32[136,128]{1,0:T(8,128)S(1)}, u32[]{:S(2)}, u32[]{:S(2)}) collective-permute-start(f32[136,128]{1,0:T(8,128)S(1)} %add_add_fusion.1), channel_id=1, source_target_pairs={{0,8},{8,0},{16,24},{24,16},{1,9},{9,1},{17,25},{25,17},{2,10},{10... | collective-permute-start | bytes 208904 | tf_op jit(solution)/shard_map/ppermute | solution.py:297
  160.6 1.3 collective-permute-start.19

commit v7 on v6

--- a/solution.py
+++ b/solution.py
@@ -231,23 +231,23 @@
     factorize(work, factor_ref, inverse_ref)
 
     inverse = inverse_ref[...]
-    tail = [pack_ref[2 * half + r : 2 * half + r + 1, :] for r in (1, 2)]
-    column = jnp.sum(inverse * jnp.concatenate(tail, axis=1), axis=1, keepdims=True)
-    shifted = pltpu.roll(factor_ref[...], count - 1, 1)
-    projected = jnp.where(iota((count, count), 1) == count - 1, column, shifted)
-    projected_ref[...] = projected
-    operator_ref[...] = dot(projected, inverse, dims=((1,), (1,)), precision=HIGHEST)
     stores = []
-    for index, (source, target) in enumerate(zip(own_squares, square_refs)):
-        copy = pltpu.make_async_copy(source, target, square_sem.at[index])
-        copy.start()
-        stores.append(copy)
-
     turned_high, turned_low = split(inverse.T)
     turned = jnp.concatenate([turned_high, turned_high, turned_low], axis=0)
     tiles = 0
     done = 0
-    for high_ref, low_ref in zip(highs, lows):
+    for chunk, (high_ref, low_ref) in enumerate(zip(highs, lows)):
+        if chunk == chunks - 1:
+            tail = [pack_ref[2 * half + r : 2 * half + r + 1, :] for r in (1, 2)]
+            column = jnp.sum(inverse * jnp.concatenate(tail, axis=1), axis=1, keepdims=True)
+            shifted = pltpu.roll(factor_ref[...], count - 1, 1)
+            projected = jnp.where(iota((count, count), 1) == count - 1, column, shifted)
+            projected_ref[...] = projected
+            operator_ref[...] = dot(projected, inverse, dims=((1,), (1,)), precision=HIGHEST)
+            for index, (source, target) in enumerate(zip(own_squares, square_refs)):
+                copy = pltpu.make_async_copy(source, target, square_sem.at[index])
+                copy.start()
+                stores.append(copy)
         for at in range(0, high_ref.shape[0], BASIS_TILE):
             size = min(BASIS_TILE, high_ref.shape[0] - at)
             high, low = high_ref[at : at + size, :], low_ref[at : at + size, :]

time: 174 us -> 174 us (level)
  no operation moved by 1% of the time
where the time goes in v7:
time: 174 us
  starting transfers between devices  75.9 us (44%)
  waiting for transfers between devices  56.8 us (33%)
  Pallas kernels  21.3 us (12%)
  local copies, waits for them, and re-layouts  11.7 us (7%)
  matrix products  6.97 us (4%)
    ppermute x20, starting transfers between devices, swap(): return lax.ppermute(values, axis, [(i, i ^ step) for i in range(size)])  75.9 us
    ppermute x20, waiting for transfers between devices, swap(): return lax.ppermute(values, axis, [(i, i ^ step) for i in range(size)])  56.8 us
    pallas_call x1, Pallas kernels, finish(): pl.pallas_call(functools.partial(finish_kernel, chunks=chunks, samples=sa...  11.6 us
    dynamic_slice x5, local copies, waits for them, and re-layouts, cut(): lax.dynamic_slice(values, (0, target * depth + start), (own_cols, size))  9.75 us
    pallas_call x4, Pallas kernels, add_chunk(): pl.pallas_call(functools.partial(body, peers=peers), out_shape=sums + ter...  9.75 us
    dot_general x1, matrix products, shards(): jnp.dot(columns, last_snapshot, precision=HIGHEST, preferred_element_type...  6.97 us
  transfers between devices with their start and end apart: 20, of which 11 were waited for; matrix products, arithmetic and copies ran while one was open for 9% of the time, Pallas kernels for 5%

profile of v7, /device:TPU:0, one launch (start us, length us, event | category | flops | bytes accessed | tf_op | source)
XLA Modules:
  0.0 173.7 jit_solution(866124234271554461)
XLA Ops:
  0.6 0.0 copy-start
  0.7 1.1 dynamic-slice_bitcast_fusion
  1.8 4.1 %collective-permute-start.10 = (f32[64,1024]{1,0:T(8,128)S(1)}, f32[64,1024]{1,0:T(8,128)S(1)}, u32[]{:S(2)}, u32[]{:S(2)}) collective-permute-start(f32[64,1024]{1,0:T(8,128)S(1)} %get-tuple-element.28), channel_id=1, source_target_pairs={{0,16},{8,24},{16,0},{24,8},{1,17},{9,25},{17,1},{25,9},{2,18},{10... | collective-permute-start | bytes 786440 | tf_op jit(solution)/shard_map/ppermute | solution.py:297
  5.9 1.3 collective-permute-start.11
  7.2 0.0 copy-done
  7.2 7.0 %convolution_bitcast_fusion = f32[64]{0:T(128)S(1)} fusion(f32[64,24576]{1,0:T(8,128)} %bitcast.14, f32[24576,1]{0,1:T(1,128)S(1)} %bitcast.12), kind=kOutput, calls=%fused_computation | convolution fusion | flops 18874368 | bytes 6390016 | tf_op jit(solution)/shard_map/dot_general | solution.py:339
  14.2 1.8 %constant_dynamic-slice_fusion = (f32[64,1024]{1,0:T(8,128)}, f32[64,1024]{1,0:T(8,128)S(1)}) fusion(f32[64,24576]{1,0:T(8,128)} %bitcast.15, s32[]{:T(128)S(6)} %select_n.66, s32[]{:T(128)S(6)} %select_n.65), kind=kLoop, calls=%fused_computation.5 | loop fusion | bytes 1048584 | tf_op jit(solution)/shard_map/dynamic_slice | solution.py:332
  16.0 0.2 collective-permute-start.9
  16.2 2.7 %constant_dynamic-slice_fusion.6 = (f32[64,2048]{1,0:T(8,128)}, f32[64,2048]{1,0:T(8,128)}, f32[64,2048]{1,0:T(8,128)}, f32[64,2048]{1,0:T(8,128)S(1)}) fusion(f32[64,24576]{1,0:T(8,128)} %bitcast.16, s32[]{:T(128)S(6)} %select_n.60, s32[]{:T(128)S(6)} %select_n.59, s32[]{:T(128)S(6)} %select_n.58, s32[]{:T(128)S(6)} %select_n.57), kind=kLoop, calls=%fused_computation.11 | loop fusion | bytes 4194320 | tf_op jit(solution)/shard_map/dynamic_slice | solution.py:332
  18.9 2.9 %collective-permute-start.5 = (f32[64,2048]{1,0:T(8,128)}, f32[64,2048]{1,0:T(8,128)}, u32[]{:S(2)}, u32[]{:S(2)}) collective-permute-start(f32[64,2048]{1,0:T(8,128)} %get-tuple-element.54), channel_id=1, source_target_pairs={{0,24},{8,16},{16,8},{24,0},{1,25},{9,17},{17,9},{25,1},{2,26},{10... | collective-permute-start | bytes 1572872 | tf_op jit(solution)/shard_map/ppermute | solution.py:297
  21.9 2.9 %constant_dynamic-slice_fusion.2 = (f32[64,2304]{1,0:T(8,128)}, f32[64,2304]{1,0:T(8,128)}, f32[64,2304]{1,0:T(8,128)}, f32[64,2304]{1,0:T(8,128)S(1)}) fusion(f32[64,24576]{1,0:T(8,128)} %bitcast.17, s32[]{:T(128)S(6)} %select_n.64, s32[]{:T(128)S(6)} %select_n.63, s32[]{:T(128)S(6)} %select_n.62, s32[]{:T(128)S(6)} %select_n.61), kind=kLoop, calls=%fused_computation.7 | loop fusion | bytes 4718608 | tf_op jit(solution)/shard_map/dynamic_slice | solution.py:332
  24.7 0.9 collective-permute-start.8
  25.6 0.0 collective-permute-done.10.refs_2_
  25.6 1.0 collective-permute-start.7
  26.6 0.0 collective-permute-done.11.refs_3_
  26.6 0.0 copy-start.1
  26.6 0.7 copy-done.1
  27.3 40.4 %collective-permute-start.6 = (f32[64,2304]{1,0:T(8,128)}, f32[64,2304]{1,0:T(8,128)S(1)}, u32[]{:S(2)}, u32[]{:S(2)}) collective-permute-start(f32[64,2304]{1,0:T(8,128)} %get-tuple-element.52), channel_id=1, source_target_pairs={{0,8},{8,0},{16,24},{24,16},{1,9},{9,1},{17,25},{25,17},{2,10},{10... | collective-permute-start | bytes 1769480 | tf_op jit(solution)/shard_map/ppermute | solution.py:297
  67.7 0.0 collective-permute-done.9.refs_1_
  67.7 1.3 collective-permute-start.4
  69.0 0.0 collective-permute-done.5.refs_3_
  69.0 9.3 %collective-permute-start.3 = (f32[64,2048]{1,0:T(8,128)}, f32[64,2048]{1,0:T(8,128)}, u32[]{:S(2)}, u32[]{:S(2)}) collective-permute-start(f32[64,2048]{1,0:T(8,128)} %get-tuple-element.56), channel_id=1, source_target_pairs={{0,8},{8,0},{16,24},{24,16},{1,9},{9,1},{17,25},{25,17},{2,10},{10... | collective-permute-start | bytes 1572872 | tf_op jit(solution)/shard_map/ppermute | solution.py:297
  78.3 0.3 dynamic_update_slice.3
  78.6 1.3 constant_dynamic-slice_fusion.10
  80.0 0.0 copy-start.2
  80.0 0.9 copy-done.2
  80.9 2.3 %gram_chunk.4 = (f32[3,128,128]{2,1,0:T(8,128)S(1)}, bf16[1024,256]{1,0:T(8,128)(2,1)S(1)}, bf16[1024,256]{1,0:T(8,128)(2,1)S(1)}) custom-call(f32[64,1024]{1,0:T(8,128)S(1)} %get-tuple-element.49.refs_0_, f32[64,1024]{1,0:T(8,128)} %collective-permute-done.9.refs_1_, f32[64,1024]{1,0:T(8,128)S(1)} %collective-permute-done.10.refs_2_, f32[64,1024]{1,0:T(8,128)S(1)} %copy-done.2), custom_call_target="tpu_custom_call" | custom-call | flops 805306368 | bytes 2097152 | tf_op jit(solution)/shard_map/gram_chunk/pallas_call | solution.py:111
  83.2 0.0 collective-permute-done.8.refs_3_
  83.2 2.9 %collective-permute-start.2 = (f32[64,768]{1,0:T(8,128)S(1)}, f32[64,768]{1,0:T(8,128)S(1)}, u32[]{:S(2)}, u32[]{:S(2)}) collective-permute-start(f32[64,768]{1,0:T(8,128)S(1)} %get-tuple-element.58), channel_id=1, source_target_pairs={{0,24},{8,16},{16,8},{24,0},{1,25},{9,17},{17,9},{25,1},{2,26},{10... | collective-permute-start | bytes 589832 | tf_op jit(solution)/shard_map/ppermute | solution.py:297
  86.1 32.3 %collective-permute-done.7.refs_2_ = f32[64,2304]{1,0:T(8,128)S(1)} collective-permute-done((f32[64,2304]{1,0:T(8,128)}, f32[64,2304]{1,0:T(8,128)S(1)}, u32[]{:S(2)}, u32[]{:S(2)}) %collective-permute-start.7) | collective-permute-done | bytes 589856 | tf_op jit(solution)/shard_map/ppermute | solution.py:297
  118.4 0.0 collective-permute-start.1
  118.4 0.0 collective-permute-done.6.refs_1_
  118.4 3.4 %collective-permute-start = (f32[64,768]{1,0:T(8,128)S(1)}, f32[64,768]{1,0:T(8,128)S(1)}, u32[]{:S(2)}, u32[]{:S(2)}) collective-permute-start(f32[64,768]{1,0:T(8,128)S(1)} %get-tuple-element.60), channel_id=1, source_target_pairs={{0,8},{8,0},{16,24},{24,16},{1,9},{9,1},{17,25},{25,17},{2,10},{10... | collective-permute-start | bytes 589832 | tf_op jit(solution)/shard_map/ppermute | solution.py:297
  121.8 2.6 %gram_chunk.5 = (f32[3,128,128]{2,1,0:T(8,128)S(1)}, bf16[2304,256]{1,0:T(8,128)(2,1)S(1)}, bf16[2304,256]{1,0:T(8,128)(2,1)S(1)}) custom-call(f32[64,2304]{1,0:T(8,128)S(1)} %get-tuple-element.53.refs_0_, f32[64,2304]{1,0:T(8,128)S(1)} %collective-permute-done.6.refs_1_, f32[64,2304]{1,0:T(8,128)S(1)} %collective-permute-done.7.refs_2_, ...), custom_call_target="tpu_custom_call" | custom-call | flops 1811939328 | bytes 4718592 | tf_op jit(solution)/shard_map/gram_chunk/pallas_call | solution.py:111
  124.4 9.6 %collective-permute-done.4.refs_2_ = f32[64,2048]{1,0:T(8,128)} collective-permute-done((f32[64,2048]{1,0:T(8,128)}, f32[64,2048]{1,0:T(8,128)}, u32[]{:S(2)}, u32[]{:S(2)}) %collective-permute-start.4) | collective-permute-done | bytes 524320 | tf_op jit(solution)/shard_map/ppermute | solution.py:297
  134.0 0.0 collective-permute-done.3.refs_1_
  134.0 3.7 %gram_chunk.6 = (f32[3,128,128]{2,1,0:T(8,128)S(1)}, bf16[2048,256]{1,0:T(8,128)(2,1)S(1)}, bf16[2048,256]{1,0:T(8,128)(2,1)S(1)}) custom-call(f32[64,2048]{1,0:T(8,128)S(1)} %get-tuple-element.57.refs_0_, f32[64,2048]{1,0:T(8,128)} %collective-permute-done.3.refs_1_, f32[64,2048]{1,0:T(8,128)} %collective-permute-done.4.refs_2_, ...), custom_call_target="tpu_custom_call" | custom-call | flops 1610612736 | bytes 4194304 | tf_op jit(solution)/shard_map/gram_chunk/pallas_call | solution.py:111
  137.7 0.0 collective-permute-done.2.refs_3_
  137.7 3.8 %collective-permute-done.1.refs_2_ = f32[64,768]{1,0:T(8,128)S(1)} collective-permute-done((f32[64,768]{1,0:T(8,128)S(1)}, f32[64,768]{1,0:T(8,128)S(1)}, u32[]{:S(2)}, u32[]{:S(2)}) %collective-permute-start.1) | collective-permute-done | bytes 196640 | tf_op jit(solution)/shard_map/ppermute | solution.py:297
  141.5 0.0 collective-permute-done.refs_1_
  141.5 1.1 gram_chunk.7
  142.6 0.1 collective-permute-start.12
  142.7 1.2 collective-permute-done.12
  143.9 2.6 %collective-permute-start.15 = (f32[136,128]{1,0:T(8,128)S(1)}, f32[136,128]{1,0:T(8,128)S(1)}, u32[]{:S(2)}, u32[]{:S(2)}) collective-permute-start(f32[136,128]{1,0:T(8,128)S(1)} %add.161), channel_id=1, source_target_pairs={{0,6},{1,7},{2,4},{3,5},{4,2},{5,3},{6,0},{7,1},{8,14},{9,15},{10,... | collective-permute-start | bytes 208904 | tf_op jit(solution)/shard_map/ppermute | solution.py:297
  146.5 0.5 collective-permute-start.14
  147.0 0.5 collective-permute-start.13
  147.5 1.7 %collective-permute-done.15 = f32[136,128]{1,0:T(8,128)S(1)} collective-permute-done((f32[136,128]{1,0:T(8,128)S(1)}, f32[136,128]{1,0:T(8,128)S(1)}, u32[]{:S(2)}, u32[]{:S(2)}) %collective-permute-start.15) | collective-permute-done | bytes 69664 | tf_op jit(solution)/shard_map/ppermute | solution.py:297
  149.2 1.6 collective-permute-done.14
  150.8 0.5 collective-permute-done.13
  151.3 3.6 %collective-permute-start.18 = (f32[136,128]{1,0:T(8,128)S(1)}, f32[136,128]{1,0:T(8,128)S(1)}, u32[]{:S(2)}, u32[]{:S(2)}) collective-permute-start(f32[136,128]{1,0:T(8,128)S(1)} %add_add_fusion.1), channel_id=1, source_target_pairs={{0,24},{8,16},{16,8},{24,0},{1,25},{9,17},{17,9},{25,1},{2,26},{10... | collective-permute-start | bytes 208904 | tf_op jit(solution)/shard_map/ppermute | solution.py:297
  154.9 0.0 collective-permute-start.17
  154.9 0.9 collective-permute-start.16
  155.8 1.8 %collective-permute-done.18 = f32[136,128]{1,0:T(8,128)S(1)} collective-permute-done((f32[136,128]{1,0:T(8,128)S(1)}, f32[136,128]{1,0:T(8,128)S(1)}, u32[]{:S(2)}, u32[]{:S(2)}) %collective-permute-start.18) | collective-permute-done | bytes 69664 | tf_op jit(solution)/shard_map/ppermute | solution.py:297
  157.6 2.5 %collective-permute-done.17 = f32[136,128]{1,0:T(8,128)S(1)} collective-permute-done((f32[136,128]{1,0:T(8,128)S(1)}, f32[136,128]{1,0:T(8,128)S(1)}, u32[]{:S(2)}, u32[]{:S(2)}) %collective-permute-start.17) | collective-permute-done | bytes 69664 | tf_op jit(solution)/shard_map/ppermute | solution.py:297
  160.1 0.5 collective-permute-done.16
  160.6 0.1 collective-permute-start.19
  160.7 1.2 collective-permute-done.19.refs_1_
  162.0 11.6 %factor_and_basis.1 = (f32[6144,256]{1,0:T(8,128)}, f32[256,256]{1,0:T(8,128)}, f32[256,256]{1,0:T(8,128)}, f32[256,256]{1,0:T(8,128)}) custom-call(f32[136,128]{1,0:T(8,128)S(1)} %add_add_fusion.refs_0_, f32[136,128]{1,0:T(8,128)S(1)} %collective-permute-done.19.refs_1_, bf16[1024,256]{1,0:T(8,128)(2,1)S(1)} %get-tuple-element.36.refs_2_, ...), custom_call_target="tpu_custom_call" | custom-call | tf_op jit(solution)/shard_map/factor_and_basis/pallas_call | solution.py:276
  (4 shorter events, 0.0 us)
Async XLA Ops:
  0.6 6.6 %copy-start = (f32[24576]{0:T(1024)S(1)}, f32[24576]{0:T(1024)}, u32[]{:S(2)}) copy-start(f32[24576]{0:T(1024)} %param.3) | copy-start | bytes 294916
  1.8 23.8 %collective-permute-start.10 = (f32[64,1024]{1,0:T(8,128)S(1)}, f32[64,1024]{1,0:T(8,128)S(1)}, u32[]{:S(2)}, u32[]{:S(2)}) collective-permute-start(f32[64,1024]{1,0:T(8,128)S(1)} %get-tuple-element.28), channel_id=1, source_target_pairs={{0,16},{8,24},{16,0},{24,8},{1,17},{9,25},{17,1},{25,9},{2,18},{10... | collective-permute-start | bytes 786440 | tf_op jit(solution)/shard_map/ppermute | solution.py:297
  5.9 20.8 %collective-permute-start.11 = (f32[64,1024]{1,0:T(8,128)S(1)}, f32[64,1024]{1,0:T(8,128)S(1)}, u32[]{:S(2)}, u32[]{:S(2)}) collective-permute-start(f32[64,1024]{1,0:T(8,128)S(1)} %get-tuple-element.29), channel_id=1, source_target_pairs={{0,24},{8,16},{16,8},{24,0},{1,25},{9,17},{17,9},{25,1},{2,26},{10... | collective-permute-start | bytes 786440 | tf_op jit(solution)/shard_map/ppermute | solution.py:297
  16.0 51.7 %collective-permute-start.9 = (f32[64,1024]{1,0:T(8,128)}, f32[64,1024]{1,0:T(8,128)}, u32[]{:S(2)}, u32[]{:S(2)}) collective-permute-start(f32[64,1024]{1,0:T(8,128)} %get-tuple-element.48), channel_id=1, source_target_pairs={{0,8},{8,0},{16,24},{24,16},{1,9},{9,1},{17,25},{25,17},{2,10},{10... | collective-permute-start | bytes 786440 | tf_op jit(solution)/shard_map/ppermute | solution.py:297
  18.9 50.1 %collective-permute-start.5 = (f32[64,2048]{1,0:T(8,128)}, f32[64,2048]{1,0:T(8,128)}, u32[]{:S(2)}, u32[]{:S(2)}) collective-permute-start(f32[64,2048]{1,0:T(8,128)} %get-tuple-element.54), channel_id=1, source_target_pairs={{0,24},{8,16},{16,8},{24,0},{1,25},{9,17},{17,9},{25,1},{2,26},{10... | collective-permute-start | bytes 1572872 | tf_op jit(solution)/shard_map/ppermute | solution.py:297
  24.7 58.5 %collective-permute-start.8 = (f32[64,2304]{1,0:T(8,128)}, f32[64,2304]{1,0:T(8,128)S(1)}, u32[]{:S(2)}, u32[]{:S(2)}) collective-permute-start(f32[64,2304]{1,0:T(8,128)} %get-tuple-element.50), channel_id=1, source_target_pairs={{0,24},{8,16},{16,8},{24,0},{1,25},{9,17},{17,9},{25,1},{2,26},{10... | collective-permute-start | bytes 1769480 | tf_op jit(solution)/shard_map/ppermute | solution.py:297
  25.6 92.8 %collective-permute-start.7 = (f32[64,2304]{1,0:T(8,128)}, f32[64,2304]{1,0:T(8,128)S(1)}, u32[]{:S(2)}, u32[]{:S(2)}) collective-permute-start(f32[64,2304]{1,0:T(8,128)} %get-tuple-element.51), channel_id=1, source_target_pairs={{0,16},{8,24},{16,0},{24,8},{1,17},{9,25},{17,1},{25,9},{2,18},{10... | collective-permute-start | bytes 1769480 | tf_op jit(solution)/shard_map/ppermute | solution.py:297
  26.6 0.7 copy-start.1
  27.3 91.1 %collective-permute-start.6 = (f32[64,2304]{1,0:T(8,128)}, f32[64,2304]{1,0:T(8,128)S(1)}, u32[]{:S(2)}, u32[]{:S(2)}) collective-permute-start(f32[64,2304]{1,0:T(8,128)} %get-tuple-element.52), channel_id=1, source_target_pairs={{0,8},{8,0},{16,24},{24,16},{1,9},{9,1},{17,25},{25,17},{2,10},{10... | collective-permute-start | bytes 1769480 | tf_op jit(solution)/shard_map/ppermute | solution.py:297
  67.7 66.3 %collective-permute-start.4 = (f32[64,2048]{1,0:T(8,128)}, f32[64,2048]{1,0:T(8,128)}, u32[]{:S(2)}, u32[]{:S(2)}) collective-permute-start(f32[64,2048]{1,0:T(8,128)} %get-tuple-element.55), channel_id=1, source_target_pairs={{0,16},{8,24},{16,0},{24,8},{1,17},{9,25},{17,1},{25,9},{2,18},{10... | collective-permute-start | bytes 1572872 | tf_op jit(solution)/shard_map/ppermute | solution.py:297
  69.0 64.9 %collective-permute-start.3 = (f32[64,2048]{1,0:T(8,128)}, f32[64,2048]{1,0:T(8,128)}, u32[]{:S(2)}, u32[]{:S(2)}) collective-permute-start(f32[64,2048]{1,0:T(8,128)} %get-tuple-element.56), channel_id=1, source_target_pairs={{0,8},{8,0},{16,24},{24,16},{1,9},{9,1},{17,25},{25,17},{2,10},{10... | collective-permute-start | bytes 1572872 | tf_op jit(solution)/shard_map/ppermute | solution.py:297
  80.0 1.0 copy-start.2
  83.2 54.5 %collective-permute-start.2 = (f32[64,768]{1,0:T(8,128)S(1)}, f32[64,768]{1,0:T(8,128)S(1)}, u32[]{:S(2)}, u32[]{:S(2)}) collective-permute-start(f32[64,768]{1,0:T(8,128)S(1)} %get-tuple-element.58), channel_id=1, source_target_pairs={{0,24},{8,16},{16,8},{24,0},{1,25},{9,17},{17,9},{25,1},{2,26},{10... | collective-permute-start | bytes 589832 | tf_op jit(solution)/shard_map/ppermute | solution.py:297
  118.4 23.1 %collective-permute-start.1 = (f32[64,768]{1,0:T(8,128)S(1)}, f32[64,768]{1,0:T(8,128)S(1)}, u32[]{:S(2)}, u32[]{:S(2)}) collective-permute-start(f32[64,768]{1,0:T(8,128)S(1)} %get-tuple-element.59), channel_id=1, source_target_pairs={{0,16},{8,24},{16,0},{24,8},{1,17},{9,25},{17,1},{25,9},{2,18},{10... | collective-permute-start | bytes 589832 | tf_op jit(solution)/shard_map/ppermute | solution.py:297
  118.4 23.1 %collective-permute-start = (f32[64,768]{1,0:T(8,128)S(1)}, f32[64,768]{1,0:T(8,128)S(1)}, u32[]{:S(2)}, u32[]{:S(2)}) collective-permute-start(f32[64,768]{1,0:T(8,128)S(1)} %get-tuple-element.60), channel_id=1, source_target_pairs={{0,8},{8,0},{16,24},{24,16},{1,9},{9,1},{17,25},{25,17},{2,10},{10... | collective-permute-start | bytes 589832 | tf_op jit(solution)/shard_map/ppermute | solution.py:297
  142.6 1.3 collective-permute-start.12
  143.9 5.3 %collective-permute-start.15 = (f32[136,128]{1,0:T(8,128)S(1)}, f32[136,128]{1,0:T(8,128)S(1)}, u32[]{:S(2)}, u32[]{:S(2)}) collective-permute-start(f32[136,128]{1,0:T(8,128)S(1)} %add.161), channel_id=1, source_target_pairs={{0,6},{1,7},{2,4},{3,5},{4,2},{5,3},{6,0},{7,1},{8,14},{9,15},{10,... | collective-permute-start | bytes 208904 | tf_op jit(solution)/shard_map/ppermute | solution.py:297
  146.5 4.3 %collective-permute-start.14 = (f32[136,128]{1,0:T(8,128)S(1)}, f32[136,128]{1,0:T(8,128)S(1)}, u32[]{:S(2)}, u32[]{:S(2)}) collective-permute-start(f32[136,128]{1,0:T(8,128)S(1)} %add.161), channel_id=1, source_target_pairs={{0,4},{1,5},{2,6},{3,7},{4,0},{5,1},{6,2},{7,3},{8,12},{9,13},{10,... | collective-permute-start | bytes 208904 | tf_op jit(solution)/shard_map/ppermute | solution.py:297
  147.0 4.3 %collective-permute-start.13 = (f32[136,128]{1,0:T(8,128)S(1)}, f32[136,128]{1,0:T(8,128)S(1)}, u32[]{:S(2)}, u32[]{:S(2)}) collective-permute-start(f32[136,128]{1,0:T(8,128)S(1)} %add.161), channel_id=1, source_target_pairs={{0,2},{1,3},{2,0},{3,1},{4,6},{5,7},{6,4},{7,5},{8,10},{9,11},{10,... | collective-permute-start | bytes 208904 | tf_op jit(solution)/shard_map/ppermute | solution.py:297
  151.3 6.3 %collective-permute-start.18 = (f32[136,128]{1,0:T(8,128)S(1)}, f32[136,128]{1,0:T(8,128)S(1)}, u32[]{:S(2)}, u32[]{:S(2)}) collective-permute-start(f32[136,128]{1,0:T(8,128)S(1)} %add_add_fusion.1), channel_id=1, source_target_pairs={{0,24},{8,16},{16,8},{24,0},{1,25},{9,17},{17,9},{25,1},{2,26},{10... | collective-permute-start | bytes 208904 | tf_op jit(solution)/shard_map/ppermute | solution.py:297
  154.9 5.3 %collective-permute-start.17 = (f32[136,128]{1,0:T(8,128)S(1)}, f32[136,128]{1,0:T(8,128)S(1)}, u32[]{:S(2)}, u32[]{:S(2)}) collective-permute-start(f32[136,128]{1,0:T(8,128)S(1)} %add_add_fusion.1), channel_id=1, source_target_pairs={{0,16},{8,24},{16,0},{24,8},{1,17},{9,25},{17,1},{25,9},{2,18},{10... | collective-permute-start | bytes 208904 | tf_op jit(solution)/shard_map/ppermute | solution.py:297
  154.9 5.7 %collective-permute-start.16 = (f32[136,128]{1,0:T(8,128)S(1)}, f32[136,128]{1,0:T(8,128)S(1)}, u32[]{:S(2)}, u32[]{:S(2)}) collective-permute-start(f32[136,128]{1,0:T(8,128)S(1)} %add_add_fusion.1), channel_id=1, source_target_pairs={{0,8},{8,0},{16,24},{24,16},{1,9},{9,1},{17,25},{25,17},{2,10},{10... | collective-permute-start | bytes 208904 | tf_op jit(solution)/shard_map/ppermute | solution.py:297
  160.6 1.3 collective-permute-start.19
